TPU v7x, 256 devices: a whole 4x4x8 slice. The times are simulated.
256 devices in a mesh: slab: 128 (over y, x, z), kv: 2 (over core).
Axes of the slice: x: 4, y: 4, z: 8, core: 2. Of those that a mesh axis runs over, the one named last changes fastest.
Arguments:
- queries: bfloat16 [131072, 512], P('slab'), may hold values from -6 to 6
- grad_out: bfloat16 [131072, 512], P('slab'), may hold values from -6 to 6
- attn_out: bfloat16 [131072, 512], P('slab'), may hold values from -6 to 6
- row_lse: float32 [131072], P('slab'), may hold values from 5.5 to 7.5
- keys: bfloat16 [2, 2048, 512], P('kv', 'slab'), may hold values from -6 to 6
- values: bfloat16 [2, 2048, 512], P('kv', 'slab'), may hold values from -6 to 6
Outputs:
- grad_queries: bfloat16 [131072, 512], P('slab', 'kv')
- grad_keys: bfloat16 [2, 2048, 512], P('kv', 'slab')
- grad_values: bfloat16 [2, 2048, 512], P('kv', 'slab')
All inputs are finite; a program needn't handle non-finite values.
Results may differ from a plain program's by a relative error of at most 0.005.
Values may be sent and summed in bfloat16 or wider, within the bound.
No kernel may reach another device: no remote copies, remote signals or barrier semaphores. Data moves between devices by JAX's collectives and lax.ppermute only.
A program may use at most 128 MiB of HBM per device.

v0:
```python
import jax
import jax.numpy as jnp
from jax import lax
from jax.sharding import Mesh
from jax.sharding import PartitionSpec as P

SLAB = ("slab_0", "slab_1", "slab_2")


def side_by_side(arrays, axis, dim, along):
    both = jnp.concatenate(arrays, axis=along)
    result, at, finished = (lax.all_gather(both, axis, axis=dim, tiled=True), 0, [])
    for a in arrays:
        finished.append(lax.slice_in_dim(result, at, at + a.shape[along], axis=along))
        at += a.shape[along]
    return tuple(finished)


def split_up(x, dim, length):
    dims = x.shape
    blocks = x.reshape(*dims[:dim], length, dims[dim] // length, *dims[dim + 1 :])
    return jnp.moveaxis(blocks, dim, 0)


def summed_on_arrival(x, axis, dim):
    length = lax.axis_size(axis)
    blocks = lax.all_to_all(split_up(x, dim, length), axis, 0, 0, tiled=True)
    return jnp.sum(blocks, axis=0)


def sum_by_axis(x, axes, dim):
    if not axes:
        return x
    nearer = lax.psum_scatter(x, axes[0], scatter_dimension=dim, tiled=True)
    return sum_by_axis(nearer, axes[1:], dim)


def contract_last(left, right):
    return lax.dot_general(
        left, right, (((1,), (1,)), ((), ())), preferred_element_type=jnp.float32
    )


def contract_first(left, right):
    return lax.dot_general(
        left, right, (((0,), (0,)), ((), ())), preferred_element_type=jnp.float32
    )


def panel_work(query_rows, grad_rows, lse_rows, stats, panel_keys, panel_values, score_scale):
    scores = contract_last(query_rows, panel_keys) * score_scale
    probs = jnp.exp(scores - lse_rows[:, None])
    probs_low = probs.astype(jnp.bfloat16)
    dprobs = contract_last(grad_rows, panel_values)
    dscores = (probs * (dprobs - stats[:, None])).astype(jnp.bfloat16)
    grad_part = jnp.dot(dscores, panel_keys, preferred_element_type=jnp.float32) * score_scale
    return (grad_part, probs_low, dscores)


def on_device(queries, grad_out, attn_out, row_lse, keys, values):
    channels = queries.shape[1]
    score_scale = channels ** (-0.5)
    stats = jnp.sum(grad_out.astype(jnp.float32) * attn_out.astype(jnp.float32), axis=1)
    panel_keys, panel_values = side_by_side((keys[0], values[0]), SLAB, 0, 1)
    grad_part, probs_low, dscores = panel_work(
        queries, grad_out, row_lse, stats, panel_keys, panel_values, score_scale
    )
    grad_queries = summed_on_arrival(grad_part, "kv", 1).astype(jnp.bfloat16)
    key_grad = contract_first(dscores, queries) * score_scale
    value_grad = contract_first(probs_low, grad_out)
    combined = sum_by_axis(jnp.concatenate([key_grad, value_grad], axis=1), SLAB, 0)
    grad_keys = combined[:, :channels].astype(jnp.bfloat16)[None]
    grad_values = combined[:, channels:].astype(jnp.bfloat16)[None]
    return (grad_queries, grad_keys, grad_values)


def solution(mesh):
    torus = Mesh(
        mesh.devices.reshape(4, 4, 8, mesh.shape["kv"]), ("slab_0", "slab_1", "slab_2", "kv")
    )
    placed = (
        P(SLAB, None),
        P(SLAB, None),
        P(SLAB, None),
        P(SLAB),
        P("kv", SLAB, None),
        P("kv", SLAB, None),
    )
    return jax.shard_map(
        on_device,
        mesh=torus,
        in_specs=placed,
        out_specs=(P(SLAB, "kv"), P("kv", SLAB, None), P("kv", SLAB, None)),
        check_vma=False,
    )
```

profile of v0, /device:TPU:24, one launch (start us, length us, event | category | flops | bytes accessed | tf_op | source)
XLA Modules:
  0.0 313.6 jit_solution(7220852868477064714)
XLA Ops:
  7.2 0.0 all-gather.2.cloned.1.call-start
  7.2 1.4 pad_maximum_fusion.1
  8.7 0.0 reduce-scatter.6.cloned.1.call-start
  8.7 1.9 multiply_reduce_fusion
  10.6 121.4 %all-gather.2.cloned.1.call-done = bf16[2048,1024]{1,0:T(8,128)(2,1)} async-done(((bf16[16,1024]{1,0:T(8,128)(2,1)}), bf16[2048,1024]{1,0:T(8,128)(2,1)}) %all-gather.2.cloned.1.call-update) | async-done | bytes 4194320 | tf_op jit(solution)/shard_map/all_gather | solution.py:12
  132.0 4.1 %fusion.8 = f32[2048,1024]{1,0:T(8,128)S(1)} fusion(bf16[1024,512]{1,0:T(8,128)(2,1)S(1)} %copy-done, bf16[2048,1024]{1,0:T(8,128)(2,1)} %all-gather.2.cloned.1.call-done), kind=kOutput, calls=%fused_computation.12 | convolution fusion | flops 2147483648 | bytes 11534336 | tf_op jit(solution)/shard_map/dot_general | solution.py:39
  136.1 2.6 fusion.1
  138.7 3.2 %multiply_convert_fusion = bf16[2048,1024]{1,0:T(8,128)(2,1)S(1)} fusion(f32[2048,1024]{1,0:T(8,128)S(1)} %fusion.8, f32[1024]{0:T(1024)S(1)} %multiply_reduce_fusion, f32[1024]{0:T(1024)S(1)} %copy-done.3, bf16[1024,512]{1,0:T(8,128)(2,1)S(1)} %copy-done.1, bf16[2048,1024]{1,0:T(8,128)(2,1)S(1)} %copy-done.2), kind=kOutput, calls=%fused_computation.1 | convolution fusion | flops 2157969408 | bytes 15736832 | tf_op jit(solution)/shard_map/dot_general | solution.py:39
  142.0 1.9 copy-done.4
  143.9 2.5 convolution_multiply_fusion
  146.4 3.8 %pad_maximum_fusion = f32[2048,1024]{0,1:T(8,128)} fusion(f32[2048,512]{0,1:T(8,128)S(1)} %fusion.1, f32[2048,512]{0,1:T(8,128)S(1)} %convolution_multiply_fusion), kind=kLoop, calls=%fused_computation | loop fusion | flops 2097152 | bytes 16777216 | tf_op jit(solution)/shard_map/concatenate | solution.py:71
  150.2 0.0 reduce-scatter.8.cloned.1.call-start
  150.3 78.0 %reduce-scatter.6.cloned.1.call-done = f32[512,1024]{0,1:T(8,128)} async-done(((f32[2048,1024]{0,1:T(8,128)}), f32[512,1024]{0,1:T(8,128)}) %reduce-scatter.6.cloned.1.call-update) | async-done | bytes 2097168 | tf_op jit(solution)/shard_map/reduce_scatter | solution.py:34
  228.3 0.2 reduce-scatter.10.cloned.1.call-start
  228.5 36.2 %reduce-scatter.8.cloned.1.call-done = f32[128,1024]{0,1:T(8,128)} async-done(((f32[512,1024]{0,1:T(8,128)}), f32[128,1024]{0,1:T(8,128)}) %reduce-scatter.8.cloned.1.call-update) | async-done | bytes 524304 | tf_op jit(solution)/shard_map/reduce_scatter | solution.py:34
  264.7 2.0 copy.14
  266.8 5.2 %fusion.10 = f32[1024,512]{0,1:T(8,128)S(1)} fusion(bf16[2048,1024]{1,0:T(8,128)(2,1)} %copy-done.4, bf16[2048,1024]{1,0:T(8,128)(2,1)} %all-gather.2.cloned.1.call-done), kind=kOutput, calls=%fused_computation.14 | convolution fusion | flops 2148007936 | bytes 8388608 | tf_op jit(solution)/shard_map/dot_general | solution.py:56
  272.0 5.4 %all_to_all.5 = f32[2,1024,256]{1,2,0:T(8,128)S(1)} all-to-all(f32[2,1024,256]{1,2,0:T(8,128)S(1)} %bitcast.16), channel_id=1, replica_groups=mesh['slab_0'=4,'slab_1'=4,'slab_2'=8,'kv'=2] {'kv'}, dimensions={0} | all-to-all | bytes 4194304 | tf_op jit(solution)/shard_map/all_to_all | solution.py:27
  277.4 1.1 reduce_sum.19
  278.5 2.0 copy.11
  280.6 24.1 %reduce-scatter.10.cloned.1.call-done = f32[16,1024]{1,0:T(8,128)} async-done(((f32[128,1024]{1,0:T(8,128)}), f32[16,1024]{1,0:T(8,128)}) %reduce-scatter.10.cloned.1.call-update) | async-done | bytes 65552
  304.6 1.0 copy.15
  305.7 0.7 copy.12
  306.4 0.7 copy.13
  (14 shorter events, 0.1 us)
Async XLA Ops:
  7.2 124.8 %copy-start = (bf16[1024,512]{1,0:T(8,128)(2,1)S(1)}, bf16[1024,512]{1,0:T(8,128)(2,1)}, u32[]{:S(2)}) copy-start(bf16[1024,512]{1,0:T(8,128)(2,1)} %param.6) | copy-start | bytes 3145732
  7.2 124.8 %all-gather.2.cloned.1.call-start = ((), (), s32[]{:S(2)}) async-start(), calls=%async_computation.4 | async-start | bytes 4227072 | tf_op jit(solution)/shard_map/all_gather | solution.py:12
  8.7 219.6 %reduce-scatter.6.cloned.1.call-start = ((), (), s32[]{:S(2)}) async-start(), calls=%async_computation.5 | async-start | bytes 10485760 | tf_op jit(solution)/shard_map/reduce_scatter | solution.py:34
  10.6 125.5 %copy-start.1 = (bf16[1024,512]{1,0:T(8,128)(2,1)S(1)}, bf16[1024,512]{1,0:T(8,128)(2,1)}, u32[]{:S(2)}) copy-start(bf16[1024,512]{1,0:T(8,128)(2,1)} %param.7) | copy-start | bytes 3145732
  10.6 125.5 %copy-start.3 = (f32[1024]{0:T(1024)S(1)}, f32[1024]{0:T(1024)}, u32[]{:S(2)}) copy-start(f32[1024]{0:T(1024)} %param.9) | copy-start | bytes 12292
  136.1 2.6 copy-start.2
  142.0 1.9 copy-start.4
  150.2 114.5 %reduce-scatter.8.cloned.1.call-start = ((), (), s32[]{:S(2)}) async-start(), calls=%async_computation.6 | async-start | bytes 2621440 | tf_op jit(solution)/shard_map/reduce_scatter | solution.py:34
  228.3 76.3 %reduce-scatter.10.cloned.1.call-start = ((), (), s32[]{:S(2)}) async-start(), calls=%async_computation.7 | async-start | bytes 589824
Sparse Core Ops, SparseCore 0:
  12.2 119.7 all-gather.1
  150.4 77.8 reduce-scatter.5
  230.8 33.8 reduce-scatter.7
  267.1 37.4 reduce-scatter.9
where the time goes:
time: 314 us
  waiting for transfers between devices  260 us (83%)
  matrix products  17.6 us (6%)
  between operations  13.9 us (4%)
  local copies, waits for them, and re-layouts  8.43 us (3%)
  other arithmetic  8.19 us (3%)
  blocking collectives  5.42 us (2%)
    all_gather x1, waiting for transfers between devices, side_by_side(): lax.all_gather(both, axis, axis=dim, tiled=True)  121 us
    reduce_scatter x2, waiting for transfers between devices, sum_by_axis(): nearer = lax.psum_scatter(x, axes[0], scatter_dimension=dim, tiled=True)  114 us
    unnamed x5, waiting for transfers between devices  24.1 us
    unnamed x15, local copies, waits for them, and re-layouts  8.42 us
    dot_general x2, matrix products, contract_last(): lax.dot_general(left, right, (((1,), (1,)), ((), ())), preferred_element_...  7.29 us
  transfers between devices with their start and end apart: 4, of which 4 were waited for; matrix products, arithmetic and copies ran while one was open for 3% of the time, Pallas kernels for 0%

commit v1 on v0

v1 whole, which is shorter than its diff:
```python
import jax
import jax.numpy as jnp
from jax import lax
from jax.sharding import Mesh
from jax.sharding import PartitionSpec as P

SLAB = ("slab_0", "slab_1", "slab_2")
F32 = jnp.float32
BF16 = jnp.bfloat16


def neighbour(i, n, turn):
    if turn == 0:
        return i ^ 1
    return (i - 1) % n if i % 2 == 0 else (i + 1) % n


def trade(x, axis, turn):
    n = lax.axis_size(axis)
    pairs = []
    for i in range(n):
        for core in range(2):
            j = neighbour(i, n, (turn + core) % 2)
            pairs.append((2 * i + core, 2 * j + core))
    return lax.ppermute(x, (axis, "kv"), pairs)


def swap(x):
    return lax.ppermute(x, "kv", [(0, 1), (1, 0)])


def contract_last(left, right):
    return lax.dot_general(left, right, (((1,), (1,)), ((), ())), preferred_element_type=F32)


def contract_first(left, right):
    return lax.dot_general(left, right, (((0,), (0,)), ((), ())), preferred_element_type=F32)


def three_parts(v):
    hi = lax.reduce_precision(v, 8, 7)
    rest = v - hi
    mid = lax.reduce_precision(rest, 8, 7)
    low = rest - mid
    return jnp.stack([hi, mid, low]).astype(BF16)


def on_device(queries, grad_out, attn_out, row_lse, keys, values):
    tokens, channels = queries.shape
    scale = channels ** (-0.5)
    core = lax.axis_index("kv")
    half = tokens // 2

    k0 = jnp.concatenate([keys[0], values[0]], axis=1)
    z1 = trade(k0, "slab_2", 0)
    z2 = trade(jnp.concatenate([k0, z1]), "slab_2", 1)
    z3 = trade(z2, "slab_2", 0)
    z4 = trade(z3, "slab_2", 1)
    zall = jnp.concatenate([k0, z1, z2, z3, z4])
    y1 = trade(zall, "slab_0", 0)
    y2 = trade(jnp.concatenate([zall, y1]), "slab_0", 1)
    mine = jnp.concatenate([zall, y1, y2])
    theirs = swap(mine)

    def my_half(a):
        return lax.dynamic_slice_in_dim(a, core * half, half, 0)

    q, g, o, lse = my_half(queries), my_half(grad_out), my_half(attn_out), my_half(row_lse)
    stats = jnp.sum(g.astype(F32) * o.astype(F32), axis=1)
    extra = three_parts(jnp.concatenate([lse, stats]))
    extra = jnp.pad(extra, ((0, 13), (0, 0)))
    pack0 = jnp.concatenate([jnp.concatenate([q, g], axis=1), extra])
    pack1 = trade(pack0, "slab_1", 0)
    pack2 = trade(pack0, "slab_1", 1)
    pack3 = trade(pack1, "slab_1", 1)

    def work(pack, panel):
        qs, gs = pack[:half, :channels], pack[:half, channels:]
        both = jnp.sum(pack[half : half + 3].astype(F32), axis=0)
        lse_t, stats_t = both[:half], both[half:]
        k, v = panel[:, :channels], panel[:, channels:]
        probs = jnp.exp(contract_last(qs, k) * scale - lse_t[:, None])
        dscores = (probs * (contract_last(gs, v) - stats_t[:, None])).astype(BF16)
        dq = jnp.dot(dscores, k, preferred_element_type=F32)
        dk = contract_first(dscores, qs)
        dv = contract_first(probs.astype(BF16), gs)
        return dq, jnp.concatenate([dk, dv], axis=1)

    dqs, mine_sum, theirs_sum = [], 0.0, 0.0
    for pack in (pack0, pack1, pack2, pack3):
        dq_a, m = work(pack, mine)
        dq_b, t = work(pack, theirs)
        dqs.append(dq_a + dq_b)
        mine_sum, theirs_sum = mine_sum + m, theirs_sum + t

    got2 = trade(dqs[2].astype(BF16), "slab_1", 1).astype(F32)
    got3 = trade(dqs[3].astype(BF16), "slab_1", 1).astype(F32)
    got1 = trade((dqs[1] + got3).astype(BF16), "slab_1", 0).astype(F32)
    dq = ((dqs[0] + got2 + got1) * scale).astype(BF16)
    width = channels // 2
    keep = lax.dynamic_slice_in_dim(dq, core * width, width, 1)
    away = swap(lax.dynamic_slice_in_dim(dq, (1 - core) * width, width, 1))
    grad_queries = jnp.where(core == 0, jnp.concatenate([keep, away]), jnp.concatenate([away, keep]))

    total = mine_sum + swap(theirs_sum.astype(BF16)).astype(F32)
    n1, n = keys.shape[1], keys.shape[1] * 8
    total = total[: 2 * n] + trade(total[2 * n :].astype(BF16), "slab_0", 1).astype(F32)
    total = total[:n] + trade(total[n:].astype(BF16), "slab_0", 0).astype(F32)
    t0, t2, t3, t4 = total[: 2 * n1], total[2 * n1 : 4 * n1], total[4 * n1 : 6 * n1], total[6 * n1 :]
    t3 = t3 + trade(t4.astype(BF16), "slab_2", 1).astype(F32)
    t2 = t2 + trade(t3.astype(BF16), "slab_2", 0).astype(F32)
    t0 = t0 + trade(t2.astype(BF16), "slab_2", 1).astype(F32)
    own = t0[:n1] + trade(t0[n1:].astype(BF16), "slab_2", 0).astype(F32)
    grad_keys = (own[:, :channels] * scale).astype(BF16)[None]
    grad_values = own[:, channels:].astype(BF16)[None]
    return (grad_queries, grad_keys, grad_values)


def solution(mesh):
    torus = Mesh(
        mesh.devices.reshape(4, 4, 8, mesh.shape["kv"]), ("slab_0", "slab_1", "slab_2", "kv")
    )
    placed = (
        P(SLAB, None),
        P(SLAB, None),
        P(SLAB, None),
        P(SLAB),
        P("kv", SLAB, None),
        P("kv", SLAB, None),
    )
    return jax.shard_map(
        on_device,
        mesh=torus,
        in_specs=placed,
        out_specs=(P(SLAB, "kv"), P("kv", SLAB, None), P("kv", SLAB, None)),
        check_vma=False,
    )
```

time: 314 us -> 149 us (0.47)
  waiting for transfers between devices: 260 us -> 64.6 us
  starting transfers between devices: 0.34 us -> 29.1 us
  matrix products: 17.6 us -> 36.6 us
  between operations: 13.9 us -> 1.2 us
  blocking collectives: 5.42 us -> 0 us
    all_gather x1 -> x0, waiting for transfers between devices: 121 us -> none  [side_by_side(): lax.all_gather(both, axis, axis=dim, tiled=True)]
    reduce_scatter x2 -> x0, waiting for transfers between devices: 114 us -> none  [sum_by_axis(): nearer = lax.psum_scatter(x, axes[0], scatter_dimension=dim, tiled=True)]
    ppermute x0 -> x21, waiting for transfers between devices: none -> 64.6 us  [the longest x18 64.3 us: trade(): return lax.ppermute(x, (axis, 'kv'), pairs)]
    ppermute x0 -> x21, starting transfers between devices: none -> 29.1 us  [the longest x18 28.6 us: trade(): return lax.ppermute(x, (axis, 'kv'), pairs)]
    unnamed x5 -> x0, waiting for transfers between devices: 24.1 us -> none
    dot_general x2 -> x16, matrix products: 5.12 us -> 16.1 us  [contract_first(): lax.dot_general(left, right, (((0,), (0,)), ((), ())), preferred_element_...]
    dot_general x2 -> x16, matrix products: 7.29 us -> 16.1 us  [contract_last(): lax.dot_general(left, right, (((1,), (1,)), ((), ())), preferred_element_...]
    all_to_all x1 -> x0, blocking collectives: 5.42 us -> none  [summed_on_arrival(): blocks = lax.all_to_all(split_up(x, dim, length), axis, 0, 0, tiled=True)]
  transfers between devices with their start and end apart: 4 -> 21, of which waited for: 4 -> 14; matrix products, arithmetic and copies ran while one was open for 3% -> 32% of each run, Pallas kernels for 0% -> 0%
where the time goes in v1:
time: 149 us; the launch traced here: 148 us
  waiting for transfers between devices  64.6 us (43%)
  matrix products  36.6 us (25%)
  starting transfers between devices  29.1 us (20%)
  other arithmetic  10.2 us (7%)
  local copies, waits for them, and re-layouts  6.35 us (4%)
    ppermute x18, waiting for transfers between devices, trade(): return lax.ppermute(x, (axis, 'kv'), pairs)  64.3 us
    ppermute x18, starting transfers between devices, trade(): return lax.ppermute(x, (axis, 'kv'), pairs)  28.6 us
    dot_general x16, matrix products, contract_last(): lax.dot_general(left, right, (((1,), (1,)), ((), ())), preferred_element_...  16.1 us
    dot_general x16, matrix products, contract_first(): lax.dot_general(left, right, (((0,), (0,)), ((), ())), preferred_element_...  16.1 us
    dot_general x8, matrix products, work(): dq = jnp.dot(dscores, k, preferred_element_type=F32)  4.39 us
    unnamed x10, local copies, waits for them, and re-layouts  3.94 us
  transfers between devices with their start and end apart: 21, of which 14 were waited for; matrix products, arithmetic and copies ran while one was open for 32% of the time, Pallas kernels for 0%

profile of v1, /device:TPU:24, one launch (start us, length us, event | category | flops | bytes accessed | tf_op | source)
XLA Modules:
  0.0 148.0 jit_solution(3804707084596163129)
XLA Ops:
  2.1 1.9 %collective-permute-start = (bf16[16,1024]{1,0:T(8,128)(2,1)S(1)}, bf16[16,1024]{1,0:T(8,128)(2,1)S(1)}, u32[]{:S(2)}, u32[]{:S(2)}) collective-permute-start(bf16[16,1024]{1,0:T(8,128)(2,1)S(1)} %get-tuple-element.29), channel_id=1, source_target_pairs={{0,2},{1,15},{2,0},{3,5},{4,6},{5,3},{6,4},{7,9},{8,10},{9,7},{10,... | collective-permute-start | bytes 98312 | tf_op jit(solution)/shard_map/ppermute | solution.py:25
  4.0 2.0 %collective-permute-done = bf16[16,1024]{1,0:T(8,128)(2,1)S(1)} collective-permute-done((bf16[16,1024]{1,0:T(8,128)(2,1)S(1)}, bf16[16,1024]{1,0:T(8,128)(2,1)S(1)}, u32[]{:S(2)}, u32[]{:S(2)}) %collective-permute-start) | collective-permute-done | bytes 32800 | tf_op jit(solution)/shard_map/ppermute | solution.py:25
  6.8 5.9 %collective-permute-start.1 = (bf16[32,1024]{1,0:T(8,128)(2,1)S(1)}, bf16[32,1024]{1,0:T(8,128)(2,1)S(1)}, u32[]{:S(2)}, u32[]{:S(2)}) collective-permute-start(bf16[32,1024]{1,0:T(8,128)(2,1)S(1)} %pad_maximum_fusion), channel_id=1, source_target_pairs={{0,14},{1,3},{2,4},{3,1},{4,2},{5,7},{6,8},{7,5},{8,6},{9,11},{10,... | collective-permute-start | bytes 196616 | tf_op jit(solution)/shard_map/ppermute | solution.py:25
  13.2 1.6 %collective-permute-done.1 = bf16[32,1024]{1,0:T(8,128)(2,1)S(1)} collective-permute-done((bf16[32,1024]{1,0:T(8,128)(2,1)S(1)}, bf16[32,1024]{1,0:T(8,128)(2,1)S(1)}, u32[]{:S(2)}, u32[]{:S(2)}) %collective-permute-start.1) | collective-permute-done | bytes 65568 | tf_op jit(solution)/shard_map/ppermute | solution.py:25
  15.5 3.6 %collective-permute-done.2 = bf16[32,1024]{1,0:T(8,128)(2,1)S(1)} collective-permute-done((bf16[32,1024]{1,0:T(8,128)(2,1)S(1)}, bf16[32,1024]{1,0:T(8,128)(2,1)S(1)}, u32[]{:S(2)}, u32[]{:S(2)}) %collective-permute-start.2) | collective-permute-done | bytes 65568 | tf_op jit(solution)/shard_map/ppermute | solution.py:25
  19.1 3.2 %collective-permute-start.3 = (bf16[32,1024]{1,0:T(8,128)(2,1)S(1)}, bf16[32,1024]{1,0:T(8,128)(2,1)S(1)}, u32[]{:S(2)}, u32[]{:S(2)}) collective-permute-start(bf16[32,1024]{1,0:T(8,128)(2,1)S(1)} %collective-permute-done.2), channel_id=1, source_target_pairs={{0,14},{1,3},{2,4},{3,1},{4,2},{5,7},{6,8},{7,5},{8,6},{9,11},{10,... | collective-permute-start | bytes 196616 | tf_op jit(solution)/shard_map/ppermute | solution.py:25
  23.0 1.6 %collective-permute-done.3 = bf16[32,1024]{1,0:T(8,128)(2,1)S(1)} collective-permute-done((bf16[32,1024]{1,0:T(8,128)(2,1)S(1)}, bf16[32,1024]{1,0:T(8,128)(2,1)S(1)}, u32[]{:S(2)}, u32[]{:S(2)}) %collective-permute-start.3) | collective-permute-done | bytes 65568 | tf_op jit(solution)/shard_map/ppermute | solution.py:25
  27.5 5.0 %collective-permute-done.4 = bf16[128,1024]{1,0:T(8,128)(2,1)S(1)} collective-permute-done((bf16[128,1024]{1,0:T(8,128)(2,1)S(1)}, bf16[128,1024]{1,0:T(8,128)(2,1)S(1)}, u32[]{:S(2)}, u32[]{:S(2)}) %collective-permute-start.4) | collective-permute-done | bytes 262176 | tf_op jit(solution)/shard_map/ppermute | solution.py:25
  35.0 2.8 %collective-permute-start.7 = (bf16[528,1024]{1,0:T(8,128)(2,1)}, bf16[528,1024]{1,0:T(8,128)(2,1)}, u32[]{:S(2)}, u32[]{:S(2)}) collective-permute-start(bf16[528,1024]{1,0:T(8,128)(2,1)} %fusion.47), channel_id=1, source_target_pairs={{0,48},{1,17},{16,32},{17,1},{32,16},{33,49},{48,0},{49,33},{2,50}... | collective-permute-start | bytes 3244040 | tf_op jit(solution)/shard_map/ppermute | solution.py:25
  38.0 5.9 %collective-permute-done.5 = bf16[256,1024]{1,0:T(8,128)(2,1)} collective-permute-done((bf16[256,1024]{1,0:T(8,128)(2,1)}, bf16[256,1024]{1,0:T(8,128)(2,1)}, u32[]{:S(2)}, u32[]{:S(2)}) %collective-permute-start.5) | collective-permute-done | bytes 524320 | tf_op jit(solution)/shard_map/ppermute | solution.py:25
  47.1 10.6 %collective-permute-done.7 = bf16[528,1024]{1,0:T(8,128)(2,1)} collective-permute-done((bf16[528,1024]{1,0:T(8,128)(2,1)}, bf16[528,1024]{1,0:T(8,128)(2,1)}, u32[]{:S(2)}, u32[]{:S(2)}) %collective-permute-start.7) | collective-permute-done | bytes 1081376 | tf_op jit(solution)/shard_map/ppermute | solution.py:25
  59.2 2.4 %collective-permute-start.10 = (bf16[528,1024]{1,0:T(8,128)(2,1)}, bf16[528,1024]{1,0:T(8,128)(2,1)S(1)}, u32[]{:S(2)}, u32[]{:S(2)}) collective-permute-start(bf16[528,1024]{1,0:T(8,128)(2,1)} %collective-permute-done.9), channel_id=1, source_target_pairs={{0,48},{1,17},{16,32},{17,1},{32,16},{33,49},{48,0},{49,33},{2,50}... | collective-permute-start | bytes 3244040 | tf_op jit(solution)/shard_map/ppermute | solution.py:25
  63.1 1.5 %fusion.19 = f32[512,512]{1,0:T(8,128)S(1)} fusion(f32[512]{0:T(512)S(1)} %get-tuple-element.35, bf16[528,1024]{1,0:T(8,128)(2,1)} %collective-permute-done.9, bf16[512,1024]{1,0:T(8,128)(2,1)S(1)} %constant_dynamic-update-slice_fusion.11), kind=kOutput, calls=%fused_computation.32 | convolution fusion | flops 268959744 | bytes 2099200 | tf_op jit(solution)/shard_map/dot_general | solution.py:33
  75.3 1.5 %fusion.22 = f32[512,512]{1,0:T(8,128)S(1)} fusion(f32[512]{0:T(512)S(1)} %get-tuple-element.31, bf16[528,1024]{1,0:T(8,128)(2,1)} %collective-permute-done.7, bf16[512,1024]{1,0:T(8,128)(2,1)S(1)} %collective-permute-done.6), kind=kOutput, calls=%fused_computation.37 | convolution fusion | flops 268959744 | bytes 2099200 | tf_op jit(solution)/shard_map/dot_general | solution.py:33
  82.8 1.5 %fusion.15 = f32[512,512]{1,0:T(8,128)S(1)} fusion(f32[512]{0:T(512)S(1)} %get-tuple-element.35, bf16[528,1024]{1,0:T(8,128)(2,1)} %collective-permute-done.9, bf16[512,1024]{1,0:T(8,128)(2,1)S(1)} %collective-permute-done.6), kind=kOutput, calls=%fused_computation.25 | convolution fusion | flops 268959744 | bytes 2099200 | tf_op jit(solution)/shard_map/dot_general | solution.py:33
  99.0 2.5 %collective-permute-start.11 = (bf16[512,512]{1,0:T(8,128)(2,1)S(1)}, bf16[512,512]{1,0:T(8,128)(2,1)S(1)}, u32[]{:S(2)}, u32[]{:S(2)}) collective-permute-start(bf16[512,512]{1,0:T(8,128)(2,1)S(1)} %fusion.46), channel_id=1, source_target_pairs={{0,48},{1,17},{16,32},{17,1},{32,16},{33,49},{48,0},{49,33},{2,50}... | collective-permute-start | bytes 1572872 | tf_op jit(solution)/shard_map/ppermute | solution.py:25
  101.9 6.7 %collective-permute-done.15 = bf16[256,1024]{0,1:T(8,128)(2,1)S(1)} collective-permute-done((bf16[256,1024]{0,1:T(8,128)(2,1)S(1)}, bf16[256,1024]{0,1:T(8,128)(2,1)S(1)}, u32[]{:S(2)}, u32[]{:S(2)}) %collective-permute-start.15) | collective-permute-done | bytes 524320 | tf_op jit(solution)/shard_map/ppermute | solution.py:25
  110.0 5.3 %collective-permute-done.16 = bf16[128,1024]{0,1:T(8,128)(2,1)S(1)} collective-permute-done((bf16[128,1024]{0,1:T(8,128)(2,1)S(1)}, bf16[128,1024]{0,1:T(8,128)(2,1)S(1)}, u32[]{:S(2)}, u32[]{:S(2)}) %collective-permute-start.16) | collective-permute-done | bytes 262176 | tf_op jit(solution)/shard_map/ppermute | solution.py:25
  115.5 3.0 %collective-permute-start.17 = (bf16[32,1024]{0,1:T(8,128)(2,1)S(1)}, bf16[32,1024]{0,1:T(8,128)(2,1)S(1)}, u32[]{:S(2)}, u32[]{:S(2)}) collective-permute-start(bf16[32,1024]{0,1:T(8,128)(2,1)S(1)} %slice.316), channel_id=1, source_target_pairs={{0,14},{1,3},{2,4},{3,1},{4,2},{5,7},{6,8},{7,5},{8,6},{9,11},{10,... | collective-permute-start | bytes 196616 | tf_op jit(solution)/shard_map/ppermute | solution.py:25
  119.0 4.2 %collective-permute-done.17 = bf16[32,1024]{0,1:T(8,128)(2,1)S(1)} collective-permute-done((bf16[32,1024]{0,1:T(8,128)(2,1)S(1)}, bf16[32,1024]{0,1:T(8,128)(2,1)S(1)}, u32[]{:S(2)}, u32[]{:S(2)}) %collective-permute-start.17) | collective-permute-done | bytes 65568 | tf_op jit(solution)/shard_map/ppermute | solution.py:25
  124.0 6.6 %collective-permute-done.18 = bf16[32,1024]{0,1:T(8,128)(2,1)S(1)} collective-permute-done((bf16[32,1024]{0,1:T(8,128)(2,1)S(1)}, bf16[32,1024]{0,1:T(8,128)(2,1)S(1)}, u32[]{:S(2)}, u32[]{:S(2)}) %collective-permute-start.18) | collective-permute-done | bytes 65568 | tf_op jit(solution)/shard_map/ppermute | solution.py:25
  130.9 3.0 %collective-permute-start.19 = (bf16[32,1024]{0,1:T(8,128)(2,1)S(1)}, bf16[32,1024]{0,1:T(8,128)(2,1)S(1)}, u32[]{:S(2)}, u32[]{:S(2)}) collective-permute-start(bf16[32,1024]{0,1:T(8,128)(2,1)S(1)} %fusion.49), channel_id=1, source_target_pairs={{0,14},{1,3},{2,4},{3,1},{4,2},{5,7},{6,8},{7,5},{8,6},{9,11},{10,... | collective-permute-start | bytes 196616 | tf_op jit(solution)/shard_map/ppermute | solution.py:25
  134.1 5.7 %collective-permute-done.19 = bf16[32,1024]{0,1:T(8,128)(2,1)S(1)} collective-permute-done((bf16[32,1024]{0,1:T(8,128)(2,1)S(1)}, bf16[32,1024]{0,1:T(8,128)(2,1)S(1)}, u32[]{:S(2)}, u32[]{:S(2)}) %collective-permute-start.19) | collective-permute-done | bytes 65568 | tf_op jit(solution)/shard_map/ppermute | solution.py:25
  141.1 5.3 %collective-permute-done.20 = bf16[16,1024]{0,1:T(8,128)(2,1)S(1)} collective-permute-done((bf16[16,1024]{0,1:T(8,128)(2,1)S(1)}, bf16[16,1024]{0,1:T(8,128)(2,1)S(1)}, u32[]{:S(2)}, u32[]{:S(2)}) %collective-permute-start.20) | collective-permute-done | bytes 32800 | tf_op jit(solution)/shard_map/ppermute | solution.py:25
  (101 shorter events, 53.2 us)
Async XLA Ops:
  0.6 33.2 %copy-start = (bf16[1024,512]{1,0:T(8,128)(2,1)S(1)}, bf16[1024,512]{1,0:T(8,128)(2,1)}, u32[]{:S(2)}) copy-start(bf16[1024,512]{1,0:T(8,128)(2,1)} %param.6) | copy-start | bytes 3145732
  0.6 25.4 %copy-start.1 = (f32[1024]{0:T(1024)S(1)}, f32[1024]{0:T(1024)}, u32[]{:S(2)}) copy-start(f32[1024]{0:T(1024)} %param.9) | copy-start | bytes 12292
  2.1 3.9 %collective-permute-start = (bf16[16,1024]{1,0:T(8,128)(2,1)S(1)}, bf16[16,1024]{1,0:T(8,128)(2,1)S(1)}, u32[]{:S(2)}, u32[]{:S(2)}) collective-permute-start(bf16[16,1024]{1,0:T(8,128)(2,1)S(1)} %get-tuple-element.29), channel_id=1, source_target_pairs={{0,2},{1,15},{2,0},{3,5},{4,6},{5,3},{6,4},{7,9},{8,10},{9,7},{10,... | collective-permute-start | bytes 98312 | tf_op jit(solution)/shard_map/ppermute | solution.py:25
  6.8 8.1 %collective-permute-start.1 = (bf16[32,1024]{1,0:T(8,128)(2,1)S(1)}, bf16[32,1024]{1,0:T(8,128)(2,1)S(1)}, u32[]{:S(2)}, u32[]{:S(2)}) collective-permute-start(bf16[32,1024]{1,0:T(8,128)(2,1)S(1)} %pad_maximum_fusion), channel_id=1, source_target_pairs={{0,14},{1,3},{2,4},{3,1},{4,2},{5,7},{6,8},{7,5},{8,6},{9,11},{10,... | collective-permute-start | bytes 196616 | tf_op jit(solution)/shard_map/ppermute | solution.py:25
  14.9 4.3 %collective-permute-start.2 = (bf16[32,1024]{1,0:T(8,128)(2,1)S(1)}, bf16[32,1024]{1,0:T(8,128)(2,1)S(1)}, u32[]{:S(2)}, u32[]{:S(2)}) collective-permute-start(bf16[32,1024]{1,0:T(8,128)(2,1)S(1)} %collective-permute-done.1), channel_id=1, source_target_pairs={{0,2},{1,15},{2,0},{3,5},{4,6},{5,3},{6,4},{7,9},{8,10},{9,7},{10,... | collective-permute-start | bytes 196616 | tf_op jit(solution)/shard_map/ppermute | solution.py:25
  19.1 5.5 %collective-permute-start.3 = (bf16[32,1024]{1,0:T(8,128)(2,1)S(1)}, bf16[32,1024]{1,0:T(8,128)(2,1)S(1)}, u32[]{:S(2)}, u32[]{:S(2)}) collective-permute-start(bf16[32,1024]{1,0:T(8,128)(2,1)S(1)} %collective-permute-done.2), channel_id=1, source_target_pairs={{0,14},{1,3},{2,4},{3,1},{4,2},{5,7},{6,8},{7,5},{8,6},{9,11},{10,... | collective-permute-start | bytes 196616 | tf_op jit(solution)/shard_map/ppermute | solution.py:25
  25.3 7.2 %collective-permute-start.4 = (bf16[128,1024]{1,0:T(8,128)(2,1)S(1)}, bf16[128,1024]{1,0:T(8,128)(2,1)S(1)}, u32[]{:S(2)}, u32[]{:S(2)}) collective-permute-start(bf16[128,1024]{1,0:T(8,128)(2,1)S(1)} %get-tuple-element.16), channel_id=1, source_target_pairs={{0,64},{1,193},{64,0},{65,129},{128,192},{129,65},{192,128},{193,1... | collective-permute-start | bytes 786440 | tf_op jit(solution)/shard_map/ppermute | solution.py:25
  33.2 10.7 %collective-permute-start.5 = (bf16[256,1024]{1,0:T(8,128)(2,1)}, bf16[256,1024]{1,0:T(8,128)(2,1)}, u32[]{:S(2)}, u32[]{:S(2)}) collective-permute-start(bf16[256,1024]{1,0:T(8,128)(2,1)} %get-tuple-element.12), channel_id=1, source_target_pairs={{0,192},{1,65},{64,128},{65,1},{128,64},{129,193},{192,0},{193,129... | collective-permute-start | bytes 1572872 | tf_op jit(solution)/shard_map/ppermute | solution.py:25
  35.0 22.7 %collective-permute-start.7 = (bf16[528,1024]{1,0:T(8,128)(2,1)}, bf16[528,1024]{1,0:T(8,128)(2,1)}, u32[]{:S(2)}, u32[]{:S(2)}) collective-permute-start(bf16[528,1024]{1,0:T(8,128)(2,1)} %fusion.47), channel_id=1, source_target_pairs={{0,48},{1,17},{16,32},{17,1},{32,16},{33,49},{48,0},{49,33},{2,50}... | collective-permute-start | bytes 3244040 | tf_op jit(solution)/shard_map/ppermute | solution.py:25
  37.8 20.7 %collective-permute-start.9 = (bf16[528,1024]{1,0:T(8,128)(2,1)}, bf16[528,1024]{1,0:T(8,128)(2,1)}, u32[]{:S(2)}, u32[]{:S(2)}) collective-permute-start(bf16[528,1024]{1,0:T(8,128)(2,1)} %fusion.47), channel_id=1, source_target_pairs={{0,16},{1,49},{16,0},{17,33},{32,48},{33,17},{48,32},{49,1},{2,18}... | collective-permute-start | bytes 3244040 | tf_op jit(solution)/shard_map/ppermute | solution.py:25
  45.0 28.8 %collective-permute-start.6 = (bf16[512,1024]{1,0:T(8,128)(2,1)S(1)}, bf16[512,1024]{1,0:T(8,128)(2,1)S(1)}, u32[]{:S(2)}, u32[]{:S(2)}) collective-permute-start(bf16[512,1024]{1,0:T(8,128)(2,1)S(1)} %constant_dynamic-update-slice_fusion.11), channel_id=1, source_target_pairs={{0,1},{1,0},{2,3},{3,2},{4,5},{5,4},{6,7},{7,6},{8,9},{9,8},{10,11... | collective-permute-start | bytes 3145736 | tf_op jit(solution)/shard_map/ppermute | solution.py:29
  59.2 31.7 %collective-permute-start.10 = (bf16[528,1024]{1,0:T(8,128)(2,1)}, bf16[528,1024]{1,0:T(8,128)(2,1)S(1)}, u32[]{:S(2)}, u32[]{:S(2)}) collective-permute-start(bf16[528,1024]{1,0:T(8,128)(2,1)} %collective-permute-done.9), channel_id=1, source_target_pairs={{0,48},{1,17},{16,32},{17,1},{32,16},{33,49},{48,0},{49,33},{2,50}... | collective-permute-start | bytes 3244040 | tf_op jit(solution)/shard_map/ppermute | solution.py:25
  80.1 43.4 %collective-permute-start.8 = (bf16[512,512]{1,0:T(8,128)(2,1)}, bf16[512,512]{1,0:T(8,128)(2,1)S(1)}, u32[]{:S(2)}, u32[]{:S(2)}) collective-permute-start(bf16[512,512]{1,0:T(8,128)(2,1)} %fusion.45), channel_id=1, source_target_pairs={{0,48},{1,17},{16,32},{17,1},{32,16},{33,49},{48,0},{49,33},{2,50}... | collective-permute-start | bytes 1572872 | tf_op jit(solution)/shard_map/ppermute | solution.py:25
  94.0 3.0 %collective-permute-start.14 = (bf16[512,1024]{0,1:T(8,128)(2,1)S(1)}, bf16[512,1024]{0,1:T(8,128)(2,1)S(1)}, u32[]{:S(2)}, u32[]{:S(2)}) collective-permute-start(bf16[512,1024]{0,1:T(8,128)(2,1)S(1)} %fusion.6), channel_id=1, source_target_pairs={{0,1},{1,0},{2,3},{3,2},{4,5},{5,4},{6,7},{7,6},{8,9},{9,8},{10,11... | collective-permute-start | bytes 3145736 | tf_op jit(solution)/shard_map/ppermute | solution.py:29
  98.2 10.5 %collective-permute-start.15 = (bf16[256,1024]{0,1:T(8,128)(2,1)S(1)}, bf16[256,1024]{0,1:T(8,128)(2,1)S(1)}, u32[]{:S(2)}, u32[]{:S(2)}) collective-permute-start(bf16[256,1024]{0,1:T(8,128)(2,1)S(1)} %slice.314), channel_id=1, source_target_pairs={{0,192},{1,65},{64,128},{65,1},{128,64},{129,193},{192,0},{193,129... | collective-permute-start | bytes 1572872 | tf_op jit(solution)/shard_map/ppermute | solution.py:25
  99.0 10.5 %collective-permute-start.11 = (bf16[512,512]{1,0:T(8,128)(2,1)S(1)}, bf16[512,512]{1,0:T(8,128)(2,1)S(1)}, u32[]{:S(2)}, u32[]{:S(2)}) collective-permute-start(bf16[512,512]{1,0:T(8,128)(2,1)S(1)} %fusion.46), channel_id=1, source_target_pairs={{0,48},{1,17},{16,32},{17,1},{32,16},{33,49},{48,0},{49,33},{2,50}... | collective-permute-start | bytes 1572872 | tf_op jit(solution)/shard_map/ppermute | solution.py:25
  108.9 6.5 %collective-permute-start.16 = (bf16[128,1024]{0,1:T(8,128)(2,1)S(1)}, bf16[128,1024]{0,1:T(8,128)(2,1)S(1)}, u32[]{:S(2)}, u32[]{:S(2)}) collective-permute-start(bf16[128,1024]{0,1:T(8,128)(2,1)S(1)} %slice.317), channel_id=1, source_target_pairs={{0,64},{1,193},{64,0},{65,129},{128,192},{129,65},{192,128},{193,1... | collective-permute-start | bytes 786440 | tf_op jit(solution)/shard_map/ppermute | solution.py:25
  109.9 13.6 %collective-permute-start.12 = (bf16[512,512]{1,0:T(8,128)(2,1)S(1)}, bf16[512,512]{1,0:T(8,128)(2,1)S(1)}, u32[]{:S(2)}, u32[]{:S(2)}) collective-permute-start(bf16[512,512]{1,0:T(8,128)(2,1)S(1)} %fusion.41), channel_id=1, source_target_pairs={{0,16},{1,49},{16,0},{17,33},{32,48},{33,17},{48,32},{49,1},{2,18}... | collective-permute-start | bytes 1572872 | tf_op jit(solution)/shard_map/ppermute | solution.py:25
  115.5 7.7 %collective-permute-start.17 = (bf16[32,1024]{0,1:T(8,128)(2,1)S(1)}, bf16[32,1024]{0,1:T(8,128)(2,1)S(1)}, u32[]{:S(2)}, u32[]{:S(2)}) collective-permute-start(bf16[32,1024]{0,1:T(8,128)(2,1)S(1)} %slice.316), channel_id=1, source_target_pairs={{0,14},{1,3},{2,4},{3,1},{4,2},{5,7},{6,8},{7,5},{8,6},{9,11},{10,... | collective-permute-start | bytes 196616 | tf_op jit(solution)/shard_map/ppermute | solution.py:25
  123.4 7.3 %collective-permute-start.18 = (bf16[32,1024]{0,1:T(8,128)(2,1)S(1)}, bf16[32,1024]{0,1:T(8,128)(2,1)S(1)}, u32[]{:S(2)}, u32[]{:S(2)}) collective-permute-start(bf16[32,1024]{0,1:T(8,128)(2,1)S(1)} %fusion.48), channel_id=1, source_target_pairs={{0,2},{1,15},{2,0},{3,5},{4,6},{5,3},{6,4},{7,9},{8,10},{9,7},{10,... | collective-permute-start | bytes 196616 | tf_op jit(solution)/shard_map/ppermute | solution.py:25
  130.9 8.9 %collective-permute-start.19 = (bf16[32,1024]{0,1:T(8,128)(2,1)S(1)}, bf16[32,1024]{0,1:T(8,128)(2,1)S(1)}, u32[]{:S(2)}, u32[]{:S(2)}) collective-permute-start(bf16[32,1024]{0,1:T(8,128)(2,1)S(1)} %fusion.49), channel_id=1, source_target_pairs={{0,14},{1,3},{2,4},{3,1},{4,2},{5,7},{6,8},{7,5},{8,6},{9,11},{10,... | collective-permute-start | bytes 196616 | tf_op jit(solution)/shard_map/ppermute | solution.py:25
  134.0 6.2 %collective-permute-start.13 = (bf16[512,256]{1,0:T(8,128)(2,1)S(1)}, bf16[512,256]{1,0:T(8,128)(2,1)S(1)}, u32[]{:S(2)}, u32[]{:S(2)}) collective-permute-start(bf16[512,256]{1,0:T(8,128)(2,1)S(1)} %get-tuple-element.11), channel_id=1, source_target_pairs={{0,1},{1,0},{2,3},{3,2},{4,5},{5,4},{6,7},{7,6},{8,9},{9,8},{10,11... | collective-permute-start | bytes 786440 | tf_op jit(solution)/shard_map/ppermute | solution.py:29
  140.0 6.5 %collective-permute-start.20 = (bf16[16,1024]{0,1:T(8,128)(2,1)S(1)}, bf16[16,1024]{0,1:T(8,128)(2,1)S(1)}, u32[]{:S(2)}, u32[]{:S(2)}) collective-permute-start(bf16[16,1024]{0,1:T(8,128)(2,1)S(1)} %slice.315), channel_id=1, source_target_pairs={{0,2},{1,15},{2,0},{3,5},{4,6},{5,3},{6,4},{7,9},{8,10},{9,7},{10,... | collective-permute-start | bytes 98312 | tf_op jit(solution)/shard_map/ppermute | solution.py:25

commit v2 on v1

v2 whole, which is shorter than its diff:
```python
import jax
import jax.numpy as jnp
from jax import lax
from jax.experimental import pallas as pl
from jax.experimental.pallas import tpu as pltpu
from jax.sharding import Mesh
from jax.sharding import PartitionSpec as P

SLAB = ("slab_0", "slab_1", "slab_2")
F32 = jnp.float32
BF16 = jnp.bfloat16


def neighbour(i, n, turn):
    if turn == 0:
        return i ^ 1
    return (i - 1) % n if i % 2 == 0 else (i + 1) % n


def trade(x, axis, turn):
    n = lax.axis_size(axis)
    pairs = []
    for i in range(n):
        for core in range(2):
            j = neighbour(i, n, (turn + core) % 2)
            pairs.append((2 * i + core, 2 * j + core))
    return lax.ppermute(x, (axis, "kv"), pairs)


def swap(x):
    return lax.ppermute(x, "kv", [(0, 1), (1, 0)])


def three_parts(v):
    hi = lax.reduce_precision(v, 8, 7)
    rest = v - hi
    mid = lax.reduce_precision(rest, 8, 7)
    low = rest - mid
    return jnp.stack([hi, mid, low]).astype(BF16)


def dot(left, right, ld, rd):
    return lax.dot_general(left, right, (((ld,), (rd,)), ((), ())), preferred_element_type=F32)


def block_kernel(n_packs, first, add, pack_refs, panel_ref, dq_in, sum_in, dq_out, sum_out):
    half, channels = dq_out[0].shape
    log2e = 1.4426950408889634
    scale = channels ** (-0.5) * log2e
    k, v = panel_ref[:, :channels], panel_ref[:, channels:]
    dk, dv = None, None
    for i in range(n_packs):
        q, g = pack_refs[i][:half, :channels], pack_refs[i][:half, channels:]
        both = jnp.sum(pack_refs[i][half:, :].astype(F32), axis=0, keepdims=True)
        lse, stats = both[:, :half] * log2e, both[:, half:]
        probs = jnp.exp2(dot(k, q, 1, 1) * scale - lse)
        dscores = (probs * (dot(v, g, 1, 1) - stats)).astype(BF16)
        dk_i = dot(dscores, q, 1, 0)
        dv_i = dot(probs.astype(BF16), g, 1, 0)
        dk = dk_i if dk is None else dk + dk_i
        dv = dv_i if dv is None else dv + dv_i
        dq = dot(dscores, k, 0, 0)
        dq_out[i][...] = dq if first else dq_in[i][...] + dq
    if add:
        dk, dv = dk + sum_in[:, :channels], dv + sum_in[:, channels:]
    sum_out[:, :channels] = dk.astype(sum_out.dtype)
    sum_out[:, channels:] = dv.astype(sum_out.dtype)


def block_work(packs, panel, dqs, total, out_type):
    n_packs, first, add = len(packs), dqs is None, total is not None
    half, channels = packs[0].shape[0] - 16, packs[0].shape[1] // 2
    keys = panel.shape[0]

    def body(*refs):
        refs = list(refs)
        pack_refs = [refs.pop(0) for _ in range(n_packs)]
        panel_ref = refs.pop(0)
        dq_in = None if first else [refs.pop(0) for _ in range(n_packs)]
        sum_in = refs.pop(0) if add else None
        dq_out = [refs.pop(0) for _ in range(n_packs)]
        block_kernel(n_packs, first, add, pack_refs, panel_ref, dq_in, sum_in, dq_out, refs.pop(0))

    args = [*packs, panel, *([] if first else dqs), *([total] if add else [])]
    aliases = {} if first else {n_packs + 1 + i: i for i in range(n_packs)}
    if add and out_type == F32:
        aliases[len(args) - 1] = n_packs
    vmem = pl.BlockSpec(memory_space=pltpu.VMEM)
    out = pl.pallas_call(
        body,
        out_shape=[jax.ShapeDtypeStruct((half, channels), F32)] * n_packs
        + [jax.ShapeDtypeStruct((keys, 2 * channels), out_type)],
        in_specs=[vmem] * len(args),
        out_specs=[vmem] * (n_packs + 1),
        input_output_aliases=aliases,
        cost_estimate=pl.CostEstimate(
            flops=10 * n_packs * half * keys * channels,
            bytes_accessed=2 * n_packs * half * channels * 2,
            transcendentals=n_packs * half * keys,
        ),
        compiler_params=pltpu.CompilerParams(vmem_limit_bytes=16 * 1024 * 1024),
    )(*args)
    return list(out[:n_packs]), out[n_packs]


def steps(queries, grad_out, attn_out, row_lse, keys, values):
    tokens, channels = queries.shape
    scale = channels ** (-0.5)
    core = lax.axis_index("kv")
    half = tokens // 2

    def my_half(a):
        return lax.dynamic_slice_in_dim(a, core * half, half, 0)

    q, g, o, lse = my_half(queries), my_half(grad_out), my_half(attn_out), my_half(row_lse)
    stats = jnp.sum(g.astype(F32) * o.astype(F32), axis=1)
    extra = three_parts(jnp.concatenate([lse, stats]))
    extra = jnp.pad(extra, ((0, 13), (0, 0)))
    pack0 = jnp.concatenate([jnp.concatenate([q, g], axis=1), extra])
    pack1 = trade(pack0, "slab_1", 0)
    pack2 = trade(pack0, "slab_1", 1)
    pack3 = trade(pack1, "slab_1", 1)

    k0 = jnp.concatenate([keys[0], values[0]], axis=1)
    z1 = trade(k0, "slab_2", 0)
    z2 = trade(jnp.concatenate([k0, z1]), "slab_2", 1)
    z3 = trade(z2, "slab_2", 0)
    z4 = trade(z3, "slab_2", 1)
    zall = jnp.concatenate([k0, z1, z2, z3, z4])
    y1 = trade(zall, "slab_0", 0)
    near = jnp.concatenate([zall, y1])
    far = trade(near, "slab_0", 1)
    near_other = swap(near)
    far_other = swap(far)

    a = [pack0, pack1]
    b = [pack2, pack3]
    dqa, near_sum = block_work(a, near, None, None, F32)
    dqa, near_osum = block_work(a, near_other, dqa, None, F32)
    dqa, far_sum = block_work(a, far, dqa, None, F32)
    dqa, far_osum = block_work(a, far_other, dqa, None, F32)
    dqb, far_osum = block_work(b, far_other, None, far_osum, BF16)
    dqb, far_sum = block_work(b, far, dqb, far_sum, F32)
    dqb, near_osum = block_work(b, near_other, dqb, near_osum, BF16)
    dqb, near_sum = block_work(b, near, dqb, near_sum, F32)

    far_sum = far_sum + swap(far_osum).astype(F32)
    near_sum = near_sum + swap(near_osum).astype(F32)
    n1, n = keys.shape[1], keys.shape[1] * 8
    total = near_sum + trade(far_sum.astype(BF16), "slab_0", 1).astype(F32)
    total = total[:n] + trade(total[n:].astype(BF16), "slab_0", 0).astype(F32)
    t0, t2, t3, t4 = total[: 2 * n1], total[2 * n1 : 4 * n1], total[4 * n1 : 6 * n1], total[6 * n1 :]
    t3 = t3 + trade(t4.astype(BF16), "slab_2", 1).astype(F32)
    t2 = t2 + trade(t3.astype(BF16), "slab_2", 0).astype(F32)
    t0 = t0 + trade(t2.astype(BF16), "slab_2", 1).astype(F32)
    own = t0[:n1] + trade(t0[n1:].astype(BF16), "slab_2", 0).astype(F32)
    grad_keys = (own[:, :channels] * scale).astype(BF16)[None]
    grad_values = own[:, channels:].astype(BF16)[None]

    got3 = trade(dqb[1].astype(BF16), "slab_1", 1).astype(F32)
    got2 = trade(dqb[0].astype(BF16), "slab_1", 1).astype(F32)
    got1 = trade((dqa[1] + got3).astype(BF16), "slab_1", 0).astype(F32)
    dq = ((dqa[0] + got2 + got1) * scale).astype(BF16)
    width = channels // 2
    keep = lax.dynamic_slice_in_dim(dq, core * width, width, 1)
    away = swap(lax.dynamic_slice_in_dim(dq, (1 - core) * width, width, 1))
    grad_queries = jnp.where(core == 0, jnp.concatenate([keep, away]), jnp.concatenate([away, keep]))
    return (grad_queries, grad_keys, grad_values)


def solution(mesh):
    torus = Mesh(
        mesh.devices.reshape(4, 4, 8, mesh.shape["kv"]), ("slab_0", "slab_1", "slab_2", "kv")
    )
    placed = (
        P(SLAB, None),
        P(SLAB, None),
        P(SLAB, None),
        P(SLAB),
        P("kv", SLAB, None),
        P("kv", SLAB, None),
    )
    return jax.shard_map(
        steps,
        mesh=torus,
        in_specs=placed,
        out_specs=(P(SLAB, "kv"), P("kv", SLAB, None), P("kv", SLAB, None)),
        check_vma=False,
    )
```

time: 149 us -> 112 us (0.75)
  the two profiles are of different devices: /device:TPU:24 before, /device:TPU:6 now
where the time goes in v2:
time: 112 us
  waiting for transfers between devices  56.3 us (50%)
  starting transfers between devices  31.8 us (28%)
  Pallas kernels  15.1 us (13%)
  other arithmetic  5.04 us (4%)
  local copies, waits for them, and re-layouts  2.74 us (2%)
    ppermute x18, waiting for transfers between devices, trade(): return lax.ppermute(x, (axis, 'kv'), pairs)  56.3 us
    ppermute x18, starting transfers between devices, trade(): return lax.ppermute(x, (axis, 'kv'), pairs)  30.8 us
    pallas_call x8, Pallas kernels, block_work(): pl.pallas_call(body, out_shape=[jax.ShapeDtypeStruct((half, channels), F3...  15.1 us
  transfers between devices with their start and end apart: 23, of which 16 were waited for; matrix products, arithmetic and copies ran while one was open for 3% of the time, Pallas kernels for 12%

profile of v2, /device:TPU:6, one launch (start us, length us, event | category | flops | bytes accessed | tf_op | source)
XLA Modules:
  0.0 112.0 jit_solution(9439659079888834906)
XLA Ops:
  5.2 2.0 %collective-permute-start.1 = (bf16[16,1024]{1,0:T(8,128)(2,1)S(1)}, bf16[16,1024]{1,0:T(8,128)(2,1)S(1)}, u32[]{:S(2)}, u32[]{:S(2)}) collective-permute-start(bf16[16,1024]{1,0:T(8,128)(2,1)S(1)} %get-tuple-element.63), channel_id=1, source_target_pairs={{0,2},{1,15},{2,0},{3,5},{4,6},{5,3},{6,4},{7,9},{8,10},{9,7},{10,... | collective-permute-start | bytes 98312 | tf_op jit(solution)/shard_map/ppermute | solution.py:27
  7.2 2.0 %collective-permute-done.1 = bf16[16,1024]{1,0:T(8,128)(2,1)S(1)} collective-permute-done((bf16[16,1024]{1,0:T(8,128)(2,1)S(1)}, bf16[16,1024]{1,0:T(8,128)(2,1)S(1)}, u32[]{:S(2)}, u32[]{:S(2)}) %collective-permute-start.1) | collective-permute-done | bytes 32800 | tf_op jit(solution)/shard_map/ppermute | solution.py:27
  9.2 5.9 %collective-permute-start.2 = (bf16[32,1024]{1,0:T(8,128)(2,1)S(1)}, bf16[32,1024]{1,0:T(8,128)(2,1)S(1)}, u32[]{:S(2)}, u32[]{:S(2)}) collective-permute-start(bf16[32,1024]{1,0:T(8,128)(2,1)S(1)} %pad_maximum_fusion.1), channel_id=1, source_target_pairs={{0,14},{1,3},{2,4},{3,1},{4,2},{5,7},{6,8},{7,5},{8,6},{9,11},{10,... | collective-permute-start | bytes 196616 | tf_op jit(solution)/shard_map/ppermute | solution.py:27
  15.1 2.2 %collective-permute-done.2 = bf16[32,1024]{1,0:T(8,128)(2,1)S(1)} collective-permute-done((bf16[32,1024]{1,0:T(8,128)(2,1)S(1)}, bf16[32,1024]{1,0:T(8,128)(2,1)S(1)}, u32[]{:S(2)}, u32[]{:S(2)}) %collective-permute-start.2) | collective-permute-done | bytes 65568 | tf_op jit(solution)/shard_map/ppermute | solution.py:27
  17.3 4.2 %collective-permute-done.3 = bf16[32,1024]{1,0:T(8,128)(2,1)S(1)} collective-permute-done((bf16[32,1024]{1,0:T(8,128)(2,1)S(1)}, bf16[32,1024]{1,0:T(8,128)(2,1)S(1)}, u32[]{:S(2)}, u32[]{:S(2)}) %collective-permute-start.3) | collective-permute-done | bytes 65568 | tf_op jit(solution)/shard_map/ppermute | solution.py:27
  21.6 3.2 %collective-permute-start.4 = (bf16[32,1024]{1,0:T(8,128)(2,1)S(1)}, bf16[32,1024]{1,0:T(8,128)(2,1)S(1)}, u32[]{:S(2)}, u32[]{:S(2)}) collective-permute-start(bf16[32,1024]{1,0:T(8,128)(2,1)S(1)} %collective-permute-done.3), channel_id=1, source_target_pairs={{0,14},{1,3},{2,4},{3,1},{4,2},{5,7},{6,8},{7,5},{8,6},{9,11},{10,... | collective-permute-start | bytes 196616 | tf_op jit(solution)/shard_map/ppermute | solution.py:27
  24.8 2.2 %collective-permute-done.4 = bf16[32,1024]{1,0:T(8,128)(2,1)S(1)} collective-permute-done((bf16[32,1024]{1,0:T(8,128)(2,1)S(1)}, bf16[32,1024]{1,0:T(8,128)(2,1)S(1)}, u32[]{:S(2)}, u32[]{:S(2)}) %collective-permute-start.4) | collective-permute-done | bytes 65568 | tf_op jit(solution)/shard_map/ppermute | solution.py:27
  28.7 6.7 %collective-permute-done.5 = bf16[128,1024]{1,0:T(8,128)(2,1)S(1)} collective-permute-done((bf16[128,1024]{1,0:T(8,128)(2,1)S(1)}, bf16[128,1024]{1,0:T(8,128)(2,1)S(1)}, u32[]{:S(2)}, u32[]{:S(2)}) %collective-permute-start.5) | collective-permute-done | bytes 262176 | tf_op jit(solution)/shard_map/ppermute | solution.py:27
  35.5 3.0 %collective-permute-start.6 = (bf16[256,1024]{1,0:T(8,128)(2,1)S(1)}, bf16[256,1024]{1,0:T(8,128)(2,1)S(1)}, u32[]{:S(2)}, u32[]{:S(2)}) collective-permute-start(bf16[256,1024]{1,0:T(8,128)(2,1)S(1)} %constant_dynamic-update-slice_fusion.5.refs_2_), channel_id=1, source_target_pairs={{0,192},{1,65},{64,128},{65,1},{128,64},{129,193},{192,0},{193,129... | collective-permute-start | bytes 1572872 | tf_op jit(solution)/shard_map/ppermute | solution.py:27
  38.5 3.2 %collective-permute-start.10 = (bf16[528,1024]{1,0:T(8,128)(2,1)S(1)}, bf16[528,1024]{1,0:T(8,128)(2,1)S(1)}, u32[]{:S(2)}, u32[]{:S(2)}) collective-permute-start(bf16[528,1024]{1,0:T(8,128)(2,1)S(1)} %collective-permute-done.refs_1_), channel_id=1, source_target_pairs={{0,48},{1,17},{16,32},{17,1},{32,16},{33,49},{48,0},{49,33},{2,50}... | collective-permute-start | bytes 3244040 | tf_op jit(solution)/shard_map/ppermute | solution.py:27
  41.7 4.2 %collective-permute-done.6.refs_2_ = bf16[256,1024]{1,0:T(8,128)(2,1)S(1)} collective-permute-done((bf16[256,1024]{1,0:T(8,128)(2,1)S(1)}, bf16[256,1024]{1,0:T(8,128)(2,1)S(1)}, u32[]{:S(2)}, u32[]{:S(2)}) %collective-permute-start.6) | collective-permute-done | bytes 524320 | tf_op jit(solution)/shard_map/ppermute | solution.py:27
  54.8 11.6 %collective-permute-done.10.refs_1_ = bf16[528,1024]{1,0:T(8,128)(2,1)S(1)} collective-permute-done((bf16[528,1024]{1,0:T(8,128)(2,1)S(1)}, bf16[528,1024]{1,0:T(8,128)(2,1)S(1)}, u32[]{:S(2)}, u32[]{:S(2)}) %collective-permute-start.10) | collective-permute-done | bytes 1081376 | tf_op jit(solution)/shard_map/ppermute | solution.py:27
  68.3 2.0 %shard_map.90 = (f32[512,512]{1,0:T(8,128)S(1)}, f32[512,512]{1,0:T(8,128)S(1)}, f32[256,1024]{1,0:T(8,128)S(1)}) custom-call(bf16[528,1024]{1,0:T(8,128)(2,1)S(1)} %collective-permute-done.9.refs_0_, bf16[528,1024]{1,0:T(8,128)(2,1)S(1)} %collective-permute-done.10.refs_1_, ...), custom_call_target="tpu_custom_call", output_to_operand_aliasing={{0}: (3, {}), {1}: (4, {}), {2}: (5, {})} | custom-call | flops 1342177280 | bytes 2097152 | tf_op jit(solution)/shard_map/pallas_call | solution.py:89
  73.6 2.0 %shard_map.92 = (f32[512,512]{1,0:T(8,128)S(1)}, f32[512,512]{1,0:T(8,128)S(1)}, f32[256,1024]{1,0:T(8,128)S(1)}) custom-call(bf16[528,1024]{1,0:T(8,128)(2,1)S(1)} %collective-permute-done.9.refs_0_, bf16[528,1024]{1,0:T(8,128)(2,1)S(1)} %collective-permute-done.10.refs_1_, ...), custom_call_target="tpu_custom_call", output_to_operand_aliasing={{0}: (3, {}), {1}: (4, {}), {2}: (5, {})} | custom-call | flops 1342177280 | bytes 2097152 | tf_op jit(solution)/shard_map/pallas_call | solution.py:89
  75.8 3.3 %collective-permute-start.11 = (bf16[512,512]{1,0:T(8,128)(2,1)S(1)}, bf16[512,512]{1,0:T(8,128)(2,1)S(1)}, u32[]{:S(2)}, u32[]{:S(2)}) collective-permute-start(bf16[512,512]{1,0:T(8,128)(2,1)S(1)} %convert_element_type.72), channel_id=1, source_target_pairs={{0,48},{1,17},{16,32},{17,1},{32,16},{33,49},{48,0},{49,33},{2,50}... | collective-permute-start | bytes 1572872 | tf_op jit(solution)/shard_map/ppermute | solution.py:27
  79.1 4.5 %collective-permute-done.17 = bf16[256,1024]{1,0:T(8,128)(2,1)S(1)} collective-permute-done((bf16[256,1024]{1,0:T(8,128)(2,1)S(1)}, bf16[256,1024]{1,0:T(8,128)(2,1)S(1)}, u32[]{:S(2)}, u32[]{:S(2)}) %collective-permute-start.17) | collective-permute-done | bytes 524320 | tf_op jit(solution)/shard_map/ppermute | solution.py:27
  84.0 2.1 %collective-permute-done.12 = bf16[512,512]{1,0:T(8,128)(2,1)S(1)} collective-permute-done((bf16[512,512]{1,0:T(8,128)(2,1)S(1)}, bf16[512,512]{1,0:T(8,128)(2,1)S(1)}, u32[]{:S(2)}, u32[]{:S(2)}) %collective-permute-start.12) | collective-permute-done | bytes 524320 | tf_op jit(solution)/shard_map/ppermute | solution.py:27
  87.1 3.3 %collective-permute-done.18 = bf16[128,1024]{1,0:T(8,128)(2,1)S(1)} collective-permute-done((bf16[128,1024]{1,0:T(8,128)(2,1)S(1)}, bf16[128,1024]{1,0:T(8,128)(2,1)S(1)}, u32[]{:S(2)}, u32[]{:S(2)}) %collective-permute-start.18) | collective-permute-done | bytes 262176 | tf_op jit(solution)/shard_map/ppermute | solution.py:27
  90.5 3.5 %collective-permute-start.19 = (bf16[32,1024]{1,0:T(8,128)(2,1)S(1)}, bf16[32,1024]{1,0:T(8,128)(2,1)S(1)}, u32[]{:S(2)}, u32[]{:S(2)}) collective-permute-start(bf16[32,1024]{1,0:T(8,128)(2,1)S(1)} %slice.75), channel_id=1, source_target_pairs={{0,14},{1,3},{2,4},{3,1},{4,2},{5,7},{6,8},{7,5},{8,6},{9,11},{10,... | collective-permute-start | bytes 196616 | tf_op jit(solution)/shard_map/ppermute | solution.py:27
  94.0 2.2 %collective-permute-done.19 = bf16[32,1024]{1,0:T(8,128)(2,1)S(1)} collective-permute-done((bf16[32,1024]{1,0:T(8,128)(2,1)S(1)}, bf16[32,1024]{1,0:T(8,128)(2,1)S(1)}, u32[]{:S(2)}, u32[]{:S(2)}) %collective-permute-start.19) | collective-permute-done | bytes 65568 | tf_op jit(solution)/shard_map/ppermute | solution.py:27
  96.7 4.5 %collective-permute-done.20 = bf16[32,1024]{1,0:T(8,128)(2,1)S(1)} collective-permute-done((bf16[32,1024]{1,0:T(8,128)(2,1)S(1)}, bf16[32,1024]{1,0:T(8,128)(2,1)S(1)}, u32[]{:S(2)}, u32[]{:S(2)}) %collective-permute-start.20) | collective-permute-done | bytes 65568 | tf_op jit(solution)/shard_map/ppermute | solution.py:27
  101.2 3.2 %collective-permute-start.21 = (bf16[32,1024]{1,0:T(8,128)(2,1)S(1)}, bf16[32,1024]{1,0:T(8,128)(2,1)S(1)}, u32[]{:S(2)}, u32[]{:S(2)}) collective-permute-start(bf16[32,1024]{1,0:T(8,128)(2,1)S(1)} %fusion.1), channel_id=1, source_target_pairs={{0,14},{1,3},{2,4},{3,1},{4,2},{5,7},{6,8},{7,5},{8,6},{9,11},{10,... | collective-permute-start | bytes 196616 | tf_op jit(solution)/shard_map/ppermute | solution.py:27
  104.6 2.2 %collective-permute-done.21 = bf16[32,1024]{1,0:T(8,128)(2,1)S(1)} collective-permute-done((bf16[32,1024]{1,0:T(8,128)(2,1)S(1)}, bf16[32,1024]{1,0:T(8,128)(2,1)S(1)}, u32[]{:S(2)}, u32[]{:S(2)}) %collective-permute-start.21) | collective-permute-done | bytes 65568 | tf_op jit(solution)/shard_map/ppermute | solution.py:27
  107.9 2.9 %collective-permute-done.22 = bf16[16,1024]{1,0:T(8,128)(2,1)S(1)} collective-permute-done((bf16[16,1024]{1,0:T(8,128)(2,1)S(1)}, bf16[16,1024]{1,0:T(8,128)(2,1)S(1)}, u32[]{:S(2)}, u32[]{:S(2)}) %collective-permute-start.22) | collective-permute-done | bytes 32800 | tf_op jit(solution)/shard_map/ppermute | solution.py:27
  (67 shorter events, 24.8 us)
Async XLA Ops:
  0.6 2.3 %copy-start = (bf16[1024,512]{1,0:T(8,128)(2,1)S(1)}, bf16[1024,512]{1,0:T(8,128)(2,1)}, u32[]{:S(2)}) copy-start(bf16[1024,512]{1,0:T(8,128)(2,1)} %param.7) | copy-start | bytes 3145732
  4.3 34.2 %collective-permute-start = (bf16[528,1024]{1,0:T(8,128)(2,1)S(1)}, bf16[528,1024]{1,0:T(8,128)(2,1)S(1)}, u32[]{:S(2)}, u32[]{:S(2)}) collective-permute-start(bf16[528,1024]{1,0:T(8,128)(2,1)S(1)} %pad_maximum_fusion.refs_0_), channel_id=1, source_target_pairs={{0,16},{1,49},{16,0},{17,33},{32,48},{33,17},{48,32},{49,1},{2,18}... | collective-permute-start | bytes 3244040 | tf_op jit(solution)/shard_map/ppermute | solution.py:27
  5.2 4.0 %collective-permute-start.1 = (bf16[16,1024]{1,0:T(8,128)(2,1)S(1)}, bf16[16,1024]{1,0:T(8,128)(2,1)S(1)}, u32[]{:S(2)}, u32[]{:S(2)}) collective-permute-start(bf16[16,1024]{1,0:T(8,128)(2,1)S(1)} %get-tuple-element.63), channel_id=1, source_target_pairs={{0,2},{1,15},{2,0},{3,5},{4,6},{5,3},{6,4},{7,9},{8,10},{9,7},{10,... | collective-permute-start | bytes 98312 | tf_op jit(solution)/shard_map/ppermute | solution.py:27
  9.2 8.1 %collective-permute-start.2 = (bf16[32,1024]{1,0:T(8,128)(2,1)S(1)}, bf16[32,1024]{1,0:T(8,128)(2,1)S(1)}, u32[]{:S(2)}, u32[]{:S(2)}) collective-permute-start(bf16[32,1024]{1,0:T(8,128)(2,1)S(1)} %pad_maximum_fusion.1), channel_id=1, source_target_pairs={{0,14},{1,3},{2,4},{3,1},{4,2},{5,7},{6,8},{7,5},{8,6},{9,11},{10,... | collective-permute-start | bytes 196616 | tf_op jit(solution)/shard_map/ppermute | solution.py:27
  17.3 4.3 %collective-permute-start.3 = (bf16[32,1024]{1,0:T(8,128)(2,1)S(1)}, bf16[32,1024]{1,0:T(8,128)(2,1)S(1)}, u32[]{:S(2)}, u32[]{:S(2)}) collective-permute-start(bf16[32,1024]{1,0:T(8,128)(2,1)S(1)} %collective-permute-done.2), channel_id=1, source_target_pairs={{0,2},{1,15},{2,0},{3,5},{4,6},{5,3},{6,4},{7,9},{8,10},{9,7},{10,... | collective-permute-start | bytes 196616 | tf_op jit(solution)/shard_map/ppermute | solution.py:27
  21.6 5.5 %collective-permute-start.4 = (bf16[32,1024]{1,0:T(8,128)(2,1)S(1)}, bf16[32,1024]{1,0:T(8,128)(2,1)S(1)}, u32[]{:S(2)}, u32[]{:S(2)}) collective-permute-start(bf16[32,1024]{1,0:T(8,128)(2,1)S(1)} %collective-permute-done.3), channel_id=1, source_target_pairs={{0,14},{1,3},{2,4},{3,1},{4,2},{5,7},{6,8},{7,5},{8,6},{9,11},{10,... | collective-permute-start | bytes 196616 | tf_op jit(solution)/shard_map/ppermute | solution.py:27
  27.1 8.4 %collective-permute-start.5 = (bf16[128,1024]{1,0:T(8,128)(2,1)S(1)}, bf16[128,1024]{1,0:T(8,128)(2,1)S(1)}, u32[]{:S(2)}, u32[]{:S(2)}) collective-permute-start(bf16[128,1024]{1,0:T(8,128)(2,1)S(1)} %get-tuple-element.53), channel_id=1, source_target_pairs={{0,64},{1,193},{64,0},{65,129},{128,192},{129,65},{192,128},{193,1... | collective-permute-start | bytes 786440 | tf_op jit(solution)/shard_map/ppermute | solution.py:27
  35.5 10.5 %collective-permute-start.6 = (bf16[256,1024]{1,0:T(8,128)(2,1)S(1)}, bf16[256,1024]{1,0:T(8,128)(2,1)S(1)}, u32[]{:S(2)}, u32[]{:S(2)}) collective-permute-start(bf16[256,1024]{1,0:T(8,128)(2,1)S(1)} %constant_dynamic-update-slice_fusion.5.refs_2_), channel_id=1, source_target_pairs={{0,192},{1,65},{64,128},{65,1},{128,64},{129,193},{192,0},{193,129... | collective-permute-start | bytes 1572872 | tf_op jit(solution)/shard_map/ppermute | solution.py:27
  38.4 16.4 %collective-permute-start.9 = (bf16[528,1024]{1,0:T(8,128)(2,1)S(1)}, bf16[528,1024]{1,0:T(8,128)(2,1)S(1)}, u32[]{:S(2)}, u32[]{:S(2)}) collective-permute-start(bf16[528,1024]{1,0:T(8,128)(2,1)S(1)} %pad_maximum_fusion.refs_0_), channel_id=1, source_target_pairs={{0,48},{1,17},{16,32},{17,1},{32,16},{33,49},{48,0},{49,33},{2,50}... | collective-permute-start | bytes 3244040 | tf_op jit(solution)/shard_map/ppermute | solution.py:27
  38.5 27.9 %collective-permute-start.10 = (bf16[528,1024]{1,0:T(8,128)(2,1)S(1)}, bf16[528,1024]{1,0:T(8,128)(2,1)S(1)}, u32[]{:S(2)}, u32[]{:S(2)}) collective-permute-start(bf16[528,1024]{1,0:T(8,128)(2,1)S(1)} %collective-permute-done.refs_1_), channel_id=1, source_target_pairs={{0,48},{1,17},{16,32},{17,1},{32,16},{33,49},{48,0},{49,33},{2,50}... | collective-permute-start | bytes 3244040 | tf_op jit(solution)/shard_map/ppermute | solution.py:27
  41.7 6.1 %collective-permute-start.8 = (bf16[256,1024]{1,0:T(8,128)(2,1)S(1)}, bf16[256,1024]{1,0:T(8,128)(2,1)S(1)}, u32[]{:S(2)}, u32[]{:S(2)}) collective-permute-start(bf16[256,1024]{1,0:T(8,128)(2,1)S(1)} %constant_dynamic-update-slice_fusion.5.refs_2_), channel_id=1, source_target_pairs={{0,1},{1,0},{2,3},{3,2},{4,5},{5,4},{6,7},{7,6},{8,9},{9,8},{10,11... | collective-permute-start | bytes 1572872 | tf_op jit(solution)/shard_map/ppermute | solution.py:31
  45.9 5.6 %collective-permute-start.7 = (bf16[256,1024]{1,0:T(8,128)(2,1)S(1)}, bf16[256,1024]{1,0:T(8,128)(2,1)S(1)}, u32[]{:S(2)}, u32[]{:S(2)}) collective-permute-start(bf16[256,1024]{1,0:T(8,128)(2,1)S(1)} %collective-permute-done.6.refs_2_), channel_id=1, source_target_pairs={{0,1},{1,0},{2,3},{3,2},{4,5},{5,4},{6,7},{7,6},{8,9},{9,8},{10,11... | collective-permute-start | bytes 1572872 | tf_op jit(solution)/shard_map/ppermute | solution.py:31
  68.2 4.8 %collective-permute-start.16 = (bf16[256,1024]{1,0:T(8,128)(2,1)S(1)}, bf16[256,1024]{1,0:T(8,128)(2,1)S(1)}, u32[]{:S(2)}, u32[]{:S(2)}) collective-permute-start(bf16[256,1024]{1,0:T(8,128)(2,1)S(1)} %get-tuple-element.50), channel_id=1, source_target_pairs={{0,1},{1,0},{2,3},{3,2},{4,5},{5,4},{6,7},{7,6},{8,9},{9,8},{10,11... | collective-permute-start | bytes 1572872 | tf_op jit(solution)/shard_map/ppermute | solution.py:31
  72.2 6.9 %collective-permute-start.15 = (bf16[256,1024]{1,0:T(8,128)(2,1)S(1)}, bf16[256,1024]{1,0:T(8,128)(2,1)S(1)}, u32[]{:S(2)}, u32[]{:S(2)}) collective-permute-start(bf16[256,1024]{1,0:T(8,128)(2,1)S(1)} %get-tuple-element.48), channel_id=1, source_target_pairs={{0,1},{1,0},{2,3},{3,2},{4,5},{5,4},{6,7},{7,6},{8,9},{9,8},{10,11... | collective-permute-start | bytes 1572872 | tf_op jit(solution)/shard_map/ppermute | solution.py:31
  73.2 10.5 %collective-permute-start.17 = (bf16[256,1024]{1,0:T(8,128)(2,1)S(1)}, bf16[256,1024]{1,0:T(8,128)(2,1)S(1)}, u32[]{:S(2)}, u32[]{:S(2)}) collective-permute-start(bf16[256,1024]{1,0:T(8,128)(2,1)S(1)} %add_convert_fusion), channel_id=1, source_target_pairs={{0,192},{1,65},{64,128},{65,1},{128,64},{129,193},{192,0},{193,129... | collective-permute-start | bytes 1572872 | tf_op jit(solution)/shard_map/ppermute | solution.py:27
  75.6 10.5 %collective-permute-start.12 = (bf16[512,512]{1,0:T(8,128)(2,1)S(1)}, bf16[512,512]{1,0:T(8,128)(2,1)S(1)}, u32[]{:S(2)}, u32[]{:S(2)}) collective-permute-start(bf16[512,512]{1,0:T(8,128)(2,1)S(1)} %convert_element_type.74), channel_id=1, source_target_pairs={{0,48},{1,17},{16,32},{17,1},{32,16},{33,49},{48,0},{49,33},{2,50}... | collective-permute-start | bytes 1572872 | tf_op jit(solution)/shard_map/ppermute | solution.py:27
  75.8 20.6 %collective-permute-start.11 = (bf16[512,512]{1,0:T(8,128)(2,1)S(1)}, bf16[512,512]{1,0:T(8,128)(2,1)S(1)}, u32[]{:S(2)}, u32[]{:S(2)}) collective-permute-start(bf16[512,512]{1,0:T(8,128)(2,1)S(1)} %convert_element_type.72), channel_id=1, source_target_pairs={{0,48},{1,17},{16,32},{17,1},{32,16},{33,49},{48,0},{49,33},{2,50}... | collective-permute-start | bytes 1572872 | tf_op jit(solution)/shard_map/ppermute | solution.py:27
  83.9 6.5 %collective-permute-start.18 = (bf16[128,1024]{1,0:T(8,128)(2,1)S(1)}, bf16[128,1024]{1,0:T(8,128)(2,1)S(1)}, u32[]{:S(2)}, u32[]{:S(2)}) collective-permute-start(bf16[128,1024]{1,0:T(8,128)(2,1)S(1)} %slice.74), channel_id=1, source_target_pairs={{0,64},{1,193},{64,0},{65,129},{128,192},{129,65},{192,128},{193,1... | collective-permute-start | bytes 786440 | tf_op jit(solution)/shard_map/ppermute | solution.py:27
  87.1 9.4 %collective-permute-start.13 = (bf16[512,512]{1,0:T(8,128)(2,1)}, bf16[512,512]{1,0:T(8,128)(2,1)S(1)}, u32[]{:S(2)}, u32[]{:S(2)}) collective-permute-start(bf16[512,512]{1,0:T(8,128)(2,1)} %add_convert_fusion.1), channel_id=1, source_target_pairs={{0,16},{1,49},{16,0},{17,33},{32,48},{33,17},{48,32},{49,1},{2,18}... | collective-permute-start | bytes 1572872 | tf_op jit(solution)/shard_map/ppermute | solution.py:27
  90.5 5.8 %collective-permute-start.19 = (bf16[32,1024]{1,0:T(8,128)(2,1)S(1)}, bf16[32,1024]{1,0:T(8,128)(2,1)S(1)}, u32[]{:S(2)}, u32[]{:S(2)}) collective-permute-start(bf16[32,1024]{1,0:T(8,128)(2,1)S(1)} %slice.75), channel_id=1, source_target_pairs={{0,14},{1,3},{2,4},{3,1},{4,2},{5,7},{6,8},{7,5},{8,6},{9,11},{10,... | collective-permute-start | bytes 196616 | tf_op jit(solution)/shard_map/ppermute | solution.py:27
  96.3 4.9 %collective-permute-start.20 = (bf16[32,1024]{1,0:T(8,128)(2,1)S(1)}, bf16[32,1024]{1,0:T(8,128)(2,1)S(1)}, u32[]{:S(2)}, u32[]{:S(2)}) collective-permute-start(bf16[32,1024]{1,0:T(8,128)(2,1)S(1)} %fusion), channel_id=1, source_target_pairs={{0,2},{1,15},{2,0},{3,5},{4,6},{5,3},{6,4},{7,9},{8,10},{9,7},{10,... | collective-permute-start | bytes 196616 | tf_op jit(solution)/shard_map/ppermute | solution.py:27
  101.2 5.6 %collective-permute-start.21 = (bf16[32,1024]{1,0:T(8,128)(2,1)S(1)}, bf16[32,1024]{1,0:T(8,128)(2,1)S(1)}, u32[]{:S(2)}, u32[]{:S(2)}) collective-permute-start(bf16[32,1024]{1,0:T(8,128)(2,1)S(1)} %fusion.1), channel_id=1, source_target_pairs={{0,14},{1,3},{2,4},{3,1},{4,2},{5,7},{6,8},{7,5},{8,6},{9,11},{10,... | collective-permute-start | bytes 196616 | tf_op jit(solution)/shard_map/ppermute | solution.py:27
  104.5 2.4 %collective-permute-start.14 = (bf16[512,256]{1,0:T(8,128)(2,1)S(1)}, bf16[512,256]{1,0:T(8,128)(2,1)S(1)}, u32[]{:S(2)}, u32[]{:S(2)}) collective-permute-start(bf16[512,256]{1,0:T(8,128)(2,1)S(1)} %get-tuple-element.52), channel_id=1, source_target_pairs={{0,1},{1,0},{2,3},{3,2},{4,5},{5,4},{6,7},{7,6},{8,9},{9,8},{10,11... | collective-permute-start | bytes 786440 | tf_op jit(solution)/shard_map/ppermute | solution.py:31
  106.8 4.0 %collective-permute-start.22 = (bf16[16,1024]{1,0:T(8,128)(2,1)S(1)}, bf16[16,1024]{1,0:T(8,128)(2,1)S(1)}, u32[]{:S(2)}, u32[]{:S(2)}) collective-permute-start(bf16[16,1024]{1,0:T(8,128)(2,1)S(1)} %slice.76), channel_id=1, source_target_pairs={{0,2},{1,15},{2,0},{3,5},{4,6},{5,3},{6,4},{7,9},{8,10},{9,7},{10,... | collective-permute-start | bytes 98312 | tf_op jit(solution)/shard_map/ppermute | solution.py:27
  (2 other events, 2.2 us)

commit v3 on v2

--- a/solution.py
+++ b/solution.py
@@ -1,3 +1,5 @@
+import functools
+
 import jax
 import jax.numpy as jnp
 from jax import lax
@@ -31,12 +33,111 @@
     return lax.ppermute(x, "kv", [(0, 1), (1, 0)])
 
 
-def three_parts(v):
-    hi = lax.reduce_precision(v, 8, 7)
-    rest = v - hi
-    mid = lax.reduce_precision(rest, 8, 7)
-    low = rest - mid
-    return jnp.stack([hi, mid, low]).astype(BF16)
+def across(x):
+    return lax.all_to_all(x, "slab_2", 0, 0, tiled=True)
+
+
+def pack_kernel(
+    core_ref, q_hbm, g_hbm, o_hbm, lse_hbm, k_hbm, v_hbm, out_ref, own_ref, o_half, lse_ref, kv_ref, sems
+):
+    half, channels = o_half.shape
+    core = core_ref[0]
+    piece = 128
+    n = half // piece
+    copies = []
+    for i in range(n):
+        rows = pl.ds(pl.multiple_of(core * half + i * piece, piece), piece)
+        to = slice(i * piece, (i + 1) * piece)
+        copies.append(
+            (
+                pltpu.make_async_copy(g_hbm.at[rows, :], out_ref.at[to, channels:], sems.at[i]),
+                pltpu.make_async_copy(o_hbm.at[rows, :], o_half.at[to, :], sems.at[n + i]),
+                pltpu.make_async_copy(q_hbm.at[rows, :], out_ref.at[to, :channels], sems.at[2 * n + i]),
+            )
+        )
+    small = [
+        pltpu.make_async_copy(lse_hbm, lse_ref, sems.at[3 * n]),
+        pltpu.make_async_copy(k_hbm.at[0], kv_ref.at[:, :channels], sems.at[3 * n + 1]),
+        pltpu.make_async_copy(v_hbm.at[0], kv_ref.at[:, channels:], sems.at[3 * n + 2]),
+    ]
+    for copy in small:
+        copy.start()
+    for trio in copies:
+        trio[0].start()
+        trio[1].start()
+    for trio in copies:
+        trio[2].start()
+    for copy in small:
+        copy.wait()
+    for i in range(own_ref.shape[0]):
+        own_ref[i] = kv_ref[...]
+
+    def line(first):
+        return jnp.concatenate([lse_ref[i : i + 1, :] for i in range(first, first + n)], axis=1)
+
+    lse = jnp.where(core == 0, line(0), line(n))
+    pieces = []
+    for i in range(n):
+        copies[i][0].wait()
+        copies[i][1].wait()
+        to = slice(i * piece, (i + 1) * piece)
+        product = out_ref[to, channels:].astype(F32) * o_half[to, :].astype(F32)
+        column = jnp.sum(product, axis=1, keepdims=True)
+        pieces.append(jnp.transpose(jnp.broadcast_to(column, (piece, 128)))[:1, :])
+    stats = jnp.concatenate(pieces, axis=1)
+    row = lax.broadcasted_iota(jnp.int32, (16, half), 0)
+    for at, v in ((0, lse), (half, stats)):
+        hi = v.astype(BF16).astype(F32)
+        mid = (v - hi).astype(BF16).astype(F32)
+        low = v - hi - mid
+        terms = jnp.where(row == 0, hi, jnp.where(row == 1, mid, jnp.where(row == 2, low, 0.0)))
+        out_ref[half:, at : at + half] = terms.astype(BF16)
+    for trio in copies:
+        trio[2].wait()
+
+
+def make_pack(core, queries, grad_out, attn_out, row_lse, keys, values):
+    tokens, channels = queries.shape
+    half = tokens // 2
+    arrays = (queries, grad_out, attn_out, row_lse.reshape(-1, 128), keys, values)
+    arrays = [pltpu.with_memory_space_constraint(a, pltpu.HBM) for a in arrays]
+    hbm = pl.BlockSpec(memory_space=pltpu.HBM)
+    vmem = pl.BlockSpec(memory_space=pltpu.VMEM)
+    rows = keys.shape[1]
+    return pl.pallas_call(
+        pack_kernel,
+        out_shape=[
+            jax.ShapeDtypeStruct((half + 16, 2 * channels), BF16),
+            jax.ShapeDtypeStruct((8, rows, 2 * channels), BF16),
+        ],
+        in_specs=[pl.BlockSpec(memory_space=pltpu.SMEM)] + [hbm] * 6,
+        out_specs=[vmem, vmem],
+        scratch_shapes=[
+            pltpu.VMEM((half, channels), BF16),
+            pltpu.VMEM((tokens // 128, 128), F32),
+            pltpu.VMEM((rows, 2 * channels), BF16),
+            pltpu.SemaphoreType.DMA((15,)),
+        ],
+        compiler_params=pltpu.CompilerParams(vmem_limit_bytes=16 * 1024 * 1024),
+        name="pack",
+    )(core.reshape(1), *arrays)
+
+
+def finish_kernel(scale, parts_ref, k_ref, v_ref):
+    channels = k_ref.shape[2]
+    own = jnp.sum(parts_ref[...].astype(F32), axis=0)
+    k_ref[0] = (own[:, :channels] * scale).astype(BF16)
+    v_ref[0] = own[:, channels:].astype(BF16)
+
+
+def finish(parts, scale):
+    rows, channels = parts.shape[1], parts.shape[2] // 2
+    return pl.pallas_call(
+        functools.partial(finish_kernel, scale),
+        out_shape=[jax.ShapeDtypeStruct((1, rows, channels), BF16)] * 2,
+        compiler_params=pltpu.CompilerParams(vmem_limit_bytes=4 * 1024 * 1024),
+        name="finish",
+    )(parts)
 
 
 def dot(left, right, ld, rd):
@@ -104,37 +205,24 @@
 
 
 def steps(queries, grad_out, attn_out, row_lse, keys, values):
-    tokens, channels = queries.shape
+    _, channels = queries.shape
     scale = channels ** (-0.5)
     core = lax.axis_index("kv")
-    half = tokens // 2
-
-    def my_half(a):
-        return lax.dynamic_slice_in_dim(a, core * half, half, 0)
-
-    q, g, o, lse = my_half(queries), my_half(grad_out), my_half(attn_out), my_half(row_lse)
-    stats = jnp.sum(g.astype(F32) * o.astype(F32), axis=1)
-    extra = three_parts(jnp.concatenate([lse, stats]))
-    extra = jnp.pad(extra, ((0, 13), (0, 0)))
-    pack0 = jnp.concatenate([jnp.concatenate([q, g], axis=1), extra])
+
+    pack0, k0 = make_pack(core, queries, grad_out, attn_out, row_lse, keys, values)
     pack1 = trade(pack0, "slab_1", 0)
     pack2 = trade(pack0, "slab_1", 1)
     pack3 = trade(pack1, "slab_1", 1)
 
-    k0 = jnp.concatenate([keys[0], values[0]], axis=1)
-    z1 = trade(k0, "slab_2", 0)
-    z2 = trade(jnp.concatenate([k0, z1]), "slab_2", 1)
-    z3 = trade(z2, "slab_2", 0)
-    z4 = trade(z3, "slab_2", 1)
-    zall = jnp.concatenate([k0, z1, z2, z3, z4])
+    zall = across(k0).reshape(-1, k0.shape[2])
     y1 = trade(zall, "slab_0", 0)
     near = jnp.concatenate([zall, y1])
     far = trade(near, "slab_0", 1)
     near_other = swap(near)
     far_other = swap(far)
 
-    a = [pack0, pack1]
-    b = [pack2, pack3]
+    a = [pack0, pack1, pack2]
+    b = [pack3]
     dqa, near_sum = block_work(a, near, None, None, F32)
     dqa, near_osum = block_work(a, near_other, dqa, None, F32)
     dqa, far_sum = block_work(a, far, dqa, None, F32)
@@ -149,22 +237,19 @@
     n1, n = keys.shape[1], keys.shape[1] * 8
     total = near_sum + trade(far_sum.astype(BF16), "slab_0", 1).astype(F32)
     total = total[:n] + trade(total[n:].astype(BF16), "slab_0", 0).astype(F32)
-    t0, t2, t3, t4 = total[: 2 * n1], total[2 * n1 : 4 * n1], total[4 * n1 : 6 * n1], total[6 * n1 :]
-    t3 = t3 + trade(t4.astype(BF16), "slab_2", 1).astype(F32)
-    t2 = t2 + trade(t3.astype(BF16), "slab_2", 0).astype(F32)
-    t0 = t0 + trade(t2.astype(BF16), "slab_2", 1).astype(F32)
-    own = t0[:n1] + trade(t0[n1:].astype(BF16), "slab_2", 0).astype(F32)
-    grad_keys = (own[:, :channels] * scale).astype(BF16)[None]
-    grad_values = own[:, channels:].astype(BF16)[None]
-
-    got3 = trade(dqb[1].astype(BF16), "slab_1", 1).astype(F32)
-    got2 = trade(dqb[0].astype(BF16), "slab_1", 1).astype(F32)
+    parts = across(total.astype(BF16).reshape(8, n1, -1))
+    grad_keys, grad_values = finish(parts, scale)
+
+    got3 = trade(dqb[0].astype(BF16), "slab_1", 1).astype(F32)
+    got2 = trade(dqa[2].astype(BF16), "slab_1", 1).astype(F32)
     got1 = trade((dqa[1] + got3).astype(BF16), "slab_1", 0).astype(F32)
     dq = ((dqa[0] + got2 + got1) * scale).astype(BF16)
     width = channels // 2
     keep = lax.dynamic_slice_in_dim(dq, core * width, width, 1)
     away = swap(lax.dynamic_slice_in_dim(dq, (1 - core) * width, width, 1))
-    grad_queries = jnp.where(core == 0, jnp.concatenate([keep, away]), jnp.concatenate([away, keep]))
+    grad_queries = jnp.where(
+        core == 0, jnp.concatenate([keep, away]), jnp.concatenate([away, keep])
+    )
     return (grad_queries, grad_keys, grad_values)
 
 

time: 112 us -> 107 us (0.955)
  the two profiles are of different devices: /device:TPU:6 before, /device:TPU:24 now
where the time goes in v3:
time: 107 us; the launch traced here: 105 us
  waiting for transfers between devices  50.2 us (47%)
  Pallas kernels  23.4 us (22%)
  starting transfers between devices  22.3 us (21%)
  other arithmetic  7.36 us (7%)
  local copies, waits for them, and re-layouts  1.31 us (1%)
    ppermute x10, waiting for transfers between devices, trade(): return lax.ppermute(x, (axis, 'kv'), pairs)  28.3 us
    all_to_all x2, waiting for transfers between devices, across(): return lax.all_to_all(x, 'slab_2', 0, 0, tiled=True)  20.7 us
    pallas_call x8, Pallas kernels, block_work(): pl.pallas_call(body, out_shape=[jax.ShapeDtypeStruct((half, channels), F3...  20.3 us
    all_to_all x2, starting transfers between devices, across(): return lax.all_to_all(x, 'slab_2', 0, 0, tiled=True)  11.9 us
    ppermute x10, starting transfers between devices, trade(): return lax.ppermute(x, (axis, 'kv'), pairs)  8.83 us
    pallas_call x1, Pallas kernels, make_pack(): pl.pallas_call(pack_kernel, out_shape=[jax.ShapeDtypeStruct((half + 16, 2...  2.47 us
  transfers between devices with their start and end apart: 17, of which 9 were waited for; matrix products, arithmetic and copies ran while one was open for 6% of the time, Pallas kernels for 18%

profile of v3, /device:TPU:24, one launch (start us, length us, event | category | flops | bytes accessed | tf_op | source)
XLA Modules:
  0.0 105.5 jit_solution(4749360862677489605)
XLA Ops:
  0.6 2.5 %pack.1 = (bf16[528,1024]{1,0:T(8,128)(2,1)S(1)}, bf16[8,16,1024]{2,1,0:T(8,128)(2,1)}) custom-call(s32[1]{0:T(128)} %bitcast.core_ref, bf16[1024,512]{1,0:T(8,128)(2,1)} %q_hbm.1, bf16[1024,512]{1,0:T(8,128)(2,1)} %g_hbm.1, bf16[1024,512]{1,0:T(8,128)(2,1)} %o_hbm.1, f32[8,128]{1,0:T(8,128)} %bitcast.6, bf16[1,16,512]{2,1,0:T(8,128)(2,1)} %k_hbm.1, ...), custom_call_target="tpu_custom_call" | custom-call | tf_op jit(solution)/shard_map/pack/pallas_call | solution.py:107
  3.1 1.6 %collective-permute-start = (bf16[528,1024]{1,0:T(8,128)(2,1)S(1)}, bf16[528,1024]{1,0:T(8,128)(2,1)S(1)}, u32[]{:S(2)}, u32[]{:S(2)}) collective-permute-start(bf16[528,1024]{1,0:T(8,128)(2,1)S(1)} %get-tuple-element.31.refs_0_), channel_id=1, source_target_pairs={{0,16},{1,49},{16,0},{17,33},{32,48},{33,17},{48,32},{49,1},{2,18}... | collective-permute-start | bytes 3244040 | tf_op jit(solution)/shard_map/ppermute | solution.py:29
  4.7 8.5 %all-to-all-start = ((bf16[8,16,1024]{2,1,0:T(8,128)(2,1)}), bf16[8,16,1024]{2,1,0:T(8,128)(2,1)S(1)}, u32[]{:S(2)}, u32[]{:S(2)}) async-start(bf16[8,16,1024]{2,1,0:T(8,128)(2,1)} %get-tuple-element.32), calls=%async_computation | async-start | bytes 524288 | tf_op jit(solution)/shard_map/all_to_all | solution.py:37
  13.2 2.1 %collective-permute-start.1 = (bf16[528,1024]{1,0:T(8,128)(2,1)S(1)}, bf16[528,1024]{1,0:T(8,128)(2,1)}, u32[]{:S(2)}, u32[]{:S(2)}) collective-permute-start(bf16[528,1024]{1,0:T(8,128)(2,1)S(1)} %get-tuple-element.31.refs_0_), channel_id=1, source_target_pairs={{0,48},{1,17},{16,32},{17,1},{32,16},{33,49},{48,0},{49,33},{2,50}... | collective-permute-start | bytes 3244040 | tf_op jit(solution)/shard_map/ppermute | solution.py:29
  15.3 10.8 %all-to-all-done = bf16[8,16,1024]{2,1,0:T(8,128)(2,1)S(1)} async-done(((bf16[8,16,1024]{2,1,0:T(8,128)(2,1)}), bf16[8,16,1024]{2,1,0:T(8,128)(2,1)S(1)}, u32[]{:S(2)}, u32[]{:S(2)}) %all-to-all-start) | async-done | bytes 262176 | tf_op jit(solution)/shard_map/all_to_all | solution.py:37
  26.8 5.6 %collective-permute-done.2 = bf16[128,1024]{1,0:T(8,128)(2,1)S(1)} collective-permute-done((bf16[128,1024]{1,0:T(8,128)(2,1)S(1)}, bf16[128,1024]{1,0:T(8,128)(2,1)S(1)}, u32[]{:S(2)}, u32[]{:S(2)}) %collective-permute-start.2) | collective-permute-done | bytes 262176 | tf_op jit(solution)/shard_map/ppermute | solution.py:29
  33.2 9.7 %collective-permute-done.3.refs_3_.refs_1_ = bf16[256,1024]{1,0:T(8,128)(2,1)S(1)} collective-permute-done((bf16[256,1024]{1,0:T(8,128)(2,1)S(1)}, bf16[256,1024]{1,0:T(8,128)(2,1)S(1)}, u32[]{:S(2)}, u32[]{:S(2)}) %collective-permute-start.3) | collective-permute-done | bytes 524320 | tf_op jit(solution)/shard_map/ppermute | solution.py:29
  42.9 1.2 %copy-done.1 = bf16[528,1024]{1,0:T(8,128)(2,1)S(1)} copy-done((bf16[528,1024]{1,0:T(8,128)(2,1)S(1)}, bf16[528,1024]{1,0:T(8,128)(2,1)}, u32[]{:S(2)}) %copy-start.1) | copy-done | bytes 1081368
  44.2 3.8 %shard_map.85 = (f32[512,512]{1,0:T(8,128)S(1)}, f32[512,512]{1,0:T(8,128)S(1)}, f32[512,512]{1,0:T(8,128)S(1)}, f32[256,1024]{1,0:T(8,128)S(1)}) custom-call(bf16[528,1024]{1,0:T(8,128)(2,1)S(1)} %copy-done.1, bf16[528,1024]{1,0:T(8,128)(2,1)S(1)} %collective-permute-done.refs_1_, bf16[528,1024]{1,0:T(8,128)(2,1)} %collective-permute-done.1.refs_2_, ...), custom_call_target="tpu_custom_call" | custom-call | flops 2013265920 | bytes 3145728 | tf_op jit(solution)/shard_map/pallas_call | solution.py:190
  48.0 4.0 %shard_map.86 = (f32[512,512]{1,0:T(8,128)S(1)}, f32[512,512]{1,0:T(8,128)S(1)}, f32[512,512]{1,0:T(8,128)S(1)}, f32[256,1024]{1,0:T(8,128)S(1)}) custom-call(bf16[528,1024]{1,0:T(8,128)(2,1)S(1)} %copy-done.1, bf16[528,1024]{1,0:T(8,128)(2,1)S(1)} %collective-permute-done.refs_1_, ...), custom_call_target="tpu_custom_call", output_to_operand_aliasing={{0}: (4, {}), {1}: (5, {}), {2}: (6, {})} | custom-call | flops 2013265920 | bytes 3145728 | tf_op jit(solution)/shard_map/pallas_call | solution.py:190
  52.1 4.1 %shard_map.87 = (f32[512,512]{1,0:T(8,128)S(1)}, f32[512,512]{1,0:T(8,128)S(1)}, f32[512,512]{1,0:T(8,128)S(1)}, f32[256,1024]{1,0:T(8,128)S(1)}) custom-call(bf16[528,1024]{1,0:T(8,128)(2,1)S(1)} %copy-done.1, bf16[528,1024]{1,0:T(8,128)(2,1)S(1)} %collective-permute-done.refs_1_, ...), custom_call_target="tpu_custom_call", output_to_operand_aliasing={{0}: (4, {}), {1}: (5, {}), {2}: (6, {})} | custom-call | flops 2013265920 | bytes 3145728 | tf_op jit(solution)/shard_map/pallas_call | solution.py:190
  56.2 4.0 %shard_map.88 = (f32[512,512]{1,0:T(8,128)S(1)}, f32[512,512]{1,0:T(8,128)S(1)}, f32[512,512]{1,0:T(8,128)S(1)}, f32[256,1024]{1,0:T(8,128)S(1)}) custom-call(bf16[528,1024]{1,0:T(8,128)(2,1)S(1)} %copy-done.2, bf16[528,1024]{1,0:T(8,128)(2,1)S(1)} %collective-permute-done.refs_1_, ...), custom_call_target="tpu_custom_call", output_to_operand_aliasing={{0}: (4, {}), {1}: (5, {}), {2}: (6, {})} | custom-call | flops 2013265920 | bytes 3145728 | tf_op jit(solution)/shard_map/pallas_call | solution.py:190
  62.1 1.1 %shard_map.90 = (f32[512,512]{1,0:T(8,128)S(1)}, f32[256,1024]{1,0:T(8,128)S(1)}) custom-call(bf16[528,1024]{1,0:T(8,128)(2,1)S(1)} %collective-permute-done.7.refs_0_, bf16[256,1024]{1,0:T(8,128)(2,1)S(1)} %collective-permute-done.3.refs_3_.refs_1_, f32[512,512]{1,0:T(8,128)S(1)} %get-tuple-element.46.refs_2_, ...), custom_call_target="tpu_custom_call", output_to_operand_aliasing={{0}: (2, {}), {1}: (3, {})} | custom-call | flops 671088640 | bytes 1048576 | tf_op jit(solution)/shard_map/pallas_call | solution.py:190
  63.2 1.1 %shard_map.91 = (f32[512,512]{1,0:T(8,128)S(1)}, bf16[256,1024]{1,0:T(8,128)(2,1)S(1)}) custom-call(bf16[528,1024]{1,0:T(8,128)(2,1)S(1)} %collective-permute-done.7.refs_0_, bf16[256,1024]{1,0:T(8,128)(2,1)S(1)} %collective-permute-done.5.refs_3_.refs_1_, f32[512,512]{1,0:T(8,128)S(1)} %get-tuple-element.48.refs_2_, ...), custom_call_target="tpu_custom_call", output_to_operand_aliasing={{0}: (2, {})} | custom-call | flops 671088640 | bytes 1048576 | tf_op jit(solution)/shard_map/pallas_call | solution.py:190
  64.3 1.1 %shard_map.92 = (f32[512,512]{1,0:T(8,128)S(1)}, f32[256,1024]{1,0:T(8,128)S(1)}) custom-call(bf16[528,1024]{1,0:T(8,128)(2,1)S(1)} %collective-permute-done.7.refs_0_, bf16[256,1024]{1,0:T(8,128)(2,1)S(1)} %pad_maximum_fusion.refs_3_.refs_1_, f32[512,512]{1,0:T(8,128)S(1)} %get-tuple-element.50.refs_2_, ...), custom_call_target="tpu_custom_call", output_to_operand_aliasing={{0}: (2, {}), {1}: (3, {})} | custom-call | flops 671088640 | bytes 1048576 | tf_op jit(solution)/shard_map/pallas_call | solution.py:190
  68.1 2.7 %collective-permute-start.6 = (bf16[512,512]{1,0:T(8,128)(2,1)}, bf16[512,512]{1,0:T(8,128)(2,1)S(1)}, u32[]{:S(2)}, u32[]{:S(2)}) collective-permute-start(bf16[512,512]{1,0:T(8,128)(2,1)} %convert_element_type.40), channel_id=1, source_target_pairs={{0,48},{1,17},{16,32},{17,1},{32,16},{33,49},{48,0},{49,33},{2,50}... | collective-permute-start | bytes 1572872 | tf_op jit(solution)/shard_map/ppermute | solution.py:29
  70.9 5.1 %collective-permute-done.8 = bf16[512,512]{1,0:T(8,128)(2,1)S(1)} collective-permute-done((bf16[512,512]{1,0:T(8,128)(2,1)S(1)}, bf16[512,512]{1,0:T(8,128)(2,1)S(1)}, u32[]{:S(2)}, u32[]{:S(2)}) %collective-permute-start.8) | collective-permute-done | bytes 524320 | tf_op jit(solution)/shard_map/ppermute | solution.py:29
  77.7 1.4 %convert_add_fusion = f32[256,1024]{1,0:T(8,128)S(1)} fusion(bf16[256,1024]{1,0:T(8,128)(2,1)} %collective-permute-done.13, f32[256,1024]{1,0:T(8,128)S(1)} %get-tuple-element.53, bf16[256,1024]{1,0:T(8,128)(2,1)} %collective-permute-done.11), kind=kLoop, calls=%fused_computation | loop fusion | flops 1048576 | bytes 3145728 | tf_op jit(solution)/shard_map/add | solution.py:238
  79.3 4.8 %collective-permute-done.6 = bf16[512,512]{1,0:T(8,128)(2,1)S(1)} collective-permute-done((bf16[512,512]{1,0:T(8,128)(2,1)}, bf16[512,512]{1,0:T(8,128)(2,1)S(1)}, u32[]{:S(2)}, u32[]{:S(2)}) %collective-permute-start.6) | collective-permute-done | bytes 524320 | tf_op jit(solution)/shard_map/ppermute | solution.py:29
  84.2 2.2 %collective-permute-done.9 = bf16[512,512]{1,0:T(8,128)(2,1)} collective-permute-done((bf16[512,512]{1,0:T(8,128)(2,1)}, bf16[512,512]{1,0:T(8,128)(2,1)}, u32[]{:S(2)}, u32[]{:S(2)}) %collective-permute-start.9) | collective-permute-done | bytes 524320 | tf_op jit(solution)/shard_map/ppermute | solution.py:29
  86.4 1.3 %multiply_convert_fusion = bf16[512,512]{1,0:T(8,128)(2,1)S(1)} fusion(bf16[512,512]{1,0:T(8,128)(2,1)} %collective-permute-done.9, f32[512,512]{1,0:T(8,128)S(1)} %get-tuple-element.42, bf16[512,512]{1,0:T(8,128)(2,1)S(1)} %collective-permute-done.6), kind=kLoop, calls=%fused_computation.2 | loop fusion | flops 1572864 | bytes 2621440 | tf_op jit(solution)/shard_map/convert_element_type | solution.py:246
  88.5 3.4 %all-to-all-start.1 = ((bf16[8,16,1024]{2,1,0:T(8,128)(2,1)}), bf16[8,16,1024]{2,1,0:T(8,128)(2,1)S(1)}, u32[]{:S(2)}, u32[]{:S(2)}) async-start(bf16[8,16,1024]{2,1,0:T(8,128)(2,1)} %bitcast.3), calls=%async_computation.1 | async-start | bytes 524288 | tf_op jit(solution)/shard_map/all_to_all | solution.py:37
  92.7 1.2 %collective-permute-done.10 = bf16[512,256]{1,0:T(8,128)(2,1)S(1)} collective-permute-done((bf16[512,256]{1,0:T(8,128)(2,1)S(1)}, bf16[512,256]{1,0:T(8,128)(2,1)S(1)}, u32[]{:S(2)}, u32[]{:S(2)}) %collective-permute-start.10) | collective-permute-done | bytes 262176 | tf_op jit(solution)/shard_map/ppermute | solution.py:33
  94.9 9.9 %all-to-all-done.1.parts_ref = bf16[8,16,1024]{2,1,0:T(8,128)(2,1)S(1)} async-done(((bf16[8,16,1024]{2,1,0:T(8,128)(2,1)}), bf16[8,16,1024]{2,1,0:T(8,128)(2,1)S(1)}, u32[]{:S(2)}, u32[]{:S(2)}) %all-to-all-start.1) | async-done | bytes 262176 | tf_op jit(solution)/shard_map/all_to_all | solution.py:37
  (37 shorter events, 11.3 us)
Async XLA Ops:
  3.1 39.8 %copy-start = (bf16[528,1024]{1,0:T(8,128)(2,1)}, bf16[528,1024]{1,0:T(8,128)(2,1)S(1)}, u32[]{:S(2)}) copy-start(bf16[528,1024]{1,0:T(8,128)(2,1)S(1)} %get-tuple-element.31.refs_0_) | copy-start | bytes 3244036
  3.1 29.6 %collective-permute-start = (bf16[528,1024]{1,0:T(8,128)(2,1)S(1)}, bf16[528,1024]{1,0:T(8,128)(2,1)S(1)}, u32[]{:S(2)}, u32[]{:S(2)}) collective-permute-start(bf16[528,1024]{1,0:T(8,128)(2,1)S(1)} %get-tuple-element.31.refs_0_), channel_id=1, source_target_pairs={{0,16},{1,49},{16,0},{17,33},{32,48},{33,17},{48,32},{49,1},{2,18}... | collective-permute-start | bytes 3244040 | tf_op jit(solution)/shard_map/ppermute | solution.py:29
  4.7 21.3 %all-to-all-start = ((bf16[8,16,1024]{2,1,0:T(8,128)(2,1)}), bf16[8,16,1024]{2,1,0:T(8,128)(2,1)S(1)}, u32[]{:S(2)}, u32[]{:S(2)}) async-start(bf16[8,16,1024]{2,1,0:T(8,128)(2,1)} %get-tuple-element.32), calls=%async_computation | async-start | bytes 524288 | tf_op jit(solution)/shard_map/all_to_all | solution.py:37
  13.2 29.8 %collective-permute-start.1 = (bf16[528,1024]{1,0:T(8,128)(2,1)S(1)}, bf16[528,1024]{1,0:T(8,128)(2,1)}, u32[]{:S(2)}, u32[]{:S(2)}) collective-permute-start(bf16[528,1024]{1,0:T(8,128)(2,1)S(1)} %get-tuple-element.31.refs_0_), channel_id=1, source_target_pairs={{0,48},{1,17},{16,32},{17,1},{32,16},{33,49},{48,0},{49,33},{2,50}... | collective-permute-start | bytes 3244040 | tf_op jit(solution)/shard_map/ppermute | solution.py:29
  26.0 6.4 %collective-permute-start.2 = (bf16[128,1024]{1,0:T(8,128)(2,1)S(1)}, bf16[128,1024]{1,0:T(8,128)(2,1)S(1)}, u32[]{:S(2)}, u32[]{:S(2)}) collective-permute-start(bf16[128,1024]{1,0:T(8,128)(2,1)S(1)} %bitcast.4), channel_id=1, source_target_pairs={{0,64},{1,193},{64,0},{65,129},{128,192},{129,65},{192,128},{193,1... | collective-permute-start | bytes 786440 | tf_op jit(solution)/shard_map/ppermute | solution.py:29
  32.4 10.5 %collective-permute-start.3 = (bf16[256,1024]{1,0:T(8,128)(2,1)S(1)}, bf16[256,1024]{1,0:T(8,128)(2,1)S(1)}, u32[]{:S(2)}, u32[]{:S(2)}) collective-permute-start(bf16[256,1024]{1,0:T(8,128)(2,1)S(1)} %pad_maximum_fusion.refs_3_.refs_1_), channel_id=1, source_target_pairs={{0,192},{1,65},{64,128},{65,1},{128,64},{129,193},{192,0},{193,129... | collective-permute-start | bytes 1572872 | tf_op jit(solution)/shard_map/ppermute | solution.py:29
  32.8 15.3 %collective-permute-start.5 = (bf16[256,1024]{1,0:T(8,128)(2,1)S(1)}, bf16[256,1024]{1,0:T(8,128)(2,1)S(1)}, u32[]{:S(2)}, u32[]{:S(2)}) collective-permute-start(bf16[256,1024]{1,0:T(8,128)(2,1)S(1)} %pad_maximum_fusion.refs_3_.refs_1_), channel_id=1, source_target_pairs={{0,1},{1,0},{2,3},{3,2},{4,5},{5,4},{6,7},{7,6},{8,9},{9,8},{10,11... | collective-permute-start | bytes 1572872 | tf_op jit(solution)/shard_map/ppermute | solution.py:33
  32.8 27.4 %collective-permute-start.7 = (bf16[528,1024]{1,0:T(8,128)(2,1)S(1)}, bf16[528,1024]{1,0:T(8,128)(2,1)S(1)}, u32[]{:S(2)}, u32[]{:S(2)}) collective-permute-start(bf16[528,1024]{1,0:T(8,128)(2,1)S(1)} %collective-permute-done.refs_1_), channel_id=1, source_target_pairs={{0,48},{1,17},{16,32},{17,1},{32,16},{33,49},{48,0},{49,33},{2,50}... | collective-permute-start | bytes 3244040 | tf_op jit(solution)/shard_map/ppermute | solution.py:29
  42.9 13.2 %collective-permute-start.4 = (bf16[256,1024]{1,0:T(8,128)(2,1)S(1)}, bf16[256,1024]{1,0:T(8,128)(2,1)S(1)}, u32[]{:S(2)}, u32[]{:S(2)}) collective-permute-start(bf16[256,1024]{1,0:T(8,128)(2,1)S(1)} %collective-permute-done.3.refs_3_.refs_1_), channel_id=1, source_target_pairs={{0,1},{1,0},{2,3},{3,2},{4,5},{5,4},{6,7},{7,6},{8,9},{9,8},{10,11... | collective-permute-start | bytes 1572872 | tf_op jit(solution)/shard_map/ppermute | solution.py:33
  42.9 1.2 %copy-start.1 = (bf16[528,1024]{1,0:T(8,128)(2,1)S(1)}, bf16[528,1024]{1,0:T(8,128)(2,1)}, u32[]{:S(2)}) copy-start(bf16[528,1024]{1,0:T(8,128)(2,1)} %copy-done) | copy-start | bytes 3244036
  52.0 4.1 %copy-start.2 = (bf16[528,1024]{1,0:T(8,128)(2,1)S(1)}, bf16[528,1024]{1,0:T(8,128)(2,1)}, u32[]{:S(2)}) copy-start(bf16[528,1024]{1,0:T(8,128)(2,1)} %copy-done) | copy-start | bytes 3244036
  61.3 4.8 %collective-permute-start.12 = (bf16[256,1024]{1,0:T(8,128)(2,1)S(1)}, bf16[256,1024]{1,0:T(8,128)(2,1)S(1)}, u32[]{:S(2)}, u32[]{:S(2)}) collective-permute-start(bf16[256,1024]{1,0:T(8,128)(2,1)S(1)} %get-tuple-element.56), channel_id=1, source_target_pairs={{0,1},{1,0},{2,3},{3,2},{4,5},{5,4},{6,7},{7,6},{8,9},{9,8},{10,11... | collective-permute-start | bytes 1572872 | tf_op jit(solution)/shard_map/ppermute | solution.py:33
  65.5 10.5 %collective-permute-start.8 = (bf16[512,512]{1,0:T(8,128)(2,1)S(1)}, bf16[512,512]{1,0:T(8,128)(2,1)S(1)}, u32[]{:S(2)}, u32[]{:S(2)}) collective-permute-start(bf16[512,512]{1,0:T(8,128)(2,1)S(1)} %convert_element_type.42), channel_id=1, source_target_pairs={{0,48},{1,17},{16,32},{17,1},{32,16},{33,49},{48,0},{49,33},{2,50}... | collective-permute-start | bytes 1572872 | tf_op jit(solution)/shard_map/ppermute | solution.py:29
  66.1 10.9 %collective-permute-start.11 = (bf16[256,1024]{1,0:T(8,128)(2,1)S(1)}, bf16[256,1024]{1,0:T(8,128)(2,1)}, u32[]{:S(2)}, u32[]{:S(2)}) collective-permute-start(bf16[256,1024]{1,0:T(8,128)(2,1)S(1)} %get-tuple-element.54), channel_id=1, source_target_pairs={{0,1},{1,0},{2,3},{3,2},{4,5},{5,4},{6,7},{7,6},{8,9},{9,8},{10,11... | collective-permute-start | bytes 1572872 | tf_op jit(solution)/shard_map/ppermute | solution.py:33
  67.0 10.7 %collective-permute-start.13 = (bf16[256,1024]{1,0:T(8,128)(2,1)}, bf16[256,1024]{1,0:T(8,128)(2,1)}, u32[]{:S(2)}, u32[]{:S(2)}) collective-permute-start(bf16[256,1024]{1,0:T(8,128)(2,1)} %add_convert_fusion), channel_id=1, source_target_pairs={{0,192},{1,65},{64,128},{65,1},{128,64},{129,193},{192,0},{193,129... | collective-permute-start | bytes 1572872 | tf_op jit(solution)/shard_map/ppermute | solution.py:29
  68.1 16.0 %collective-permute-start.6 = (bf16[512,512]{1,0:T(8,128)(2,1)}, bf16[512,512]{1,0:T(8,128)(2,1)S(1)}, u32[]{:S(2)}, u32[]{:S(2)}) collective-permute-start(bf16[512,512]{1,0:T(8,128)(2,1)} %convert_element_type.40), channel_id=1, source_target_pairs={{0,48},{1,17},{16,32},{17,1},{32,16},{33,49},{48,0},{49,33},{2,50}... | collective-permute-start | bytes 1572872 | tf_op jit(solution)/shard_map/ppermute | solution.py:29
  76.9 9.5 %collective-permute-start.9 = (bf16[512,512]{1,0:T(8,128)(2,1)}, bf16[512,512]{1,0:T(8,128)(2,1)}, u32[]{:S(2)}, u32[]{:S(2)}) collective-permute-start(bf16[512,512]{1,0:T(8,128)(2,1)} %add_convert_fusion.1), channel_id=1, source_target_pairs={{0,16},{1,49},{16,0},{17,33},{32,48},{33,17},{48,32},{49,1},{2,18}... | collective-permute-start | bytes 1572872 | tf_op jit(solution)/shard_map/ppermute | solution.py:29
  79.2 8.5 %collective-permute-start.14 = (bf16[128,1024]{1,0:T(8,128)(2,1)S(1)}, bf16[128,1024]{1,0:T(8,128)(2,1)S(1)}, u32[]{:S(2)}, u32[]{:S(2)}) collective-permute-start(bf16[128,1024]{1,0:T(8,128)(2,1)S(1)} %slice.15), channel_id=1, source_target_pairs={{0,64},{1,193},{64,0},{65,129},{128,192},{129,65},{192,128},{193,1... | collective-permute-start | bytes 786440 | tf_op jit(solution)/shard_map/ppermute | solution.py:29
  88.5 16.4 %all-to-all-start.1 = ((bf16[8,16,1024]{2,1,0:T(8,128)(2,1)}), bf16[8,16,1024]{2,1,0:T(8,128)(2,1)S(1)}, u32[]{:S(2)}, u32[]{:S(2)}) async-start(bf16[8,16,1024]{2,1,0:T(8,128)(2,1)} %bitcast.3), calls=%async_computation.1 | async-start | bytes 524288 | tf_op jit(solution)/shard_map/all_to_all | solution.py:37
  91.9 2.0 %collective-permute-start.10 = (bf16[512,256]{1,0:T(8,128)(2,1)S(1)}, bf16[512,256]{1,0:T(8,128)(2,1)S(1)}, u32[]{:S(2)}, u32[]{:S(2)}) collective-permute-start(bf16[512,256]{1,0:T(8,128)(2,1)S(1)} %get-tuple-element.60), channel_id=1, source_target_pairs={{0,1},{1,0},{2,3},{3,2},{4,5},{5,4},{6,7},{7,6},{8,9},{9,8},{10,11... | collective-permute-start | bytes 786440 | tf_op jit(solution)/shard_map/ppermute | solution.py:33

commit v4 on v3

--- a/solution.py
+++ b/solution.py
@@ -38,7 +38,8 @@
 
 
 def pack_kernel(
-    core_ref, q_hbm, g_hbm, o_hbm, lse_hbm, k_hbm, v_hbm, out_ref, own_ref, o_half, lse_ref, kv_ref, sems
+    core_ref, q_hbm, g_hbm, o_hbm, lse_hbm, k_hbm, v_hbm,
+    out_ref, top_ref, low_ref, own_ref, o_half, lse_ref, kv_ref, sems,
 ):
     half, channels = o_half.shape
     core = core_ref[0]
@@ -94,6 +95,9 @@
         out_ref[half:, at : at + half] = terms.astype(BF16)
     for trio in copies:
         trio[2].wait()
+    cut = top_ref.shape[0]
+    top_ref[...] = out_ref[:cut, :]
+    low_ref[...] = out_ref[cut:, :]
 
 
 def make_pack(core, queries, grad_out, attn_out, row_lse, keys, values):
@@ -108,10 +112,12 @@
         pack_kernel,
         out_shape=[
             jax.ShapeDtypeStruct((half + 16, 2 * channels), BF16),
+            jax.ShapeDtypeStruct((half // 2, 2 * channels), BF16),
+            jax.ShapeDtypeStruct((half // 2 + 16, 2 * channels), BF16),
             jax.ShapeDtypeStruct((8, rows, 2 * channels), BF16),
         ],
         in_specs=[pl.BlockSpec(memory_space=pltpu.SMEM)] + [hbm] * 6,
-        out_specs=[vmem, vmem],
+        out_specs=[vmem] * 4,
         scratch_shapes=[
             pltpu.VMEM((half, channels), BF16),
             pltpu.VMEM((tokens // 128, 128), F32),
@@ -123,6 +129,41 @@
     )(core.reshape(1), *arrays)
 
 
+def split_sum_kernel(mine_ref, got_ref, kept_ref, sent_ref):
+    n = kept_ref.shape[0]
+    kept_ref[...] = mine_ref[:n, :] + got_ref[:n, :].astype(F32)
+    sent_ref[...] = (mine_ref[n:, :] + got_ref[n:, :].astype(F32)).astype(BF16)
+
+
+def split_sum(mine, got):
+    vmem = pl.BlockSpec(memory_space=pltpu.VMEM)
+    half = (mine.shape[0] // 2, mine.shape[1])
+    return pl.pallas_call(
+        split_sum_kernel,
+        out_shape=[jax.ShapeDtypeStruct(half, F32), jax.ShapeDtypeStruct(half, BF16)],
+        in_specs=[vmem, vmem],
+        out_specs=[vmem, vmem],
+        compiler_params=pltpu.CompilerParams(vmem_limit_bytes=4 * 1024 * 1024),
+        name="split_sum",
+    )(mine, got)
+
+
+def rounded_sum_kernel(mine_ref, got_ref, out_ref):
+    total = mine_ref[...] + got_ref[...].astype(F32)
+    out_ref[...] = total.astype(BF16).reshape(out_ref.shape)
+
+
+def rounded_sum(mine, got, rows):
+    vmem = pl.BlockSpec(memory_space=pltpu.VMEM)
+    return pl.pallas_call(
+        rounded_sum_kernel,
+        out_shape=jax.ShapeDtypeStruct((got.shape[0] // rows, rows, got.shape[1]), BF16),
+        in_specs=[vmem, vmem],
+        compiler_params=pltpu.CompilerParams(vmem_limit_bytes=4 * 1024 * 1024),
+        name="rounded_sum",
+    )(mine, got)
+
+
 def finish_kernel(scale, parts_ref, k_ref, v_ref):
     channels = k_ref.shape[2]
     own = jnp.sum(parts_ref[...].astype(F32), axis=0)
@@ -151,8 +192,13 @@
     k, v = panel_ref[:, :channels], panel_ref[:, channels:]
     dk, dv = None, None
     for i in range(n_packs):
-        q, g = pack_refs[i][:half, :channels], pack_refs[i][:half, channels:]
-        both = jnp.sum(pack_refs[i][half:, :].astype(F32), axis=0, keepdims=True)
+        parts = pack_refs[i]
+        last = parts[-1].shape[0] - 16
+        q = [p[:, :channels] for p in parts[:-1]] + [parts[-1][:last, :channels]]
+        g = [p[:, channels:] for p in parts[:-1]] + [parts[-1][:last, channels:]]
+        q = q[0] if len(q) == 1 else jnp.concatenate(q)
+        g = g[0] if len(g) == 1 else jnp.concatenate(g)
+        both = jnp.sum(parts[-1][last:, :].astype(F32), axis=0, keepdims=True)
         lse, stats = both[:, :half] * log2e, both[:, half:]
         probs = jnp.exp2(dot(k, q, 1, 1) * scale - lse)
         dscores = (probs * (dot(v, g, 1, 1) - stats)).astype(BF16)
@@ -170,20 +216,21 @@
 
 def block_work(packs, panel, dqs, total, out_type):
     n_packs, first, add = len(packs), dqs is None, total is not None
-    half, channels = packs[0].shape[0] - 16, packs[0].shape[1] // 2
+    half, channels = sum(p.shape[0] for p in packs[0]) - 16, packs[0][0].shape[1] // 2
     keys = panel.shape[0]
+    arrays = [p for pack in packs for p in pack]
 
     def body(*refs):
         refs = list(refs)
-        pack_refs = [refs.pop(0) for _ in range(n_packs)]
+        pack_refs = [[refs.pop(0) for _ in pack] for pack in packs]
         panel_ref = refs.pop(0)
         dq_in = None if first else [refs.pop(0) for _ in range(n_packs)]
         sum_in = refs.pop(0) if add else None
         dq_out = [refs.pop(0) for _ in range(n_packs)]
         block_kernel(n_packs, first, add, pack_refs, panel_ref, dq_in, sum_in, dq_out, refs.pop(0))
 
-    args = [*packs, panel, *([] if first else dqs), *([total] if add else [])]
-    aliases = {} if first else {n_packs + 1 + i: i for i in range(n_packs)}
+    args = [*arrays, panel, *([] if first else dqs), *([total] if add else [])]
+    aliases = {} if first else {len(arrays) + 1 + i: i for i in range(n_packs)}
     if add and out_type == F32:
         aliases[len(args) - 1] = n_packs
     vmem = pl.BlockSpec(memory_space=pltpu.VMEM)
@@ -209,10 +256,11 @@
     scale = channels ** (-0.5)
     core = lax.axis_index("kv")
 
-    pack0, k0 = make_pack(core, queries, grad_out, attn_out, row_lse, keys, values)
+    pack0, top, low, k0 = make_pack(core, queries, grad_out, attn_out, row_lse, keys, values)
     pack1 = trade(pack0, "slab_1", 0)
-    pack2 = trade(pack0, "slab_1", 1)
+    pack2 = (trade(top, "slab_1", 1), trade(low, "slab_1", 1))
     pack3 = trade(pack1, "slab_1", 1)
+    pack0, pack1, pack3 = (pack0,), (pack1,), (pack3,)
 
     zall = across(k0).reshape(-1, k0.shape[2])
     y1 = trade(zall, "slab_0", 0)
@@ -221,12 +269,14 @@
     near_other = swap(near)
     far_other = swap(far)
 
-    a = [pack0, pack1, pack2]
+    two = [pack0, pack1]
     b = [pack3]
-    dqa, near_sum = block_work(a, near, None, None, F32)
-    dqa, near_osum = block_work(a, near_other, dqa, None, F32)
-    dqa, far_sum = block_work(a, far, dqa, None, F32)
-    dqa, far_osum = block_work(a, far_other, dqa, None, F32)
+    dqa, near_sum = block_work(two, near, None, None, F32)
+    dqa, near_osum = block_work(two, near_other, dqa, None, F32)
+    dqc, near_sum = block_work([pack2], near, None, near_sum, F32)
+    dqc, near_osum = block_work([pack2], near_other, dqc, near_osum, F32)
+    dqa, far_sum = block_work([*two, pack2], far, dqa + dqc, None, F32)
+    dqa, far_osum = block_work([*two, pack2], far_other, dqa, None, F32)
     dqb, far_osum = block_work(b, far_other, None, far_osum, BF16)
     dqb, far_sum = block_work(b, far, dqb, far_sum, F32)
     dqb, near_osum = block_work(b, near_other, dqb, near_osum, BF16)
@@ -234,10 +284,9 @@
 
     far_sum = far_sum + swap(far_osum).astype(F32)
     near_sum = near_sum + swap(near_osum).astype(F32)
-    n1, n = keys.shape[1], keys.shape[1] * 8
-    total = near_sum + trade(far_sum.astype(BF16), "slab_0", 1).astype(F32)
-    total = total[:n] + trade(total[n:].astype(BF16), "slab_0", 0).astype(F32)
-    parts = across(total.astype(BF16).reshape(8, n1, -1))
+    n1 = keys.shape[1]
+    kept, sent = split_sum(near_sum, trade(far_sum.astype(BF16), "slab_0", 1))
+    parts = across(rounded_sum(kept, trade(sent, "slab_0", 0), n1))
     grad_keys, grad_values = finish(parts, scale)
 
     got3 = trade(dqb[0].astype(BF16), "slab_1", 1).astype(F32)

time: 107 us -> 109 us (1.019)
  the two profiles are of different devices: /device:TPU:24 before, /device:TPU:1 now
where the time goes in v4:
time: 109 us
  waiting for transfers between devices  34.1 us (31%)
  starting transfers between devices  27.6 us (25%)
  blocking collectives  20.4 us (19%)
  Pallas kernels  19.1 us (18%)
  other arithmetic  6.56 us (6%)
    ppermute x11, waiting for transfers between devices, trade(): return lax.ppermute(x, (axis, 'kv'), pairs)  22.9 us
    all_to_all x1, blocking collectives, across(): return lax.all_to_all(x, 'slab_2', 0, 0, tiled=True)  20.4 us
    pallas_call x10, Pallas kernels, block_work(): pl.pallas_call(body, out_shape=[jax.ShapeDtypeStruct((half, channels), F3...  15.8 us
    ppermute x5, starting transfers between devices, swap(): return lax.ppermute(x, 'kv', [(0, 1), (1, 0)])  14.4 us
    ppermute x11, starting transfers between devices, trade(): return lax.ppermute(x, (axis, 'kv'), pairs)  9.82 us
    all_to_all x1, waiting for transfers between devices, across(): return lax.all_to_all(x, 'slab_2', 0, 0, tiled=True)  9.62 us
    all_to_all x1, starting transfers between devices, across(): return lax.all_to_all(x, 'slab_2', 0, 0, tiled=True)  3.41 us
  transfers between devices with their start and end apart: 17, of which 10 were waited for; matrix products, arithmetic and copies ran while one was open for 6% of the time, Pallas kernels for 14%

profile of v4, /device:TPU:1, one launch (start us, length us, event | category | flops | bytes accessed | tf_op | source)
XLA Modules:
  0.0 108.6 jit_solution(16480949683458276712)
XLA Ops:
  0.6 1.8 %pack.1 = (bf16[528,1024]{1,0:T(8,128)(2,1)S(1)}, bf16[256,1024]{1,0:T(8,128)(2,1)S(1)}, bf16[272,1024]{1,0:T(8,128)(2,1)S(1)}, bf16[8,16,1024]{2,1,0:T(8,128)(2,1)S(1)}) custom-call(s32[1]{0:T(128)} %bitcast.core_ref, bf16[1024,512]{1,0:T(8,128)(2,1)} %q_hbm.1, bf16[1024,512]{1,0:T(8,128)(2,1)} %g_hbm.1, bf16[1024,512]{1,0:T(8,128)(2,1)} %o_hbm.1, ...), custom_call_target="tpu_custom_call" | custom-call | tf_op jit(solution)/shard_map/pack/pallas_call | solution.py:111
  2.5 3.4 %collective-permute-start = (bf16[528,1024]{1,0:T(8,128)(2,1)S(1)}, bf16[528,1024]{1,0:T(8,128)(2,1)S(1)}, u32[]{:S(2)}, u32[]{:S(2)}) collective-permute-start(bf16[528,1024]{1,0:T(8,128)(2,1)S(1)} %get-tuple-element.37.refs_0_), channel_id=1, source_target_pairs={{0,16},{1,49},{16,0},{17,33},{32,48},{33,17},{48,32},{49,1},{2,18}... | collective-permute-start | bytes 3244040 | tf_op jit(solution)/shard_map/ppermute | solution.py:29
  5.9 20.4 %all_to_all.10 = bf16[8,16,1024]{2,1,0:T(8,128)(2,1)S(1)} all-to-all(bf16[8,16,1024]{2,1,0:T(8,128)(2,1)S(1)} %get-tuple-element.40), channel_id=1, replica_groups=mesh['slab_0'=4,'slab_1'=4,'slab_2'=8,'kv'=2] {'slab_2'}, dimensions={0} | all-to-all | bytes 524288 | tf_op jit(solution)/shard_map/all_to_all | solution.py:37
  26.2 2.7 %collective-permute-start.3 = (bf16[128,1024]{1,0:T(8,128)(2,1)S(1)}, bf16[128,1024]{1,0:T(8,128)(2,1)S(1)}, u32[]{:S(2)}, u32[]{:S(2)}) collective-permute-start(bf16[128,1024]{1,0:T(8,128)(2,1)S(1)} %bitcast.3), channel_id=1, source_target_pairs={{0,64},{1,193},{64,0},{65,129},{128,192},{129,65},{192,128},{193,1... | collective-permute-start | bytes 786440 | tf_op jit(solution)/shard_map/ppermute | solution.py:29
  29.0 3.8 %collective-permute-done.3 = bf16[128,1024]{1,0:T(8,128)(2,1)S(1)} collective-permute-done((bf16[128,1024]{1,0:T(8,128)(2,1)S(1)}, bf16[128,1024]{1,0:T(8,128)(2,1)S(1)}, u32[]{:S(2)}, u32[]{:S(2)}) %collective-permute-start.3) | collective-permute-done | bytes 262176 | tf_op jit(solution)/shard_map/ppermute | solution.py:29
  33.2 1.5 %collective-permute-start.1 = (bf16[256,1024]{1,0:T(8,128)(2,1)S(1)}, bf16[256,1024]{1,0:T(8,128)(2,1)S(1)}, u32[]{:S(2)}, u32[]{:S(2)}) collective-permute-start(bf16[256,1024]{1,0:T(8,128)(2,1)S(1)} %get-tuple-element.38), channel_id=1, source_target_pairs={{0,48},{1,17},{16,32},{17,1},{32,16},{33,49},{48,0},{49,33},{2,50}... | collective-permute-start | bytes 1572872 | tf_op jit(solution)/shard_map/ppermute | solution.py:29
  34.6 4.8 %collective-permute-start.6 = (bf16[256,1024]{1,0:T(8,128)(2,1)S(1)}, bf16[256,1024]{1,0:T(8,128)(2,1)S(1)}, u32[]{:S(2)}, u32[]{:S(2)}) collective-permute-start(bf16[256,1024]{1,0:T(8,128)(2,1)S(1)} %pad_maximum_fusion.refs_2_.refs_1_), channel_id=1, source_target_pairs={{0,1},{1,0},{2,3},{3,2},{4,5},{5,4},{6,7},{7,6},{8,9},{9,8},{10,11... | collective-permute-start | bytes 1572872 | tf_op jit(solution)/shard_map/ppermute | solution.py:33
  39.4 1.8 %collective-permute-done.4.refs_4_.refs_1_ = bf16[256,1024]{1,0:T(8,128)(2,1)S(1)} collective-permute-done((bf16[256,1024]{1,0:T(8,128)(2,1)S(1)}, bf16[256,1024]{1,0:T(8,128)(2,1)S(1)}, u32[]{:S(2)}, u32[]{:S(2)}) %collective-permute-start.4) | collective-permute-done | bytes 524320 | tf_op jit(solution)/shard_map/ppermute | solution.py:29
  41.2 2.4 %collective-permute-start.5 = (bf16[256,1024]{1,0:T(8,128)(2,1)S(1)}, bf16[256,1024]{1,0:T(8,128)(2,1)S(1)}, u32[]{:S(2)}, u32[]{:S(2)}) collective-permute-start(bf16[256,1024]{1,0:T(8,128)(2,1)S(1)} %collective-permute-done.4.refs_4_.refs_1_), channel_id=1, source_target_pairs={{0,1},{1,0},{2,3},{3,2},{4,5},{5,4},{6,7},{7,6},{8,9},{9,8},{10,11... | collective-permute-start | bytes 1572872 | tf_op jit(solution)/shard_map/ppermute | solution.py:33
  43.6 1.8 %shard_map.85 = (f32[512,512]{1,0:T(8,128)S(1)}, f32[512,512]{1,0:T(8,128)S(1)}, f32[256,1024]{1,0:T(8,128)S(1)}) custom-call(bf16[528,1024]{1,0:T(8,128)(2,1)S(1)} %get-tuple-element.37.refs_0_, bf16[528,1024]{1,0:T(8,128)(2,1)S(1)} %collective-permute-done.refs_1_, bf16[256,1024]{1,0:T(8,128)(2,1)S(1)} %pad_maximum_fusion.refs_2_.refs_1_), custom_call_target="tpu_custom_call" | custom-call | flops 1342177280 | bytes 2097152 | tf_op jit(solution)/shard_map/pallas_call | solution.py:237
  45.4 2.1 %collective-permute-done.1.refs_0_.refs_2_ = bf16[256,1024]{1,0:T(8,128)(2,1)S(1)} collective-permute-done((bf16[256,1024]{1,0:T(8,128)(2,1)S(1)}, bf16[256,1024]{1,0:T(8,128)(2,1)S(1)}, u32[]{:S(2)}, u32[]{:S(2)}) %collective-permute-start.1) | collective-permute-done | bytes 524320 | tf_op jit(solution)/shard_map/ppermute | solution.py:29
  48.6 1.9 %shard_map.86 = (f32[512,512]{1,0:T(8,128)S(1)}, f32[512,512]{1,0:T(8,128)S(1)}, f32[256,1024]{1,0:T(8,128)S(1)}) custom-call(bf16[528,1024]{1,0:T(8,128)(2,1)S(1)} %get-tuple-element.37.refs_0_, bf16[528,1024]{1,0:T(8,128)(2,1)S(1)} %collective-permute-done.refs_1_, ...), custom_call_target="tpu_custom_call", output_to_operand_aliasing={{0}: (3, {}), {1}: (4, {})} | custom-call | flops 1342177280 | bytes 2097152 | tf_op jit(solution)/shard_map/pallas_call | solution.py:237
  51.6 2.7 %shard_map.89 = (f32[512,512]{1,0:T(8,128)S(1)}, f32[512,512]{1,0:T(8,128)S(1)}, f32[512,512]{1,0:T(8,128)S(1)}, f32[256,1024]{1,0:T(8,128)S(1)}) custom-call(bf16[528,1024]{1,0:T(8,128)(2,1)S(1)} %get-tuple-element.37.refs_0_, bf16[528,1024]{1,0:T(8,128)(2,1)S(1)} %collective-permute-done.refs_1_, ...), custom_call_target="tpu_custom_call", output_to_operand_aliasing={{0}: (5, {}), {1}: (6, {}), {2}: (7, {})} | custom-call | flops 2013265920 | bytes 3145728 | tf_op jit(solution)/shard_map/pallas_call | solution.py:237
  54.3 2.7 %shard_map.90 = (f32[512,512]{1,0:T(8,128)S(1)}, f32[512,512]{1,0:T(8,128)S(1)}, f32[512,512]{1,0:T(8,128)S(1)}, f32[256,1024]{1,0:T(8,128)S(1)}) custom-call(bf16[528,1024]{1,0:T(8,128)(2,1)S(1)} %get-tuple-element.37.refs_0_, bf16[528,1024]{1,0:T(8,128)(2,1)S(1)} %collective-permute-done.refs_1_, ...), custom_call_target="tpu_custom_call", output_to_operand_aliasing={{0}: (5, {}), {1}: (6, {}), {2}: (7, {})} | custom-call | flops 2013265920 | bytes 3145728 | tf_op jit(solution)/shard_map/pallas_call | solution.py:237
  57.1 2.0 %collective-permute-done.8.refs_0_ = bf16[528,1024]{1,0:T(8,128)(2,1)S(1)} collective-permute-done((bf16[528,1024]{1,0:T(8,128)(2,1)S(1)}, bf16[528,1024]{1,0:T(8,128)(2,1)S(1)}, u32[]{:S(2)}, u32[]{:S(2)}) %collective-permute-start.8) | collective-permute-done | bytes 1081376 | tf_op jit(solution)/shard_map/ppermute | solution.py:29
  60.1 5.4 %collective-permute-start.13 = (bf16[256,1024]{1,0:T(8,128)(2,1)S(1)}, bf16[256,1024]{1,0:T(8,128)(2,1)S(1)}, u32[]{:S(2)}, u32[]{:S(2)}) collective-permute-start(bf16[256,1024]{1,0:T(8,128)(2,1)S(1)} %get-tuple-element.66), channel_id=1, source_target_pairs={{0,1},{1,0},{2,3},{3,2},{4,5},{5,4},{6,7},{7,6},{8,9},{9,8},{10,11... | collective-permute-start | bytes 1572872 | tf_op jit(solution)/shard_map/ppermute | solution.py:33
  69.9 1.5 %collective-permute-start.7 = (bf16[512,512]{1,0:T(8,128)(2,1)}, bf16[512,512]{1,0:T(8,128)(2,1)}, u32[]{:S(2)}, u32[]{:S(2)}) collective-permute-start(bf16[512,512]{1,0:T(8,128)(2,1)} %convert_element_type.30), channel_id=1, source_target_pairs={{0,48},{1,17},{16,32},{17,1},{32,16},{33,49},{48,0},{49,33},{2,50}... | collective-permute-start | bytes 1572872 | tf_op jit(solution)/shard_map/ppermute | solution.py:29
  71.3 1.8 %collective-permute-start.12 = (bf16[256,1024]{1,0:T(8,128)(2,1)S(1)}, bf16[256,1024]{1,0:T(8,128)(2,1)}, u32[]{:S(2)}, u32[]{:S(2)}) collective-permute-start(bf16[256,1024]{1,0:T(8,128)(2,1)S(1)} %get-tuple-element.64), channel_id=1, source_target_pairs={{0,1},{1,0},{2,3},{3,2},{4,5},{5,4},{6,7},{7,6},{8,9},{9,8},{10,11... | collective-permute-start | bytes 1572872 | tf_op jit(solution)/shard_map/ppermute | solution.py:33
  74.1 3.2 %collective-permute-done.9 = bf16[512,512]{1,0:T(8,128)(2,1)S(1)} collective-permute-done((bf16[512,512]{1,0:T(8,128)(2,1)S(1)}, bf16[512,512]{1,0:T(8,128)(2,1)S(1)}, u32[]{:S(2)}, u32[]{:S(2)}) %collective-permute-start.9) | collective-permute-done | bytes 524320 | tf_op jit(solution)/shard_map/ppermute | solution.py:29
  79.7 3.0 %collective-permute-done.14.got_ref = bf16[256,1024]{1,0:T(8,128)(2,1)S(1)} collective-permute-done((bf16[256,1024]{1,0:T(8,128)(2,1)}, bf16[256,1024]{1,0:T(8,128)(2,1)S(1)}, u32[]{:S(2)}, u32[]{:S(2)}) %collective-permute-start.14) | collective-permute-done | bytes 524320 | tf_op jit(solution)/shard_map/ppermute | solution.py:29
  83.0 7.0 %collective-permute-done.10 = bf16[512,512]{1,0:T(8,128)(2,1)} collective-permute-done((bf16[512,512]{1,0:T(8,128)(2,1)}, bf16[512,512]{1,0:T(8,128)(2,1)}, u32[]{:S(2)}, u32[]{:S(2)}) %collective-permute-start.10) | collective-permute-done | bytes 524320 | tf_op jit(solution)/shard_map/ppermute | solution.py:29
  92.2 3.4 %all-to-all-start.1 = ((bf16[8,16,1024]{2,1,0:T(8,128)(2,1)}), bf16[8,16,1024]{2,1,0:T(8,128)(2,1)S(1)}, u32[]{:S(2)}, u32[]{:S(2)}) async-start(bf16[8,16,1024]{2,1,0:T(8,128)(2,1)} %rounded_sum.1), calls=%async_computation.1 | async-start | bytes 524288 | tf_op jit(solution)/shard_map/all_to_all | solution.py:37
  95.8 1.5 %collective-permute-done.11 = bf16[512,256]{1,0:T(8,128)(2,1)S(1)} collective-permute-done((bf16[512,256]{1,0:T(8,128)(2,1)S(1)}, bf16[512,256]{1,0:T(8,128)(2,1)S(1)}, u32[]{:S(2)}, u32[]{:S(2)}) %collective-permute-start.11) | collective-permute-done | bytes 262176 | tf_op jit(solution)/shard_map/ppermute | solution.py:33
  98.4 9.6 %all-to-all-done.1.parts_ref = bf16[8,16,1024]{2,1,0:T(8,128)(2,1)S(1)} async-done(((bf16[8,16,1024]{2,1,0:T(8,128)(2,1)}), bf16[8,16,1024]{2,1,0:T(8,128)(2,1)S(1)}, u32[]{:S(2)}, u32[]{:S(2)}) %all-to-all-start.1) | async-done | bytes 262176 | tf_op jit(solution)/shard_map/all_to_all | solution.py:37
  (34 shorter events, 15.7 us)
Async XLA Ops:
  2.5 36.9 %collective-permute-start = (bf16[528,1024]{1,0:T(8,128)(2,1)S(1)}, bf16[528,1024]{1,0:T(8,128)(2,1)S(1)}, u32[]{:S(2)}, u32[]{:S(2)}) collective-permute-start(bf16[528,1024]{1,0:T(8,128)(2,1)S(1)} %get-tuple-element.37.refs_0_), channel_id=1, source_target_pairs={{0,16},{1,49},{16,0},{17,33},{32,48},{33,17},{48,32},{49,1},{2,18}... | collective-permute-start | bytes 3244040 | tf_op jit(solution)/shard_map/ppermute | solution.py:29
  26.2 6.5 %collective-permute-start.3 = (bf16[128,1024]{1,0:T(8,128)(2,1)S(1)}, bf16[128,1024]{1,0:T(8,128)(2,1)S(1)}, u32[]{:S(2)}, u32[]{:S(2)}) collective-permute-start(bf16[128,1024]{1,0:T(8,128)(2,1)S(1)} %bitcast.3), channel_id=1, source_target_pairs={{0,64},{1,193},{64,0},{65,129},{128,192},{129,65},{192,128},{193,1... | collective-permute-start | bytes 786440 | tf_op jit(solution)/shard_map/ppermute | solution.py:29
  32.8 8.4 %collective-permute-start.4 = (bf16[256,1024]{1,0:T(8,128)(2,1)S(1)}, bf16[256,1024]{1,0:T(8,128)(2,1)S(1)}, u32[]{:S(2)}, u32[]{:S(2)}) collective-permute-start(bf16[256,1024]{1,0:T(8,128)(2,1)S(1)} %pad_maximum_fusion.refs_2_.refs_1_), channel_id=1, source_target_pairs={{0,192},{1,65},{64,128},{65,1},{128,64},{129,193},{192,0},{193,129... | collective-permute-start | bytes 1572872 | tf_op jit(solution)/shard_map/ppermute | solution.py:29
  33.2 14.3 %collective-permute-start.2 = (bf16[272,1024]{1,0:T(8,128)(2,1)S(1)}, bf16[272,1024]{1,0:T(8,128)(2,1)S(1)}, u32[]{:S(2)}, u32[]{:S(2)}) collective-permute-start(bf16[272,1024]{1,0:T(8,128)(2,1)S(1)} %get-tuple-element.39), channel_id=1, source_target_pairs={{0,48},{1,17},{16,32},{17,1},{32,16},{33,49},{48,0},{49,33},{2,50}... | collective-permute-start | bytes 1671176 | tf_op jit(solution)/shard_map/ppermute | solution.py:29
  33.2 14.3 %collective-permute-start.1 = (bf16[256,1024]{1,0:T(8,128)(2,1)S(1)}, bf16[256,1024]{1,0:T(8,128)(2,1)S(1)}, u32[]{:S(2)}, u32[]{:S(2)}) collective-permute-start(bf16[256,1024]{1,0:T(8,128)(2,1)S(1)} %get-tuple-element.38), channel_id=1, source_target_pairs={{0,48},{1,17},{16,32},{17,1},{32,16},{33,49},{48,0},{49,33},{2,50}... | collective-permute-start | bytes 1572872 | tf_op jit(solution)/shard_map/ppermute | solution.py:29
  34.6 13.9 %collective-permute-start.6 = (bf16[256,1024]{1,0:T(8,128)(2,1)S(1)}, bf16[256,1024]{1,0:T(8,128)(2,1)S(1)}, u32[]{:S(2)}, u32[]{:S(2)}) collective-permute-start(bf16[256,1024]{1,0:T(8,128)(2,1)S(1)} %pad_maximum_fusion.refs_2_.refs_1_), channel_id=1, source_target_pairs={{0,1},{1,0},{2,3},{3,2},{4,5},{5,4},{6,7},{7,6},{8,9},{9,8},{10,11... | collective-permute-start | bytes 1572872 | tf_op jit(solution)/shard_map/ppermute | solution.py:33
  39.4 19.6 %collective-permute-start.8 = (bf16[528,1024]{1,0:T(8,128)(2,1)S(1)}, bf16[528,1024]{1,0:T(8,128)(2,1)S(1)}, u32[]{:S(2)}, u32[]{:S(2)}) collective-permute-start(bf16[528,1024]{1,0:T(8,128)(2,1)S(1)} %collective-permute-done.refs_1_), channel_id=1, source_target_pairs={{0,48},{1,17},{16,32},{17,1},{32,16},{33,49},{48,0},{49,33},{2,50}... | collective-permute-start | bytes 3244040 | tf_op jit(solution)/shard_map/ppermute | solution.py:29
  41.2 13.1 %collective-permute-start.5 = (bf16[256,1024]{1,0:T(8,128)(2,1)S(1)}, bf16[256,1024]{1,0:T(8,128)(2,1)S(1)}, u32[]{:S(2)}, u32[]{:S(2)}) collective-permute-start(bf16[256,1024]{1,0:T(8,128)(2,1)S(1)} %collective-permute-done.4.refs_4_.refs_1_), channel_id=1, source_target_pairs={{0,1},{1,0},{2,3},{3,2},{4,5},{5,4},{6,7},{7,6},{8,9},{9,8},{10,11... | collective-permute-start | bytes 1572872 | tf_op jit(solution)/shard_map/ppermute | solution.py:33
  60.1 13.0 %collective-permute-start.13 = (bf16[256,1024]{1,0:T(8,128)(2,1)S(1)}, bf16[256,1024]{1,0:T(8,128)(2,1)S(1)}, u32[]{:S(2)}, u32[]{:S(2)}) collective-permute-start(bf16[256,1024]{1,0:T(8,128)(2,1)S(1)} %get-tuple-element.66), channel_id=1, source_target_pairs={{0,1},{1,0},{2,3},{3,2},{4,5},{5,4},{6,7},{7,6},{8,9},{9,8},{10,11... | collective-permute-start | bytes 1572872 | tf_op jit(solution)/shard_map/ppermute | solution.py:33
  68.9 8.4 %collective-permute-start.9 = (bf16[512,512]{1,0:T(8,128)(2,1)S(1)}, bf16[512,512]{1,0:T(8,128)(2,1)S(1)}, u32[]{:S(2)}, u32[]{:S(2)}) collective-permute-start(bf16[512,512]{1,0:T(8,128)(2,1)S(1)} %convert_element_type.32), channel_id=1, source_target_pairs={{0,48},{1,17},{16,32},{17,1},{32,16},{33,49},{48,0},{49,33},{2,50}... | collective-permute-start | bytes 1572872 | tf_op jit(solution)/shard_map/ppermute | solution.py:29
  69.9 13.2 %collective-permute-start.7 = (bf16[512,512]{1,0:T(8,128)(2,1)}, bf16[512,512]{1,0:T(8,128)(2,1)}, u32[]{:S(2)}, u32[]{:S(2)}) collective-permute-start(bf16[512,512]{1,0:T(8,128)(2,1)} %convert_element_type.30), channel_id=1, source_target_pairs={{0,48},{1,17},{16,32},{17,1},{32,16},{33,49},{48,0},{49,33},{2,50}... | collective-permute-start | bytes 1572872 | tf_op jit(solution)/shard_map/ppermute | solution.py:29
  71.3 7.1 %collective-permute-start.12 = (bf16[256,1024]{1,0:T(8,128)(2,1)S(1)}, bf16[256,1024]{1,0:T(8,128)(2,1)}, u32[]{:S(2)}, u32[]{:S(2)}) collective-permute-start(bf16[256,1024]{1,0:T(8,128)(2,1)S(1)} %get-tuple-element.64), channel_id=1, source_target_pairs={{0,1},{1,0},{2,3},{3,2},{4,5},{5,4},{6,7},{7,6},{8,9},{9,8},{10,11... | collective-permute-start | bytes 1572872 | tf_op jit(solution)/shard_map/ppermute | solution.py:33
  74.1 8.6 %collective-permute-start.14 = (bf16[256,1024]{1,0:T(8,128)(2,1)}, bf16[256,1024]{1,0:T(8,128)(2,1)S(1)}, u32[]{:S(2)}, u32[]{:S(2)}) collective-permute-start(bf16[256,1024]{1,0:T(8,128)(2,1)} %add_convert_fusion), channel_id=1, source_target_pairs={{0,192},{1,65},{64,128},{65,1},{128,64},{129,193},{192,0},{193,129... | collective-permute-start | bytes 1572872 | tf_op jit(solution)/shard_map/ppermute | solution.py:29
  78.3 11.8 %collective-permute-start.10 = (bf16[512,512]{1,0:T(8,128)(2,1)}, bf16[512,512]{1,0:T(8,128)(2,1)}, u32[]{:S(2)}, u32[]{:S(2)}) collective-permute-start(bf16[512,512]{1,0:T(8,128)(2,1)} %add_convert_fusion.1), channel_id=1, source_target_pairs={{0,16},{1,49},{16,0},{17,33},{32,48},{33,17},{48,32},{49,1},{2,18}... | collective-permute-start | bytes 1572872 | tf_op jit(solution)/shard_map/ppermute | solution.py:29
  82.8 8.7 %collective-permute-start.15 = (bf16[128,1024]{1,0:T(8,128)(2,1)S(1)}, bf16[128,1024]{1,0:T(8,128)(2,1)S(1)}, u32[]{:S(2)}, u32[]{:S(2)}) collective-permute-start(bf16[128,1024]{1,0:T(8,128)(2,1)S(1)} %get-tuple-element.68), channel_id=1, source_target_pairs={{0,64},{1,193},{64,0},{65,129},{128,192},{129,65},{192,128},{193,1... | collective-permute-start | bytes 786440 | tf_op jit(solution)/shard_map/ppermute | solution.py:29
  92.2 15.7 %all-to-all-start.1 = ((bf16[8,16,1024]{2,1,0:T(8,128)(2,1)}), bf16[8,16,1024]{2,1,0:T(8,128)(2,1)S(1)}, u32[]{:S(2)}, u32[]{:S(2)}) async-start(bf16[8,16,1024]{2,1,0:T(8,128)(2,1)} %rounded_sum.1), calls=%async_computation.1 | async-start | bytes 524288 | tf_op jit(solution)/shard_map/all_to_all | solution.py:37
  95.7 1.6 %collective-permute-start.11 = (bf16[512,256]{1,0:T(8,128)(2,1)S(1)}, bf16[512,256]{1,0:T(8,128)(2,1)S(1)}, u32[]{:S(2)}, u32[]{:S(2)}) collective-permute-start(bf16[512,256]{1,0:T(8,128)(2,1)S(1)} %get-tuple-element.72), channel_id=1, source_target_pairs={{0,1},{1,0},{2,3},{3,2},{4,5},{5,4},{6,7},{7,6},{8,9},{9,8},{10,11... | collective-permute-start | bytes 786440 | tf_op jit(solution)/shard_map/ppermute | solution.py:33

commit v5 on v4

--- a/solution.py
+++ b/solution.py
@@ -86,7 +86,7 @@
         column = jnp.sum(product, axis=1, keepdims=True)
         pieces.append(jnp.transpose(jnp.broadcast_to(column, (piece, 128)))[:1, :])
     stats = jnp.concatenate(pieces, axis=1)
-    row = lax.broadcasted_iota(jnp.int32, (16, half), 0)
+    row = lax.broadcasted_iota(jnp.int32, (8, half), 0)
     for at, v in ((0, lse), (half, stats)):
         hi = v.astype(BF16).astype(F32)
         mid = (v - hi).astype(BF16).astype(F32)
@@ -111,9 +111,9 @@
     return pl.pallas_call(
         pack_kernel,
         out_shape=[
-            jax.ShapeDtypeStruct((half + 16, 2 * channels), BF16),
-            jax.ShapeDtypeStruct((half // 2, 2 * channels), BF16),
-            jax.ShapeDtypeStruct((half // 2 + 16, 2 * channels), BF16),
+            jax.ShapeDtypeStruct((half + 8, 2 * channels), BF16),
+            jax.ShapeDtypeStruct((half * 192 // 512, 2 * channels), BF16),
+            jax.ShapeDtypeStruct((half * 320 // 512 + 8, 2 * channels), BF16),
             jax.ShapeDtypeStruct((8, rows, 2 * channels), BF16),
         ],
         in_specs=[pl.BlockSpec(memory_space=pltpu.SMEM)] + [hbm] * 6,
@@ -129,23 +129,24 @@
     )(core.reshape(1), *arrays)
 
 
-def split_sum_kernel(mine_ref, got_ref, kept_ref, sent_ref):
+def split_sum_kernel(mine_ref, core_ref, got_ref, kept_ref, sent_ref):
     n = kept_ref.shape[0]
-    kept_ref[...] = mine_ref[:n, :] + got_ref[:n, :].astype(F32)
-    sent_ref[...] = (mine_ref[n:, :] + got_ref[n:, :].astype(F32)).astype(BF16)
-
-
-def split_sum(mine, got):
+    kept_ref[...] = mine_ref[:n, :] + core_ref[:n, :].astype(F32) + got_ref[:n, :].astype(F32)
+    low = mine_ref[n:, :] + core_ref[n:, :].astype(F32) + got_ref[n:, :].astype(F32)
+    sent_ref[...] = low.astype(BF16)
+
+
+def split_sum(mine, other_core, got):
     vmem = pl.BlockSpec(memory_space=pltpu.VMEM)
     half = (mine.shape[0] // 2, mine.shape[1])
     return pl.pallas_call(
         split_sum_kernel,
         out_shape=[jax.ShapeDtypeStruct(half, F32), jax.ShapeDtypeStruct(half, BF16)],
-        in_specs=[vmem, vmem],
+        in_specs=[vmem, vmem, vmem],
         out_specs=[vmem, vmem],
-        compiler_params=pltpu.CompilerParams(vmem_limit_bytes=4 * 1024 * 1024),
+        compiler_params=pltpu.CompilerParams(vmem_limit_bytes=6 * 1024 * 1024),
         name="split_sum",
-    )(mine, got)
+    )(mine, other_core, got)
 
 
 def rounded_sum_kernel(mine_ref, got_ref, out_ref):
@@ -193,7 +194,7 @@
     dk, dv = None, None
     for i in range(n_packs):
         parts = pack_refs[i]
-        last = parts[-1].shape[0] - 16
+        last = parts[-1].shape[0] - 8
         q = [p[:, :channels] for p in parts[:-1]] + [parts[-1][:last, :channels]]
         g = [p[:, channels:] for p in parts[:-1]] + [parts[-1][:last, channels:]]
         q = q[0] if len(q) == 1 else jnp.concatenate(q)
@@ -214,9 +215,9 @@
     sum_out[:, channels:] = dv.astype(sum_out.dtype)
 
 
-def block_work(packs, panel, dqs, total, out_type):
+def block_work(packs, panel, dqs, total, out_type, after=()):
     n_packs, first, add = len(packs), dqs is None, total is not None
-    half, channels = sum(p.shape[0] for p in packs[0]) - 16, packs[0][0].shape[1] // 2
+    half, channels = sum(p.shape[0] for p in packs[0]) - 8, packs[0][0].shape[1] // 2
     keys = panel.shape[0]
     arrays = [p for pack in packs for p in pack]
 
@@ -226,13 +227,14 @@
         panel_ref = refs.pop(0)
         dq_in = None if first else [refs.pop(0) for _ in range(n_packs)]
         sum_in = refs.pop(0) if add else None
+        refs = refs[len(after) :]
         dq_out = [refs.pop(0) for _ in range(n_packs)]
         block_kernel(n_packs, first, add, pack_refs, panel_ref, dq_in, sum_in, dq_out, refs.pop(0))
 
-    args = [*arrays, panel, *([] if first else dqs), *([total] if add else [])]
+    args = [*arrays, panel, *([] if first else dqs), *([total] if add else []), *after]
     aliases = {} if first else {len(arrays) + 1 + i: i for i in range(n_packs)}
     if add and out_type == F32:
-        aliases[len(args) - 1] = n_packs
+        aliases[len(args) - 1 - len(after)] = n_packs
     vmem = pl.BlockSpec(memory_space=pltpu.VMEM)
     out = pl.pallas_call(
         body,
@@ -252,7 +254,7 @@
 
 
 def steps(queries, grad_out, attn_out, row_lse, keys, values):
-    _, channels = queries.shape
+    tokens, channels = queries.shape
     scale = channels ** (-0.5)
     core = lax.axis_index("kv")
 
@@ -269,11 +271,13 @@
     near_other = swap(near)
     far_other = swap(far)
 
+    half = tokens // 2
     two = [pack0, pack1]
     b = [pack3]
-    dqa, near_sum = block_work(two, near, None, None, F32)
+    seen = pack1[0][half:, :128] * 2
+    dqa, near_sum = block_work(two, near, None, None, F32, (seen,))
     dqa, near_osum = block_work(two, near_other, dqa, None, F32)
-    dqc, near_sum = block_work([pack2], near, None, near_sum, F32)
+    dqc, near_sum = block_work([pack2], near, None, near_sum, F32, (near_osum,))
     dqc, near_osum = block_work([pack2], near_other, dqc, near_osum, F32)
     dqa, far_sum = block_work([*two, pack2], far, dqa + dqc, None, F32)
     dqa, far_osum = block_work([*two, pack2], far_other, dqa, None, F32)
@@ -283,9 +287,9 @@
     dqb, near_sum = block_work(b, near, dqb, near_sum, F32)
 
     far_sum = far_sum + swap(far_osum).astype(F32)
-    near_sum = near_sum + swap(near_osum).astype(F32)
+    near_got = swap(near_osum)
     n1 = keys.shape[1]
-    kept, sent = split_sum(near_sum, trade(far_sum.astype(BF16), "slab_0", 1))
+    kept, sent = split_sum(near_sum, near_got, trade(far_sum.astype(BF16), "slab_0", 1))
     parts = across(rounded_sum(kept, trade(sent, "slab_0", 0), n1))
     grad_keys, grad_values = finish(parts, scale)
 

time: 109 us -> 117 us (1.073)
  waiting for transfers between devices: 34.1 us -> 43.9 us
  starting transfers between devices: 27.6 us -> 26.4 us
  other arithmetic: 6.56 us -> 5.36 us
    ppermute x11, waiting for transfers between devices: 22.9 us -> 32.7 us  [trade(): return lax.ppermute(x, (axis, 'kv'), pairs)]
    ppermute x5, starting transfers between devices: 14.4 us -> 13.1 us  [swap(): return lax.ppermute(x, 'kv', [(0, 1), (1, 0)])]
    add x1 -> x0, other arithmetic: 1.22 us -> none  [steps(): near_sum = near_sum + swap(near_osum).astype(F32)]
  transfers between devices with their start and end apart: 17 -> 17, of which waited for: 10 -> 9; matrix products, arithmetic and copies ran while one was open for 6% -> 5% of each run, Pallas kernels for 14% -> 13%
where the time goes in v5:
time: 117 us
  waiting for transfers between devices  43.9 us (38%)
  starting transfers between devices  26.4 us (23%)
  blocking collectives  20.4 us (17%)
  Pallas kernels  20 us (17%)
  other arithmetic  5.36 us (5%)
    ppermute x11, waiting for transfers between devices, trade(): return lax.ppermute(x, (axis, 'kv'), pairs)  32.7 us
    all_to_all x1, blocking collectives, across(): return lax.all_to_all(x, 'slab_2', 0, 0, tiled=True)  20.4 us
    pallas_call x10, Pallas kernels, block_work(): pl.pallas_call(body, out_shape=[jax.ShapeDtypeStruct((half, channels), F3...  16.6 us
    ppermute x5, starting transfers between devices, swap(): return lax.ppermute(x, 'kv', [(0, 1), (1, 0)])  13.1 us
    ppermute x11, starting transfers between devices, trade(): return lax.ppermute(x, (axis, 'kv'), pairs)  9.83 us
    all_to_all x1, waiting for transfers between devices, across(): return lax.all_to_all(x, 'slab_2', 0, 0, tiled=True)  9.62 us
    all_to_all x1, starting transfers between devices, across(): return lax.all_to_all(x, 'slab_2', 0, 0, tiled=True)  3.41 us
  transfers between devices with their start and end apart: 17, of which 9 were waited for; matrix products, arithmetic and copies ran while one was open for 5% of the time, Pallas kernels for 13%

profile of v5, /device:TPU:1, one launch (start us, length us, event | category | flops | bytes accessed | tf_op | source)
XLA Modules:
  0.0 116.8 jit_solution(13739648889596047236)
XLA Ops:
  0.6 1.8 %pack.1 = (bf16[520,1024]{1,0:T(8,128)(2,1)S(1)}, bf16[192,1024]{1,0:T(8,128)(2,1)S(1)}, bf16[328,1024]{1,0:T(8,128)(2,1)S(1)}, bf16[8,16,1024]{2,1,0:T(8,128)(2,1)S(1)}) custom-call(s32[1]{0:T(128)} %bitcast.core_ref, bf16[1024,512]{1,0:T(8,128)(2,1)} %q_hbm.1, bf16[1024,512]{1,0:T(8,128)(2,1)} %g_hbm.1, bf16[1024,512]{1,0:T(8,128)(2,1)} %o_hbm.1, ...), custom_call_target="tpu_custom_call" | custom-call | tf_op jit(solution)/shard_map/pack/pallas_call | solution.py:111
  2.5 3.4 %collective-permute-start = (bf16[520,1024]{1,0:T(8,128)(2,1)S(1)}, bf16[520,1024]{1,0:T(8,128)(2,1)S(1)}, u32[]{:S(2)}, u32[]{:S(2)}) collective-permute-start(bf16[520,1024]{1,0:T(8,128)(2,1)S(1)} %get-tuple-element.37.refs_0_), channel_id=1, source_target_pairs={{0,16},{1,49},{16,0},{17,33},{32,48},{33,17},{48,32},{49,1},{2,18}... | collective-permute-start | bytes 3194888 | tf_op jit(solution)/shard_map/ppermute | solution.py:29
  5.9 20.4 %all_to_all.10 = bf16[8,16,1024]{2,1,0:T(8,128)(2,1)S(1)} all-to-all(bf16[8,16,1024]{2,1,0:T(8,128)(2,1)S(1)} %get-tuple-element.40), channel_id=1, replica_groups=mesh['slab_0'=4,'slab_1'=4,'slab_2'=8,'kv'=2] {'slab_2'}, dimensions={0} | all-to-all | bytes 524288 | tf_op jit(solution)/shard_map/all_to_all | solution.py:37
  26.2 2.7 %collective-permute-start.3 = (bf16[128,1024]{1,0:T(8,128)(2,1)S(1)}, bf16[128,1024]{1,0:T(8,128)(2,1)S(1)}, u32[]{:S(2)}, u32[]{:S(2)}) collective-permute-start(bf16[128,1024]{1,0:T(8,128)(2,1)S(1)} %bitcast.3), channel_id=1, source_target_pairs={{0,64},{1,193},{64,0},{65,129},{128,192},{129,65},{192,128},{193,1... | collective-permute-start | bytes 786440 | tf_op jit(solution)/shard_map/ppermute | solution.py:29
  29.0 3.8 %collective-permute-done.3 = bf16[128,1024]{1,0:T(8,128)(2,1)S(1)} collective-permute-done((bf16[128,1024]{1,0:T(8,128)(2,1)S(1)}, bf16[128,1024]{1,0:T(8,128)(2,1)S(1)}, u32[]{:S(2)}, u32[]{:S(2)}) %collective-permute-start.3) | collective-permute-done | bytes 262176 | tf_op jit(solution)/shard_map/ppermute | solution.py:29
  33.2 3.5 %collective-permute-start.6 = (bf16[256,1024]{1,0:T(8,128)(2,1)S(1)}, bf16[256,1024]{1,0:T(8,128)(2,1)S(1)}, u32[]{:S(2)}, u32[]{:S(2)}) collective-permute-start(bf16[256,1024]{1,0:T(8,128)(2,1)S(1)} %pad_maximum_fusion.refs_2_.refs_1_), channel_id=1, source_target_pairs={{0,1},{1,0},{2,3},{3,2},{4,5},{5,4},{6,7},{7,6},{8,9},{9,8},{10,11... | collective-permute-start | bytes 1572872 | tf_op jit(solution)/shard_map/ppermute | solution.py:33
  38.1 3.0 %collective-permute-done.4.refs_4_.refs_1_ = bf16[256,1024]{1,0:T(8,128)(2,1)S(1)} collective-permute-done((bf16[256,1024]{1,0:T(8,128)(2,1)S(1)}, bf16[256,1024]{1,0:T(8,128)(2,1)S(1)}, u32[]{:S(2)}, u32[]{:S(2)}) %collective-permute-start.4) | collective-permute-done | bytes 524320 | tf_op jit(solution)/shard_map/ppermute | solution.py:29
  41.2 2.4 %collective-permute-start.5 = (bf16[256,1024]{1,0:T(8,128)(2,1)S(1)}, bf16[256,1024]{1,0:T(8,128)(2,1)S(1)}, u32[]{:S(2)}, u32[]{:S(2)}) collective-permute-start(bf16[256,1024]{1,0:T(8,128)(2,1)S(1)} %collective-permute-done.4.refs_4_.refs_1_), channel_id=1, source_target_pairs={{0,1},{1,0},{2,3},{3,2},{4,5},{5,4},{6,7},{7,6},{8,9},{9,8},{10,11... | collective-permute-start | bytes 1572872 | tf_op jit(solution)/shard_map/ppermute | solution.py:33
  43.6 1.8 %shard_map.85 = (f32[512,512]{1,0:T(8,128)S(1)}, f32[512,512]{1,0:T(8,128)S(1)}, f32[256,1024]{1,0:T(8,128)S(1)}) custom-call(bf16[520,1024]{1,0:T(8,128)(2,1)S(1)} %get-tuple-element.37.refs_0_, bf16[520,1024]{1,0:T(8,128)(2,1)S(1)} %collective-permute-done.refs_1_, bf16[256,1024]{1,0:T(8,128)(2,1)S(1)} %pad_maximum_fusion.refs_2_.refs_1_, ...), custom_call_target="tpu_custom_call" | custom-call | flops 1342177280 | bytes 2097152 | tf_op jit(solution)/shard_map/pallas_call | solution.py:239
  45.4 1.9 %shard_map.86 = (f32[512,512]{1,0:T(8,128)S(1)}, f32[512,512]{1,0:T(8,128)S(1)}, f32[256,1024]{1,0:T(8,128)S(1)}) custom-call(bf16[520,1024]{1,0:T(8,128)(2,1)S(1)} %get-tuple-element.37.refs_0_, bf16[520,1024]{1,0:T(8,128)(2,1)S(1)} %collective-permute-done.refs_1_, ...), custom_call_target="tpu_custom_call", output_to_operand_aliasing={{0}: (3, {}), {1}: (4, {})} | custom-call | flops 1342177280 | bytes 2097152 | tf_op jit(solution)/shard_map/pallas_call | solution.py:239
  47.3 11.4 %collective-permute-done.1.refs_0_.refs_2_ = bf16[192,1024]{1,0:T(8,128)(2,1)S(1)} collective-permute-done((bf16[192,1024]{1,0:T(8,128)(2,1)S(1)}, bf16[192,1024]{1,0:T(8,128)(2,1)S(1)}, u32[]{:S(2)}, u32[]{:S(2)}) %collective-permute-start.1) | collective-permute-done | bytes 393248 | tf_op jit(solution)/shard_map/ppermute | solution.py:29
  60.9 2.7 %shard_map.89 = (f32[512,512]{1,0:T(8,128)S(1)}, f32[512,512]{1,0:T(8,128)S(1)}, f32[512,512]{1,0:T(8,128)S(1)}, f32[256,1024]{1,0:T(8,128)S(1)}) custom-call(bf16[520,1024]{1,0:T(8,128)(2,1)S(1)} %get-tuple-element.37.refs_0_, bf16[520,1024]{1,0:T(8,128)(2,1)S(1)} %collective-permute-done.refs_1_, ...), custom_call_target="tpu_custom_call", output_to_operand_aliasing={{0}: (5, {}), {1}: (6, {}), {2}: (7, {})} | custom-call | flops 2013265920 | bytes 3145728 | tf_op jit(solution)/shard_map/pallas_call | solution.py:239
  63.7 2.8 %shard_map.90 = (f32[512,512]{1,0:T(8,128)S(1)}, f32[512,512]{1,0:T(8,128)S(1)}, f32[512,512]{1,0:T(8,128)S(1)}, f32[256,1024]{1,0:T(8,128)S(1)}) custom-call(bf16[520,1024]{1,0:T(8,128)(2,1)S(1)} %get-tuple-element.37.refs_0_, bf16[520,1024]{1,0:T(8,128)(2,1)S(1)} %collective-permute-done.refs_1_, ...), custom_call_target="tpu_custom_call", output_to_operand_aliasing={{0}: (5, {}), {1}: (6, {}), {2}: (7, {})} | custom-call | flops 2013265920 | bytes 3145728 | tf_op jit(solution)/shard_map/pallas_call | solution.py:239
  67.5 5.4 %collective-permute-start.13 = (bf16[256,1024]{1,0:T(8,128)(2,1)S(1)}, bf16[256,1024]{1,0:T(8,128)(2,1)S(1)}, u32[]{:S(2)}, u32[]{:S(2)}) collective-permute-start(bf16[256,1024]{1,0:T(8,128)(2,1)S(1)} %get-tuple-element.66), channel_id=1, source_target_pairs={{0,1},{1,0},{2,3},{3,2},{4,5},{5,4},{6,7},{7,6},{8,9},{9,8},{10,11... | collective-permute-start | bytes 1572872 | tf_op jit(solution)/shard_map/ppermute | solution.py:33
  74.0 1.9 %shard_map.93 = (f32[512,512]{1,0:T(8,128)S(1)}, bf16[256,1024]{1,0:T(8,128)(2,1)}) custom-call(bf16[520,1024]{1,0:T(8,128)(2,1)S(1)} %collective-permute-done.8.refs_0_, bf16[256,1024]{1,0:T(8,128)(2,1)S(1)} %collective-permute-done.6.refs_2_.refs_1_, f32[512,512]{1,0:T(8,128)S(1)} %get-tuple-element.58.refs_2_, ...), custom_call_target="tpu_custom_call", output_to_operand_aliasing={{0}: (2, {})} | custom-call | flops 671088640 | bytes 1048576 | tf_op jit(solution)/shard_map/pallas_call | solution.py:239
  78.1 1.5 %collective-permute-start.7 = (bf16[512,512]{1,0:T(8,128)(2,1)}, bf16[512,512]{1,0:T(8,128)(2,1)}, u32[]{:S(2)}, u32[]{:S(2)}) collective-permute-start(bf16[512,512]{1,0:T(8,128)(2,1)} %convert_element_type.27), channel_id=1, source_target_pairs={{0,48},{1,17},{16,32},{17,1},{32,16},{33,49},{48,0},{49,33},{2,50}... | collective-permute-start | bytes 1572872 | tf_op jit(solution)/shard_map/ppermute | solution.py:29
  79.6 1.8 %collective-permute-start.12 = (bf16[256,1024]{1,0:T(8,128)(2,1)}, bf16[256,1024]{1,0:T(8,128)(2,1)S(1)}, u32[]{:S(2)}, u32[]{:S(2)}) collective-permute-start(bf16[256,1024]{1,0:T(8,128)(2,1)} %get-tuple-element.64), channel_id=1, source_target_pairs={{0,1},{1,0},{2,3},{3,2},{4,5},{5,4},{6,7},{7,6},{8,9},{9,8},{10,11... | collective-permute-start | bytes 1572872 | tf_op jit(solution)/shard_map/ppermute | solution.py:33
  82.3 3.2 %collective-permute-done.9 = bf16[512,512]{1,0:T(8,128)(2,1)S(1)} collective-permute-done((bf16[512,512]{1,0:T(8,128)(2,1)S(1)}, bf16[512,512]{1,0:T(8,128)(2,1)S(1)}, u32[]{:S(2)}, u32[]{:S(2)}) %collective-permute-start.9) | collective-permute-done | bytes 524320 | tf_op jit(solution)/shard_map/ppermute | solution.py:29
  86.7 4.3 %collective-permute-done.14.got_ref = bf16[256,1024]{1,0:T(8,128)(2,1)S(1)} collective-permute-done((bf16[256,1024]{1,0:T(8,128)(2,1)}, bf16[256,1024]{1,0:T(8,128)(2,1)S(1)}, u32[]{:S(2)}, u32[]{:S(2)}) %collective-permute-start.14) | collective-permute-done | bytes 524320 | tf_op jit(solution)/shard_map/ppermute | solution.py:29
  91.3 7.0 %collective-permute-done.10 = bf16[512,512]{1,0:T(8,128)(2,1)} collective-permute-done((bf16[512,512]{1,0:T(8,128)(2,1)}, bf16[512,512]{1,0:T(8,128)(2,1)}, u32[]{:S(2)}, u32[]{:S(2)}) %collective-permute-start.10) | collective-permute-done | bytes 524320 | tf_op jit(solution)/shard_map/ppermute | solution.py:29
  98.3 1.4 %multiply_convert_fusion = bf16[512,512]{1,0:T(8,128)(2,1)S(1)} fusion(bf16[512,512]{1,0:T(8,128)(2,1)} %collective-permute-done.10, f32[512,512]{1,0:T(8,128)S(1)} %get-tuple-element.52, bf16[512,512]{1,0:T(8,128)(2,1)} %collective-permute-done.7), kind=kLoop, calls=%fused_computation.1 | loop fusion | flops 1572864 | bytes 2621440 | tf_op jit(solution)/shard_map/convert_element_type | solution.py:299
  100.5 3.4 %all-to-all-start.1 = ((bf16[8,16,1024]{2,1,0:T(8,128)(2,1)}), bf16[8,16,1024]{2,1,0:T(8,128)(2,1)S(1)}, u32[]{:S(2)}, u32[]{:S(2)}) async-start(bf16[8,16,1024]{2,1,0:T(8,128)(2,1)} %rounded_sum.1), calls=%async_computation.1 | async-start | bytes 524288 | tf_op jit(solution)/shard_map/all_to_all | solution.py:37
  104.0 1.5 %collective-permute-done.11 = bf16[512,256]{1,0:T(8,128)(2,1)S(1)} collective-permute-done((bf16[512,256]{1,0:T(8,128)(2,1)S(1)}, bf16[512,256]{1,0:T(8,128)(2,1)S(1)}, u32[]{:S(2)}, u32[]{:S(2)}) %collective-permute-start.11) | collective-permute-done | bytes 262176 | tf_op jit(solution)/shard_map/ppermute | solution.py:33
  106.6 9.6 %all-to-all-done.1.parts_ref = bf16[8,16,1024]{2,1,0:T(8,128)(2,1)S(1)} async-done(((bf16[8,16,1024]{2,1,0:T(8,128)(2,1)}), bf16[8,16,1024]{2,1,0:T(8,128)(2,1)S(1)}, u32[]{:S(2)}, u32[]{:S(2)}) %all-to-all-start.1) | async-done | bytes 262176 | tf_op jit(solution)/shard_map/all_to_all | solution.py:37
  (34 shorter events, 13.4 us)
Async XLA Ops:
  2.5 34.2 %collective-permute-start = (bf16[520,1024]{1,0:T(8,128)(2,1)S(1)}, bf16[520,1024]{1,0:T(8,128)(2,1)S(1)}, u32[]{:S(2)}, u32[]{:S(2)}) collective-permute-start(bf16[520,1024]{1,0:T(8,128)(2,1)S(1)} %get-tuple-element.37.refs_0_), channel_id=1, source_target_pairs={{0,16},{1,49},{16,0},{17,33},{32,48},{33,17},{48,32},{49,1},{2,18}... | collective-permute-start | bytes 3194888 | tf_op jit(solution)/shard_map/ppermute | solution.py:29
  26.2 6.5 %collective-permute-start.3 = (bf16[128,1024]{1,0:T(8,128)(2,1)S(1)}, bf16[128,1024]{1,0:T(8,128)(2,1)S(1)}, u32[]{:S(2)}, u32[]{:S(2)}) collective-permute-start(bf16[128,1024]{1,0:T(8,128)(2,1)S(1)} %bitcast.3), channel_id=1, source_target_pairs={{0,64},{1,193},{64,0},{65,129},{128,192},{129,65},{192,128},{193,1... | collective-permute-start | bytes 786440 | tf_op jit(solution)/shard_map/ppermute | solution.py:29
  32.8 8.4 %collective-permute-start.4 = (bf16[256,1024]{1,0:T(8,128)(2,1)S(1)}, bf16[256,1024]{1,0:T(8,128)(2,1)S(1)}, u32[]{:S(2)}, u32[]{:S(2)}) collective-permute-start(bf16[256,1024]{1,0:T(8,128)(2,1)S(1)} %pad_maximum_fusion.refs_2_.refs_1_), channel_id=1, source_target_pairs={{0,192},{1,65},{64,128},{65,1},{128,64},{129,193},{192,0},{193,129... | collective-permute-start | bytes 1572872 | tf_op jit(solution)/shard_map/ppermute | solution.py:29
  33.2 25.5 %collective-permute-start.2 = (bf16[328,1024]{1,0:T(8,128)(2,1)S(1)}, bf16[328,1024]{1,0:T(8,128)(2,1)S(1)}, u32[]{:S(2)}, u32[]{:S(2)}) collective-permute-start(bf16[328,1024]{1,0:T(8,128)(2,1)S(1)} %get-tuple-element.39), channel_id=1, source_target_pairs={{0,48},{1,17},{16,32},{17,1},{32,16},{33,49},{48,0},{49,33},{2,50}... | collective-permute-start | bytes 2015240 | tf_op jit(solution)/shard_map/ppermute | solution.py:29
  33.2 12.2 %collective-permute-start.6 = (bf16[256,1024]{1,0:T(8,128)(2,1)S(1)}, bf16[256,1024]{1,0:T(8,128)(2,1)S(1)}, u32[]{:S(2)}, u32[]{:S(2)}) collective-permute-start(bf16[256,1024]{1,0:T(8,128)(2,1)S(1)} %pad_maximum_fusion.refs_2_.refs_1_), channel_id=1, source_target_pairs={{0,1},{1,0},{2,3},{3,2},{4,5},{5,4},{6,7},{7,6},{8,9},{9,8},{10,11... | collective-permute-start | bytes 1572872 | tf_op jit(solution)/shard_map/ppermute | solution.py:33
  36.7 29.8 %collective-permute-start.8 = (bf16[520,1024]{1,0:T(8,128)(2,1)S(1)}, bf16[520,1024]{1,0:T(8,128)(2,1)S(1)}, u32[]{:S(2)}, u32[]{:S(2)}) collective-permute-start(bf16[520,1024]{1,0:T(8,128)(2,1)S(1)} %collective-permute-done.refs_1_), channel_id=1, source_target_pairs={{0,48},{1,17},{16,32},{17,1},{32,16},{33,49},{48,0},{49,33},{2,50}... | collective-permute-start | bytes 3194888 | tf_op jit(solution)/shard_map/ppermute | solution.py:29
  36.9 21.8 %collective-permute-start.1 = (bf16[192,1024]{1,0:T(8,128)(2,1)S(1)}, bf16[192,1024]{1,0:T(8,128)(2,1)S(1)}, u32[]{:S(2)}, u32[]{:S(2)}) collective-permute-start(bf16[192,1024]{1,0:T(8,128)(2,1)S(1)} %get-tuple-element.38), channel_id=1, source_target_pairs={{0,48},{1,17},{16,32},{17,1},{32,16},{33,49},{48,0},{49,33},{2,50}... | collective-permute-start | bytes 1179656 | tf_op jit(solution)/shard_map/ppermute | solution.py:29
  41.2 22.5 %collective-permute-start.5 = (bf16[256,1024]{1,0:T(8,128)(2,1)S(1)}, bf16[256,1024]{1,0:T(8,128)(2,1)S(1)}, u32[]{:S(2)}, u32[]{:S(2)}) collective-permute-start(bf16[256,1024]{1,0:T(8,128)(2,1)S(1)} %collective-permute-done.4.refs_4_.refs_1_), channel_id=1, source_target_pairs={{0,1},{1,0},{2,3},{3,2},{4,5},{5,4},{6,7},{7,6},{8,9},{9,8},{10,11... | collective-permute-start | bytes 1572872 | tf_op jit(solution)/shard_map/ppermute | solution.py:33
  67.5 13.8 %collective-permute-start.13 = (bf16[256,1024]{1,0:T(8,128)(2,1)S(1)}, bf16[256,1024]{1,0:T(8,128)(2,1)S(1)}, u32[]{:S(2)}, u32[]{:S(2)}) collective-permute-start(bf16[256,1024]{1,0:T(8,128)(2,1)S(1)} %get-tuple-element.66), channel_id=1, source_target_pairs={{0,1},{1,0},{2,3},{3,2},{4,5},{5,4},{6,7},{7,6},{8,9},{9,8},{10,11... | collective-permute-start | bytes 1572872 | tf_op jit(solution)/shard_map/ppermute | solution.py:33
  77.1 8.4 %collective-permute-start.9 = (bf16[512,512]{1,0:T(8,128)(2,1)S(1)}, bf16[512,512]{1,0:T(8,128)(2,1)S(1)}, u32[]{:S(2)}, u32[]{:S(2)}) collective-permute-start(bf16[512,512]{1,0:T(8,128)(2,1)S(1)} %convert_element_type.29), channel_id=1, source_target_pairs={{0,48},{1,17},{16,32},{17,1},{32,16},{33,49},{48,0},{49,33},{2,50}... | collective-permute-start | bytes 1572872 | tf_op jit(solution)/shard_map/ppermute | solution.py:29
  78.1 13.2 %collective-permute-start.7 = (bf16[512,512]{1,0:T(8,128)(2,1)}, bf16[512,512]{1,0:T(8,128)(2,1)}, u32[]{:S(2)}, u32[]{:S(2)}) collective-permute-start(bf16[512,512]{1,0:T(8,128)(2,1)} %convert_element_type.27), channel_id=1, source_target_pairs={{0,48},{1,17},{16,32},{17,1},{32,16},{33,49},{48,0},{49,33},{2,50}... | collective-permute-start | bytes 1572872 | tf_op jit(solution)/shard_map/ppermute | solution.py:29
  79.6 7.1 %collective-permute-start.12 = (bf16[256,1024]{1,0:T(8,128)(2,1)}, bf16[256,1024]{1,0:T(8,128)(2,1)S(1)}, u32[]{:S(2)}, u32[]{:S(2)}) collective-permute-start(bf16[256,1024]{1,0:T(8,128)(2,1)} %get-tuple-element.64), channel_id=1, source_target_pairs={{0,1},{1,0},{2,3},{3,2},{4,5},{5,4},{6,7},{7,6},{8,9},{9,8},{10,11... | collective-permute-start | bytes 1572872 | tf_op jit(solution)/shard_map/ppermute | solution.py:33
  82.3 8.6 %collective-permute-start.14 = (bf16[256,1024]{1,0:T(8,128)(2,1)}, bf16[256,1024]{1,0:T(8,128)(2,1)S(1)}, u32[]{:S(2)}, u32[]{:S(2)}) collective-permute-start(bf16[256,1024]{1,0:T(8,128)(2,1)} %add_convert_fusion), channel_id=1, source_target_pairs={{0,192},{1,65},{64,128},{65,1},{128,64},{129,193},{192,0},{193,129... | collective-permute-start | bytes 1572872 | tf_op jit(solution)/shard_map/ppermute | solution.py:29
  86.5 11.8 %collective-permute-start.10 = (bf16[512,512]{1,0:T(8,128)(2,1)}, bf16[512,512]{1,0:T(8,128)(2,1)}, u32[]{:S(2)}, u32[]{:S(2)}) collective-permute-start(bf16[512,512]{1,0:T(8,128)(2,1)} %add_convert_fusion.1), channel_id=1, source_target_pairs={{0,16},{1,49},{16,0},{17,33},{32,48},{33,17},{48,32},{49,1},{2,18}... | collective-permute-start | bytes 1572872 | tf_op jit(solution)/shard_map/ppermute | solution.py:29
  91.1 8.6 %collective-permute-start.15 = (bf16[128,1024]{1,0:T(8,128)(2,1)S(1)}, bf16[128,1024]{1,0:T(8,128)(2,1)S(1)}, u32[]{:S(2)}, u32[]{:S(2)}) collective-permute-start(bf16[128,1024]{1,0:T(8,128)(2,1)S(1)} %get-tuple-element.68), channel_id=1, source_target_pairs={{0,64},{1,193},{64,0},{65,129},{128,192},{129,65},{192,128},{193,1... | collective-permute-start | bytes 786440 | tf_op jit(solution)/shard_map/ppermute | solution.py:29
  100.5 15.7 %all-to-all-start.1 = ((bf16[8,16,1024]{2,1,0:T(8,128)(2,1)}), bf16[8,16,1024]{2,1,0:T(8,128)(2,1)S(1)}, u32[]{:S(2)}, u32[]{:S(2)}) async-start(bf16[8,16,1024]{2,1,0:T(8,128)(2,1)} %rounded_sum.1), calls=%async_computation.1 | async-start | bytes 524288 | tf_op jit(solution)/shard_map/all_to_all | solution.py:37
  103.9 1.6 %collective-permute-start.11 = (bf16[512,256]{1,0:T(8,128)(2,1)S(1)}, bf16[512,256]{1,0:T(8,128)(2,1)S(1)}, u32[]{:S(2)}, u32[]{:S(2)}) collective-permute-start(bf16[512,256]{1,0:T(8,128)(2,1)S(1)} %get-tuple-element.72), channel_id=1, source_target_pairs={{0,1},{1,0},{2,3},{3,2},{4,5},{5,4},{6,7},{7,6},{8,9},{9,8},{10,11... | collective-permute-start | bytes 786440 | tf_op jit(solution)/shard_map/ppermute | solution.py:33

commit v6 on v5

--- a/solution.py
+++ b/solution.py
@@ -124,29 +124,28 @@
             pltpu.VMEM((rows, 2 * channels), BF16),
             pltpu.SemaphoreType.DMA((15,)),
         ],
-        compiler_params=pltpu.CompilerParams(vmem_limit_bytes=16 * 1024 * 1024),
+        compiler_params=pltpu.CompilerParams(vmem_limit_bytes=10 * 1024 * 1024),
         name="pack",
     )(core.reshape(1), *arrays)
 
 
-def split_sum_kernel(mine_ref, core_ref, got_ref, kept_ref, sent_ref):
+def split_sum_kernel(mine_ref, got_ref, kept_ref, sent_ref):
     n = kept_ref.shape[0]
-    kept_ref[...] = mine_ref[:n, :] + core_ref[:n, :].astype(F32) + got_ref[:n, :].astype(F32)
-    low = mine_ref[n:, :] + core_ref[n:, :].astype(F32) + got_ref[n:, :].astype(F32)
-    sent_ref[...] = low.astype(BF16)
-
-
-def split_sum(mine, other_core, got):
+    kept_ref[...] = mine_ref[:n, :] + got_ref[:n, :].astype(F32)
+    sent_ref[...] = (mine_ref[n:, :] + got_ref[n:, :].astype(F32)).astype(BF16)
+
+
+def split_sum(mine, got):
     vmem = pl.BlockSpec(memory_space=pltpu.VMEM)
     half = (mine.shape[0] // 2, mine.shape[1])
     return pl.pallas_call(
         split_sum_kernel,
         out_shape=[jax.ShapeDtypeStruct(half, F32), jax.ShapeDtypeStruct(half, BF16)],
-        in_specs=[vmem, vmem, vmem],
+        in_specs=[vmem, vmem],
         out_specs=[vmem, vmem],
-        compiler_params=pltpu.CompilerParams(vmem_limit_bytes=6 * 1024 * 1024),
+        compiler_params=pltpu.CompilerParams(vmem_limit_bytes=4 * 1024 * 1024),
         name="split_sum",
-    )(mine, other_core, got)
+    )(mine, got)
 
 
 def rounded_sum_kernel(mine_ref, got_ref, out_ref):
@@ -248,7 +247,7 @@
             bytes_accessed=2 * n_packs * half * channels * 2,
             transcendentals=n_packs * half * keys,
         ),
-        compiler_params=pltpu.CompilerParams(vmem_limit_bytes=16 * 1024 * 1024),
+        compiler_params=pltpu.CompilerParams(vmem_limit_bytes=10 * 1024 * 1024),
     )(*args)
     return list(out[:n_packs]), out[n_packs]
 
@@ -287,9 +286,9 @@
     dqb, near_sum = block_work(b, near, dqb, near_sum, F32)
 
     far_sum = far_sum + swap(far_osum).astype(F32)
-    near_got = swap(near_osum)
+    near_sum = near_sum + swap(near_osum).astype(F32)
     n1 = keys.shape[1]
-    kept, sent = split_sum(near_sum, near_got, trade(far_sum.astype(BF16), "slab_0", 1))
+    kept, sent = split_sum(near_sum, trade(far_sum.astype(BF16), "slab_0", 1))
     parts = across(rounded_sum(kept, trade(sent, "slab_0", 0), n1))
     grad_keys, grad_values = finish(parts, scale)
 

time: 117 us -> 116 us (level)
  other arithmetic: 5.36 us -> 6.57 us
  waiting for transfers between devices: 43.9 us -> 42.7 us
    add x0 -> x1, other arithmetic: none -> 1.22 us  [steps(): near_sum = near_sum + swap(near_osum).astype(F32)]
  transfers between devices with their start and end apart: 17 -> 17, of which waited for: 9 -> 9; matrix products, arithmetic and copies ran while one was open for 5% -> 6% of each run, Pallas kernels for 13% -> 13%
where the time goes in v6:
time: 116 us
  waiting for transfers between devices  42.7 us (37%)
  starting transfers between devices  26.3 us (23%)
  blocking collectives  20.4 us (18%)
  Pallas kernels  19.1 us (16%)
  other arithmetic  6.57 us (6%)
    ppermute x11, waiting for transfers between devices, trade(): return lax.ppermute(x, (axis, 'kv'), pairs)  31.6 us
    all_to_all x1, blocking collectives, across(): return lax.all_to_all(x, 'slab_2', 0, 0, tiled=True)  20.4 us
    pallas_call x10, Pallas kernels, block_work(): pl.pallas_call(body, out_shape=[jax.ShapeDtypeStruct((half, channels), F3...  15.8 us
    ppermute x5, starting transfers between devices, swap(): return lax.ppermute(x, 'kv', [(0, 1), (1, 0)])  13.1 us
    ppermute x11, starting transfers between devices, trade(): return lax.ppermute(x, (axis, 'kv'), pairs)  9.83 us
    all_to_all x1, waiting for transfers between devices, across(): return lax.all_to_all(x, 'slab_2', 0, 0, tiled=True)  9.62 us
    all_to_all x1, starting transfers between devices, across(): return lax.all_to_all(x, 'slab_2', 0, 0, tiled=True)  3.41 us
  transfers between devices with their start and end apart: 17, of which 9 were waited for; matrix products, arithmetic and copies ran while one was open for 6% of the time, Pallas kernels for 13%

profile of v6, /device:TPU:1, one launch (start us, length us, event | category | flops | bytes accessed | tf_op | source)
XLA Modules:
  0.0 116.0 jit_solution(479032817325697990)
XLA Ops:
  0.6 1.8 %pack.1 = (bf16[520,1024]{1,0:T(8,128)(2,1)S(1)}, bf16[192,1024]{1,0:T(8,128)(2,1)S(1)}, bf16[328,1024]{1,0:T(8,128)(2,1)S(1)}, bf16[8,16,1024]{2,1,0:T(8,128)(2,1)S(1)}) custom-call(s32[1]{0:T(128)} %bitcast.core_ref, bf16[1024,512]{1,0:T(8,128)(2,1)} %q_hbm.1, bf16[1024,512]{1,0:T(8,128)(2,1)} %g_hbm.1, bf16[1024,512]{1,0:T(8,128)(2,1)} %o_hbm.1, ...), custom_call_target="tpu_custom_call" | custom-call | tf_op jit(solution)/shard_map/pack/pallas_call | solution.py:111
  2.5 3.4 %collective-permute-start = (bf16[520,1024]{1,0:T(8,128)(2,1)S(1)}, bf16[520,1024]{1,0:T(8,128)(2,1)S(1)}, u32[]{:S(2)}, u32[]{:S(2)}) collective-permute-start(bf16[520,1024]{1,0:T(8,128)(2,1)S(1)} %get-tuple-element.37.refs_0_), channel_id=1, source_target_pairs={{0,16},{1,49},{16,0},{17,33},{32,48},{33,17},{48,32},{49,1},{2,18}... | collective-permute-start | bytes 3194888 | tf_op jit(solution)/shard_map/ppermute | solution.py:29
  5.9 20.4 %all_to_all.10 = bf16[8,16,1024]{2,1,0:T(8,128)(2,1)S(1)} all-to-all(bf16[8,16,1024]{2,1,0:T(8,128)(2,1)S(1)} %get-tuple-element.40), channel_id=1, replica_groups=mesh['slab_0'=4,'slab_1'=4,'slab_2'=8,'kv'=2] {'slab_2'}, dimensions={0} | all-to-all | bytes 524288 | tf_op jit(solution)/shard_map/all_to_all | solution.py:37
  26.2 2.7 %collective-permute-start.3 = (bf16[128,1024]{1,0:T(8,128)(2,1)S(1)}, bf16[128,1024]{1,0:T(8,128)(2,1)S(1)}, u32[]{:S(2)}, u32[]{:S(2)}) collective-permute-start(bf16[128,1024]{1,0:T(8,128)(2,1)S(1)} %bitcast.3), channel_id=1, source_target_pairs={{0,64},{1,193},{64,0},{65,129},{128,192},{129,65},{192,128},{193,1... | collective-permute-start | bytes 786440 | tf_op jit(solution)/shard_map/ppermute | solution.py:29
  29.0 3.8 %collective-permute-done.3 = bf16[128,1024]{1,0:T(8,128)(2,1)S(1)} collective-permute-done((bf16[128,1024]{1,0:T(8,128)(2,1)S(1)}, bf16[128,1024]{1,0:T(8,128)(2,1)S(1)}, u32[]{:S(2)}, u32[]{:S(2)}) %collective-permute-start.3) | collective-permute-done | bytes 262176 | tf_op jit(solution)/shard_map/ppermute | solution.py:29
  33.2 3.5 %collective-permute-start.6 = (bf16[256,1024]{1,0:T(8,128)(2,1)S(1)}, bf16[256,1024]{1,0:T(8,128)(2,1)S(1)}, u32[]{:S(2)}, u32[]{:S(2)}) collective-permute-start(bf16[256,1024]{1,0:T(8,128)(2,1)S(1)} %pad_maximum_fusion.refs_2_.refs_1_), channel_id=1, source_target_pairs={{0,1},{1,0},{2,3},{3,2},{4,5},{5,4},{6,7},{7,6},{8,9},{9,8},{10,11... | collective-permute-start | bytes 1572872 | tf_op jit(solution)/shard_map/ppermute | solution.py:33
  38.1 3.0 %collective-permute-done.4.refs_4_.refs_1_ = bf16[256,1024]{1,0:T(8,128)(2,1)S(1)} collective-permute-done((bf16[256,1024]{1,0:T(8,128)(2,1)S(1)}, bf16[256,1024]{1,0:T(8,128)(2,1)S(1)}, u32[]{:S(2)}, u32[]{:S(2)}) %collective-permute-start.4) | collective-permute-done | bytes 524320 | tf_op jit(solution)/shard_map/ppermute | solution.py:29
  41.2 2.4 %collective-permute-start.5 = (bf16[256,1024]{1,0:T(8,128)(2,1)S(1)}, bf16[256,1024]{1,0:T(8,128)(2,1)S(1)}, u32[]{:S(2)}, u32[]{:S(2)}) collective-permute-start(bf16[256,1024]{1,0:T(8,128)(2,1)S(1)} %collective-permute-done.4.refs_4_.refs_1_), channel_id=1, source_target_pairs={{0,1},{1,0},{2,3},{3,2},{4,5},{5,4},{6,7},{7,6},{8,9},{9,8},{10,11... | collective-permute-start | bytes 1572872 | tf_op jit(solution)/shard_map/ppermute | solution.py:33
  43.6 1.8 %shard_map.85 = (f32[512,512]{1,0:T(8,128)S(1)}, f32[512,512]{1,0:T(8,128)S(1)}, f32[256,1024]{1,0:T(8,128)S(1)}) custom-call(bf16[520,1024]{1,0:T(8,128)(2,1)S(1)} %get-tuple-element.37.refs_0_, bf16[520,1024]{1,0:T(8,128)(2,1)S(1)} %collective-permute-done.refs_1_, bf16[256,1024]{1,0:T(8,128)(2,1)S(1)} %pad_maximum_fusion.refs_2_.refs_1_, ...), custom_call_target="tpu_custom_call" | custom-call | flops 1342177280 | bytes 2097152 | tf_op jit(solution)/shard_map/pallas_call | solution.py:238
  45.4 1.9 %shard_map.86 = (f32[512,512]{1,0:T(8,128)S(1)}, f32[512,512]{1,0:T(8,128)S(1)}, f32[256,1024]{1,0:T(8,128)S(1)}) custom-call(bf16[520,1024]{1,0:T(8,128)(2,1)S(1)} %get-tuple-element.37.refs_0_, bf16[520,1024]{1,0:T(8,128)(2,1)S(1)} %collective-permute-done.refs_1_, ...), custom_call_target="tpu_custom_call", output_to_operand_aliasing={{0}: (3, {}), {1}: (4, {})} | custom-call | flops 1342177280 | bytes 2097152 | tf_op jit(solution)/shard_map/pallas_call | solution.py:238
  47.3 11.4 %collective-permute-done.1.refs_0_.refs_2_ = bf16[192,1024]{1,0:T(8,128)(2,1)S(1)} collective-permute-done((bf16[192,1024]{1,0:T(8,128)(2,1)S(1)}, bf16[192,1024]{1,0:T(8,128)(2,1)S(1)}, u32[]{:S(2)}, u32[]{:S(2)}) %collective-permute-start.1) | collective-permute-done | bytes 393248 | tf_op jit(solution)/shard_map/ppermute | solution.py:29
  60.9 2.7 %shard_map.89 = (f32[512,512]{1,0:T(8,128)S(1)}, f32[512,512]{1,0:T(8,128)S(1)}, f32[512,512]{1,0:T(8,128)S(1)}, f32[256,1024]{1,0:T(8,128)S(1)}) custom-call(bf16[520,1024]{1,0:T(8,128)(2,1)S(1)} %get-tuple-element.37.refs_0_, bf16[520,1024]{1,0:T(8,128)(2,1)S(1)} %collective-permute-done.refs_1_, ...), custom_call_target="tpu_custom_call", output_to_operand_aliasing={{0}: (5, {}), {1}: (6, {}), {2}: (7, {})} | custom-call | flops 2013265920 | bytes 3145728 | tf_op jit(solution)/shard_map/pallas_call | solution.py:238
  63.7 2.8 %shard_map.90 = (f32[512,512]{1,0:T(8,128)S(1)}, f32[512,512]{1,0:T(8,128)S(1)}, f32[512,512]{1,0:T(8,128)S(1)}, f32[256,1024]{1,0:T(8,128)S(1)}) custom-call(bf16[520,1024]{1,0:T(8,128)(2,1)S(1)} %get-tuple-element.37.refs_0_, bf16[520,1024]{1,0:T(8,128)(2,1)S(1)} %collective-permute-done.refs_1_, ...), custom_call_target="tpu_custom_call", output_to_operand_aliasing={{0}: (5, {}), {1}: (6, {}), {2}: (7, {})} | custom-call | flops 2013265920 | bytes 3145728 | tf_op jit(solution)/shard_map/pallas_call | solution.py:238
  67.5 5.4 %collective-permute-start.13 = (bf16[256,1024]{1,0:T(8,128)(2,1)S(1)}, bf16[256,1024]{1,0:T(8,128)(2,1)S(1)}, u32[]{:S(2)}, u32[]{:S(2)}) collective-permute-start(bf16[256,1024]{1,0:T(8,128)(2,1)S(1)} %get-tuple-element.66), channel_id=1, source_target_pairs={{0,1},{1,0},{2,3},{3,2},{4,5},{5,4},{6,7},{7,6},{8,9},{9,8},{10,11... | collective-permute-start | bytes 1572872 | tf_op jit(solution)/shard_map/ppermute | solution.py:33
  77.3 1.5 %collective-permute-start.7 = (bf16[512,512]{1,0:T(8,128)(2,1)}, bf16[512,512]{1,0:T(8,128)(2,1)}, u32[]{:S(2)}, u32[]{:S(2)}) collective-permute-start(bf16[512,512]{1,0:T(8,128)(2,1)} %convert_element_type.30), channel_id=1, source_target_pairs={{0,48},{1,17},{16,32},{17,1},{32,16},{33,49},{48,0},{49,33},{2,50}... | collective-permute-start | bytes 1572872 | tf_op jit(solution)/shard_map/ppermute | solution.py:29
  78.7 1.8 %collective-permute-start.12 = (bf16[256,1024]{1,0:T(8,128)(2,1)S(1)}, bf16[256,1024]{1,0:T(8,128)(2,1)}, u32[]{:S(2)}, u32[]{:S(2)}) collective-permute-start(bf16[256,1024]{1,0:T(8,128)(2,1)S(1)} %get-tuple-element.64), channel_id=1, source_target_pairs={{0,1},{1,0},{2,3},{3,2},{4,5},{5,4},{6,7},{7,6},{8,9},{9,8},{10,11... | collective-permute-start | bytes 1572872 | tf_op jit(solution)/shard_map/ppermute | solution.py:33
  81.5 3.2 %collective-permute-done.9 = bf16[512,512]{1,0:T(8,128)(2,1)S(1)} collective-permute-done((bf16[512,512]{1,0:T(8,128)(2,1)S(1)}, bf16[512,512]{1,0:T(8,128)(2,1)S(1)}, u32[]{:S(2)}, u32[]{:S(2)}) %collective-permute-start.9) | collective-permute-done | bytes 524320 | tf_op jit(solution)/shard_map/ppermute | solution.py:29
  85.9 1.2 %convert_add_fusion.mine_ref = f32[256,1024]{1,0:T(8,128)S(1)} fusion(f32[256,1024]{1,0:T(8,128)S(1)} %get-tuple-element.63, bf16[256,1024]{1,0:T(8,128)(2,1)} %collective-permute-done.12), kind=kLoop, calls=%fused_computation.1 | loop fusion | flops 524288 | bytes 2621440 | tf_op jit(solution)/shard_map/add | solution.py:289
  87.1 3.0 %collective-permute-done.14.got_ref = bf16[256,1024]{1,0:T(8,128)(2,1)S(1)} collective-permute-done((bf16[256,1024]{1,0:T(8,128)(2,1)}, bf16[256,1024]{1,0:T(8,128)(2,1)S(1)}, u32[]{:S(2)}, u32[]{:S(2)}) %collective-permute-start.14) | collective-permute-done | bytes 524320 | tf_op jit(solution)/shard_map/ppermute | solution.py:29
  90.4 7.0 %collective-permute-done.10 = bf16[512,512]{1,0:T(8,128)(2,1)} collective-permute-done((bf16[512,512]{1,0:T(8,128)(2,1)}, bf16[512,512]{1,0:T(8,128)(2,1)}, u32[]{:S(2)}, u32[]{:S(2)}) %collective-permute-start.10) | collective-permute-done | bytes 524320 | tf_op jit(solution)/shard_map/ppermute | solution.py:29
  97.4 1.4 %multiply_convert_fusion = bf16[512,512]{1,0:T(8,128)(2,1)S(1)} fusion(bf16[512,512]{1,0:T(8,128)(2,1)} %collective-permute-done.10, f32[512,512]{1,0:T(8,128)S(1)} %get-tuple-element.52, bf16[512,512]{1,0:T(8,128)(2,1)} %collective-permute-done.7), kind=kLoop, calls=%fused_computation.2 | loop fusion | flops 1572864 | bytes 2621440 | tf_op jit(solution)/shard_map/convert_element_type | solution.py:298
  99.6 3.4 %all-to-all-start.1 = ((bf16[8,16,1024]{2,1,0:T(8,128)(2,1)}), bf16[8,16,1024]{2,1,0:T(8,128)(2,1)S(1)}, u32[]{:S(2)}, u32[]{:S(2)}) async-start(bf16[8,16,1024]{2,1,0:T(8,128)(2,1)} %rounded_sum.1), calls=%async_computation.1 | async-start | bytes 524288 | tf_op jit(solution)/shard_map/all_to_all | solution.py:37
  103.2 1.5 %collective-permute-done.11 = bf16[512,256]{1,0:T(8,128)(2,1)S(1)} collective-permute-done((bf16[512,256]{1,0:T(8,128)(2,1)S(1)}, bf16[512,256]{1,0:T(8,128)(2,1)S(1)}, u32[]{:S(2)}, u32[]{:S(2)}) %collective-permute-start.11) | collective-permute-done | bytes 262176 | tf_op jit(solution)/shard_map/ppermute | solution.py:33
  105.7 9.6 %all-to-all-done.1.parts_ref = bf16[8,16,1024]{2,1,0:T(8,128)(2,1)S(1)} async-done(((bf16[8,16,1024]{2,1,0:T(8,128)(2,1)}), bf16[8,16,1024]{2,1,0:T(8,128)(2,1)S(1)}, u32[]{:S(2)}, u32[]{:S(2)}) %all-to-all-start.1) | async-done | bytes 262176 | tf_op jit(solution)/shard_map/all_to_all | solution.py:37
  (35 shorter events, 14.5 us)
Async XLA Ops:
  2.5 34.2 %collective-permute-start = (bf16[520,1024]{1,0:T(8,128)(2,1)S(1)}, bf16[520,1024]{1,0:T(8,128)(2,1)S(1)}, u32[]{:S(2)}, u32[]{:S(2)}) collective-permute-start(bf16[520,1024]{1,0:T(8,128)(2,1)S(1)} %get-tuple-element.37.refs_0_), channel_id=1, source_target_pairs={{0,16},{1,49},{16,0},{17,33},{32,48},{33,17},{48,32},{49,1},{2,18}... | collective-permute-start | bytes 3194888 | tf_op jit(solution)/shard_map/ppermute | solution.py:29
  26.2 6.5 %collective-permute-start.3 = (bf16[128,1024]{1,0:T(8,128)(2,1)S(1)}, bf16[128,1024]{1,0:T(8,128)(2,1)S(1)}, u32[]{:S(2)}, u32[]{:S(2)}) collective-permute-start(bf16[128,1024]{1,0:T(8,128)(2,1)S(1)} %bitcast.3), channel_id=1, source_target_pairs={{0,64},{1,193},{64,0},{65,129},{128,192},{129,65},{192,128},{193,1... | collective-permute-start | bytes 786440 | tf_op jit(solution)/shard_map/ppermute | solution.py:29
  32.8 8.4 %collective-permute-start.4 = (bf16[256,1024]{1,0:T(8,128)(2,1)S(1)}, bf16[256,1024]{1,0:T(8,128)(2,1)S(1)}, u32[]{:S(2)}, u32[]{:S(2)}) collective-permute-start(bf16[256,1024]{1,0:T(8,128)(2,1)S(1)} %pad_maximum_fusion.refs_2_.refs_1_), channel_id=1, source_target_pairs={{0,192},{1,65},{64,128},{65,1},{128,64},{129,193},{192,0},{193,129... | collective-permute-start | bytes 1572872 | tf_op jit(solution)/shard_map/ppermute | solution.py:29
  33.2 25.5 %collective-permute-start.2 = (bf16[328,1024]{1,0:T(8,128)(2,1)S(1)}, bf16[328,1024]{1,0:T(8,128)(2,1)S(1)}, u32[]{:S(2)}, u32[]{:S(2)}) collective-permute-start(bf16[328,1024]{1,0:T(8,128)(2,1)S(1)} %get-tuple-element.39), channel_id=1, source_target_pairs={{0,48},{1,17},{16,32},{17,1},{32,16},{33,49},{48,0},{49,33},{2,50}... | collective-permute-start | bytes 2015240 | tf_op jit(solution)/shard_map/ppermute | solution.py:29
  33.2 12.2 %collective-permute-start.6 = (bf16[256,1024]{1,0:T(8,128)(2,1)S(1)}, bf16[256,1024]{1,0:T(8,128)(2,1)S(1)}, u32[]{:S(2)}, u32[]{:S(2)}) collective-permute-start(bf16[256,1024]{1,0:T(8,128)(2,1)S(1)} %pad_maximum_fusion.refs_2_.refs_1_), channel_id=1, source_target_pairs={{0,1},{1,0},{2,3},{3,2},{4,5},{5,4},{6,7},{7,6},{8,9},{9,8},{10,11... | collective-permute-start | bytes 1572872 | tf_op jit(solution)/shard_map/ppermute | solution.py:33
  36.7 29.8 %collective-permute-start.8 = (bf16[520,1024]{1,0:T(8,128)(2,1)S(1)}, bf16[520,1024]{1,0:T(8,128)(2,1)S(1)}, u32[]{:S(2)}, u32[]{:S(2)}) collective-permute-start(bf16[520,1024]{1,0:T(8,128)(2,1)S(1)} %collective-permute-done.refs_1_), channel_id=1, source_target_pairs={{0,48},{1,17},{16,32},{17,1},{32,16},{33,49},{48,0},{49,33},{2,50}... | collective-permute-start | bytes 3194888 | tf_op jit(solution)/shard_map/ppermute | solution.py:29
  36.9 21.8 %collective-permute-start.1 = (bf16[192,1024]{1,0:T(8,128)(2,1)S(1)}, bf16[192,1024]{1,0:T(8,128)(2,1)S(1)}, u32[]{:S(2)}, u32[]{:S(2)}) collective-permute-start(bf16[192,1024]{1,0:T(8,128)(2,1)S(1)} %get-tuple-element.38), channel_id=1, source_target_pairs={{0,48},{1,17},{16,32},{17,1},{32,16},{33,49},{48,0},{49,33},{2,50}... | collective-permute-start | bytes 1179656 | tf_op jit(solution)/shard_map/ppermute | solution.py:29
  41.2 22.5 %collective-permute-start.5 = (bf16[256,1024]{1,0:T(8,128)(2,1)S(1)}, bf16[256,1024]{1,0:T(8,128)(2,1)S(1)}, u32[]{:S(2)}, u32[]{:S(2)}) collective-permute-start(bf16[256,1024]{1,0:T(8,128)(2,1)S(1)} %collective-permute-done.4.refs_4_.refs_1_), channel_id=1, source_target_pairs={{0,1},{1,0},{2,3},{3,2},{4,5},{5,4},{6,7},{7,6},{8,9},{9,8},{10,11... | collective-permute-start | bytes 1572872 | tf_op jit(solution)/shard_map/ppermute | solution.py:33
  67.5 13.0 %collective-permute-start.13 = (bf16[256,1024]{1,0:T(8,128)(2,1)S(1)}, bf16[256,1024]{1,0:T(8,128)(2,1)S(1)}, u32[]{:S(2)}, u32[]{:S(2)}) collective-permute-start(bf16[256,1024]{1,0:T(8,128)(2,1)S(1)} %get-tuple-element.66), channel_id=1, source_target_pairs={{0,1},{1,0},{2,3},{3,2},{4,5},{5,4},{6,7},{7,6},{8,9},{9,8},{10,11... | collective-permute-start | bytes 1572872 | tf_op jit(solution)/shard_map/ppermute | solution.py:33
  76.3 8.4 %collective-permute-start.9 = (bf16[512,512]{1,0:T(8,128)(2,1)S(1)}, bf16[512,512]{1,0:T(8,128)(2,1)S(1)}, u32[]{:S(2)}, u32[]{:S(2)}) collective-permute-start(bf16[512,512]{1,0:T(8,128)(2,1)S(1)} %convert_element_type.32), channel_id=1, source_target_pairs={{0,48},{1,17},{16,32},{17,1},{32,16},{33,49},{48,0},{49,33},{2,50}... | collective-permute-start | bytes 1572872 | tf_op jit(solution)/shard_map/ppermute | solution.py:29
  77.3 13.2 %collective-permute-start.7 = (bf16[512,512]{1,0:T(8,128)(2,1)}, bf16[512,512]{1,0:T(8,128)(2,1)}, u32[]{:S(2)}, u32[]{:S(2)}) collective-permute-start(bf16[512,512]{1,0:T(8,128)(2,1)} %convert_element_type.30), channel_id=1, source_target_pairs={{0,48},{1,17},{16,32},{17,1},{32,16},{33,49},{48,0},{49,33},{2,50}... | collective-permute-start | bytes 1572872 | tf_op jit(solution)/shard_map/ppermute | solution.py:29
  78.7 7.1 %collective-permute-start.12 = (bf16[256,1024]{1,0:T(8,128)(2,1)S(1)}, bf16[256,1024]{1,0:T(8,128)(2,1)}, u32[]{:S(2)}, u32[]{:S(2)}) collective-permute-start(bf16[256,1024]{1,0:T(8,128)(2,1)S(1)} %get-tuple-element.64), channel_id=1, source_target_pairs={{0,1},{1,0},{2,3},{3,2},{4,5},{5,4},{6,7},{7,6},{8,9},{9,8},{10,11... | collective-permute-start | bytes 1572872 | tf_op jit(solution)/shard_map/ppermute | solution.py:33
  81.5 8.6 %collective-permute-start.14 = (bf16[256,1024]{1,0:T(8,128)(2,1)}, bf16[256,1024]{1,0:T(8,128)(2,1)S(1)}, u32[]{:S(2)}, u32[]{:S(2)}) collective-permute-start(bf16[256,1024]{1,0:T(8,128)(2,1)} %add_convert_fusion), channel_id=1, source_target_pairs={{0,192},{1,65},{64,128},{65,1},{128,64},{129,193},{192,0},{193,129... | collective-permute-start | bytes 1572872 | tf_op jit(solution)/shard_map/ppermute | solution.py:29
  85.7 11.8 %collective-permute-start.10 = (bf16[512,512]{1,0:T(8,128)(2,1)}, bf16[512,512]{1,0:T(8,128)(2,1)}, u32[]{:S(2)}, u32[]{:S(2)}) collective-permute-start(bf16[512,512]{1,0:T(8,128)(2,1)} %add_convert_fusion.1), channel_id=1, source_target_pairs={{0,16},{1,49},{16,0},{17,33},{32,48},{33,17},{48,32},{49,1},{2,18}... | collective-permute-start | bytes 1572872 | tf_op jit(solution)/shard_map/ppermute | solution.py:29
  90.2 8.7 %collective-permute-start.15 = (bf16[128,1024]{1,0:T(8,128)(2,1)S(1)}, bf16[128,1024]{1,0:T(8,128)(2,1)S(1)}, u32[]{:S(2)}, u32[]{:S(2)}) collective-permute-start(bf16[128,1024]{1,0:T(8,128)(2,1)S(1)} %get-tuple-element.68), channel_id=1, source_target_pairs={{0,64},{1,193},{64,0},{65,129},{128,192},{129,65},{192,128},{193,1... | collective-permute-start | bytes 786440 | tf_op jit(solution)/shard_map/ppermute | solution.py:29
  99.6 15.7 %all-to-all-start.1 = ((bf16[8,16,1024]{2,1,0:T(8,128)(2,1)}), bf16[8,16,1024]{2,1,0:T(8,128)(2,1)S(1)}, u32[]{:S(2)}, u32[]{:S(2)}) async-start(bf16[8,16,1024]{2,1,0:T(8,128)(2,1)} %rounded_sum.1), calls=%async_computation.1 | async-start | bytes 524288 | tf_op jit(solution)/shard_map/all_to_all | solution.py:37
  103.1 1.6 %collective-permute-start.11 = (bf16[512,256]{1,0:T(8,128)(2,1)S(1)}, bf16[512,256]{1,0:T(8,128)(2,1)S(1)}, u32[]{:S(2)}, u32[]{:S(2)}) collective-permute-start(bf16[512,256]{1,0:T(8,128)(2,1)S(1)} %get-tuple-element.72), channel_id=1, source_target_pairs={{0,1},{1,0},{2,3},{3,2},{4,5},{5,4},{6,7},{7,6},{8,9},{9,8},{10,11... | collective-permute-start | bytes 786440 | tf_op jit(solution)/shard_map/ppermute | solution.py:33
